TPU v7x, 128 devices: a whole 4x4x4 slice. The times are simulated.
128 devices in a mesh: band: 16 (over x, z), head: 4 (over y), dp: 2 (over core).
Axes of the slice: x: 4, y: 4, z: 4, core: 2. Of those that a mesh axis runs over, the one named last changes fastest.
Arguments:
- tokens: bfloat16 [128, 1024, 512], P(('dp', 'band'), None, 'head'), parts along dimension 0, may hold values from -6 to 6
- corner_row: int32 [2048], P('dp'), parts along dimension 0, may hold values from 0 to 62
- corner_col: int32 [2048], P('dp'), parts along dimension 0, may hold values from 0 to 1022
- fraction: float32 [2, 2048], P(None, 'dp'), parts along dimension 1, may hold values from 0 to 1
- w_query: bfloat16 [512, 512], P(None, 'head'), may hold values from -2 to 2
- w_key: bfloat16 [512, 512], P(None, 'head'), may hold values from -2 to 2
- w_value: bfloat16 [512, 512], P(None, 'head'), may hold values from -0.25 to 0.25
- w_out: bfloat16 [512, 512], P('head'), may hold values from -0.25 to 0.25
- conv_kernel: float32 [25, 512], P(None, 'head'), may hold values from -1.25 to 1.25
- norm_gain: float32 [512], replicated, may hold values from 0.1 to 1.9
Outputs:
- mixed: bfloat16 [128, 1024, 512], P(('dp', 'band'), None, 'head'), parts along dimension 0
There are 2 independent parts, one for each index of `dp`. A program takes and returns all parts, laid end to end along the dimension named above; an argument that names none is the same for every part. Nothing has to cross between parts.
All inputs are finite; a program needn't handle non-finite values.
Results may differ from a plain program's by a relative error of at most 0.029.
Values may be sent and summed in bfloat16 or wider, within the bound.
No kernel may reach another device: no remote copies, remote signals or barrier semaphores. Data moves between devices by JAX's collectives and lax.ppermute only.
A program may use at most 64 MiB of HBM per device.

v0:
```python
import jax
import jax.numpy as jnp
from jax import lax
from jax.sharding import PartitionSpec as P

HEADS = 16
KER = 5


def cut_along(x, dim, devices):
    shape = x.shape
    blocks = x.reshape(*shape[:dim], devices, shape[dim] // devices, *shape[dim + 1 :])
    return jnp.moveaxis(blocks, dim, 0)


def summed_on_arrival(x, axis, dim):
    devices = lax.axis_size(axis)
    blocks = lax.all_to_all(cut_along(x, dim, devices), axis, 0, 0, tiled=True)
    return jnp.sum(blocks.astype(jnp.float32), axis=0)


def from_everyone(x, axis):
    copies = jnp.broadcast_to(x, (lax.axis_size(axis), *x.shape))
    return lax.all_to_all(copies, axis, split_axis=0, concat_axis=0, tiled=True)


def joined_along(blocks, dim):
    blocks = jnp.moveaxis(blocks, 0, dim)
    shape = blocks.shape
    return blocks.reshape(*shape[:dim], shape[dim] * shape[dim + 1], *shape[dim + 2 :])


def gather_directly(x, axis, dim):
    blocks = from_everyone(x, axis)
    return joined_along(blocks, dim)


def sent_together(arrays, axis, dim, along):
    both = jnp.concatenate(arrays, axis=along)
    whole, at, finished = (lax.all_gather(both, axis, axis=dim, tiled=True), 0, [])
    for a in arrays:
        finished.append(lax.slice_in_dim(whole, at, at + a.shape[along], axis=along))
        at += a.shape[along]
    return tuple(finished)


def padded_2(block, sides, width):
    for axis, dim in sides:
        count = lax.axis_size(axis)
        forward = [(i, i + 1) for i in range(count - 1)]
        backward = [(target, source) for source, target in forward]
        low = lax.ppermute(
            lax.slice_in_dim(block, block.shape[dim] - width, None, axis=dim), axis, forward
        )
        high = lax.ppermute(lax.slice_in_dim(block, 0, width, axis=dim), axis, backward)
        block = jnp.concatenate([low, block, high], axis=dim)
    return block


def layer_norm(values, norm_gain):
    values = values.astype(jnp.float32)
    center = jnp.mean(values, axis=-1, keepdims=True)
    spread = jnp.mean(jnp.square(values - center), axis=-1, keepdims=True)
    return ((values - center) * lax.rsqrt(spread + 1e-05) * norm_gain).astype(jnp.bfloat16)


def sample_points(normed, col_table, row_table, count):

    def add_row(index, total):
        plane = lax.dynamic_index_in_dim(normed, index, 0, keepdims=False)
        inner = jnp.dot(col_table, plane, preferred_element_type=jnp.float32)
        weight = lax.dynamic_index_in_dim(row_table, index, 1, keepdims=True)
        return total + weight * inner

    empty = jnp.zeros((count, normed.shape[2]), jnp.float32)
    return lax.fori_loop(0, normed.shape[0], add_row, empty)


def attend(query, key, value, heads):
    count, width = query.shape
    size = width // heads
    block = min(512, count)
    blocks = query.reshape(count // block, block, heads, size)
    key_heads = key.reshape(-1, heads, size)
    value_heads = value.reshape(-1, heads, size)
    scale = 1.0 / size**0.5

    def one_block(part):
        scores = (
            jnp.einsum("qhd,khd->hqk", part, key_heads, preferred_element_type=jnp.float32) * scale
        )
        top = jnp.max(scores, axis=-1, keepdims=True)
        expo = jnp.exp(scores - top)
        probs = (expo / jnp.sum(expo, axis=-1, keepdims=True)).astype(jnp.bfloat16)
        out = jnp.einsum("hqk,khd->qhd", probs, value_heads, preferred_element_type=jnp.float32)
        return out.astype(jnp.bfloat16).reshape(block, width)

    return lax.map(one_block, blocks).reshape(count, width)


def shards(
    tokens, corner_row, corner_col, fraction, w_query, w_key, w_value, w_out, conv_kernel, norm_gain
):
    band_rows, columns, channels = tokens.shape
    whole = lax.all_gather(tokens, "head", axis=2, tiled=True)
    normed = layer_norm(whole, norm_gain)
    width = normed.shape[2]
    count = band_rows * columns
    query = jnp.dot(
        normed.reshape(count, width), w_query, preferred_element_type=jnp.float32
    ).astype(jnp.bfloat16)
    channel_start = lax.axis_index("head") * channels
    normed_here = lax.dynamic_slice_in_dim(normed, channel_start, channels, 2)
    row_top = (1.0 - fraction[0]).astype(jnp.bfloat16)
    row_bottom = fraction[0].astype(jnp.bfloat16)
    col_left = (1.0 - fraction[1]).astype(jnp.bfloat16)
    col_right = fraction[1].astype(jnp.bfloat16)
    positions = lax.broadcasted_iota(jnp.int32, (1, columns), 1)
    zero_bf = jnp.zeros((), jnp.bfloat16)
    col_table = jnp.where(positions == corner_col[:, None], col_left[:, None], zero_bf) + jnp.where(
        positions == corner_col[:, None] + 1, col_right[:, None], zero_bf
    )
    band_start = lax.axis_index("band") * band_rows
    grid_rows = band_start + lax.broadcasted_iota(jnp.int32, (1, band_rows), 1)
    zero_f = jnp.zeros((), jnp.float32)
    row_table = jnp.where(
        grid_rows == corner_row[:, None], row_top.astype(jnp.float32)[:, None], zero_f
    ) + jnp.where(
        grid_rows == corner_row[:, None] + 1, row_bottom.astype(jnp.float32)[:, None], zero_f
    )
    points = corner_row.shape[0]
    share_rows = points // lax.axis_size("band")
    piece = summed_on_arrival(
        sample_points(normed_here, col_table, row_table, share_rows * lax.axis_size("band")).astype(
            jnp.bfloat16
        ),
        "band",
        0,
    ).astype(jnp.bfloat16)
    share = gather_directly(piece, "head", 1)
    key_share = jnp.dot(share, w_key, preferred_element_type=jnp.float32).astype(jnp.bfloat16)
    value_share = jnp.dot(share, w_value, preferred_element_type=jnp.float32).astype(jnp.bfloat16)
    key, value = sent_together((key_share, value_share), "band", 0, 1)
    heads_here = HEADS // lax.axis_size("head")
    attended = attend(query, key, value, heads_here)
    partial_out = jnp.dot(attended, w_out, preferred_element_type=jnp.float32).reshape(
        band_rows, columns, width
    )
    projected = summed_on_arrival(partial_out.astype(jnp.bfloat16), "head", 2)
    margin = KER // 2
    rimmed = padded_2(normed_here, (("band", 0),), margin)
    padded = jnp.pad(rimmed, ((0, 0), (margin, margin), (0, 0))).astype(jnp.float32)
    local = jnp.zeros((band_rows, columns, channels), jnp.float32)
    for first in range(KER):
        for second in range(KER):
            local = (
                local
                + conv_kernel[first * KER + second]
                * padded[first : first + band_rows, second : second + columns]
            )
    total = tokens.astype(jnp.float32) + projected + local
    return total.astype(jnp.bfloat16)


def solution(mesh):
    return jax.shard_map(
        shards,
        mesh=mesh,
        in_specs=(
            P(("dp", "band"), None, "head"),
            P("dp"),
            P("dp"),
            P(None, "dp"),
            P(None, "head"),
            P(None, "head"),
            P(None, "head"),
            P("head", None),
            P(None, "head"),
            P(),
        ),
        out_specs=P(("dp", "band"), None, "head"),
        check_vma=False,
    )
```

profile of v0, /device:TPU:0, one launch (start us, length us, event | category | flops | bytes accessed | tf_op | source)
XLA Modules:
  0.0 254.1 jit_solution(14506802089053671599)
XLA Ops:
  6.6 2.3 copy.36
  9.1 50.7 %all-gather.2.cloned.1.call-done = bf16[4,1024,512]{1,2,0:T(8,128)(2,1)} async-done(((bf16[4,1024,128]{1,2,0:T(8,128)(2,1)}), bf16[4,1024,512]{1,2,0:T(8,128)(2,1)}) %all-gather.2.cloned.1.call-update) | async-done | bytes 4194320 | tf_op jit(solution)/shard_map/all_gather | solution.py:105
  59.8 3.2 %convert_reduce_fusion = f32[4,1024]{1,0:T(4,128)S(1)} fusion(bf16[4,1024,512]{1,2,0:T(8,128)(2,1)} %all-gather.2.cloned.1.call-done), kind=kLoop, calls=%fused_computation.42 | loop fusion | flops 4190208 | bytes 4210688 | tf_op jit(solution)/shard_map/reduce_sum | solution.py:62
  63.0 0.2 copy-done.2
  63.2 1.1 fusion.76
  64.4 1.7 fusion.78
  66.1 1.9 copy-done.3
  68.1 6.2 %while.25 = (s32[]{:T(128)}, f32[1024,128]{0,1:T(8,128)S(1)}, f32[1024,4]{0,1:T(4,128)S(1)}, bf16[4,1024,128]{1,2,0:T(8,128)(2,1)S(1)}, s32[1024]{0:T(1024)S(1)}...) while((s32[]{:T(128)}, f32[1024,128]{0,1:T(8,128)S(1)}, ...), condition=%wide.region_3.4_spmd.clone, body=%wide.region_2.3_spmd.clone.sunk | while | flops 277217280 | bytes 1335423 | solution.py:76
  68.1 1.5 fusion.156
  69.7 1.5 fusion.156
  71.2 1.5 fusion.156
  72.8 1.5 fusion.156
  74.3 0.8 copy.41
  75.1 6.9 %all-to-all-start = ((bf16[16,64,128]{2,1,0:T(8,128)(2,1)}), bf16[16,64,128]{2,1,0:T(8,128)(2,1)S(1)}, u32[]{:S(2)}, u32[]{:S(2)}) async-start(bf16[16,64,128]{2,1,0:T(8,128)(2,1)} %bitcast.6), calls=%async_computation | async-start | bytes 524288 | tf_op jit(solution)/shard_map/all_to_all | solution.py:18
  82.1 6.3 %copy.38 = bf16[4,1024,512]{2,1,0:T(8,128)(2,1)} copy(bf16[4,1024,512]{1,2,0:T(8,128)(2,1)} %copy-done.3) | data formatting | bytes 8388608 | tf_op jit(solution)/shard_map/convert_element_type | solution.py:64
  88.4 2.2 all-to-all-done
  90.7 0.6 broadcast_in_dim.70
  91.3 3.3 %all-to-all-start.1 = ((bf16[4,64,128]{2,1,0:T(8,128)(2,1)}), bf16[4,64,128]{2,1,0:T(8,128)(2,1)S(1)}, u32[]{:S(2)}, u32[]{:S(2)}) async-start(bf16[4,64,128]{2,1,0:T(8,128)(2,1)} %broadcast_in_dim.70), calls=%async_computation.1 | async-start | bytes 131072 | tf_op jit(solution)/shard_map/all_to_all | solution.py:24
  94.6 3.4 %convolution_convert_fusion = bf16[4096,128]{1,0:T(8,128)(2,1)S(1)} fusion(bf16[4096,512]{1,0:T(8,128)(2,1)} %bitcast.143, bf16[512,128]{1,0:T(8,128)(2,1)S(1)} %copy-done.5), kind=kOutput, calls=%fused_computation.51 | convolution fusion | flops 537395200 | bytes 5373952 | tf_op jit(solution)/shard_map/dot_general | solution.py:109
  98.1 0.5 copy.39
  98.6 0.4 copy.60
  99.0 0.3 copy.45
  99.4 0.9 all-to-all-done.1
  100.3 0.2 convolution_convert_fusion.2
  100.4 0.2 convolution_convert_fusion.3
  100.6 22.4 %all_gather.7 = bf16[1024,256]{1,0:T(8,128)(2,1)S(1)} all-gather(bf16[64,256]{1,0:T(8,128)(2,1)S(1)} %pad_maximum_fusion), channel_id=1, replica_groups=mesh['band'=16,'head'=4,'dp'=2] {'band'}, dimensions={0}, use_global_device_ids=true | all-gather | bytes 557056 | tf_op jit(solution)/shard_map/all_gather | solution.py:40
  123.4 54.7 %while.24 = (s32[]{:T(128)}, bf16[8,512,128]{2,1,0:T(8,128)(2,1)}, bf16[8,512,4,32]{1,3,2,0:T(8,128)(2,1)S(1)}, bf16[1024,4,32]{0,2,1:T(8,128)(2,1)S(1)}, bf16[1024,4,32]{0,2,1:T(8,128)(2,1)S(1)}, /*index=5*/s32[]{:T(128)}) while((s32[]{:T(128)}, bf16[8,512,128]{2,1,0:T(8,128)(2,1)}, bf16[8,512,4,32]{1,3,2,0:T(8,128)(2,1)S(1)}, ...), condition=%wide.region_8.9_spmd, body=%wide.region_5.8_spmd.sunk | while | flops 417402880 | bytes 1720409 | solution.py:98
  123.4 2.9 %fusion.152 = f32[4,512]{1,0:T(4,128)S(1)} fusion(bf16[1024,4,32]{0,2,1:T(8,128)(2,1)S(1)} %get-tuple-element.380, bf16[8,512,4,32]{1,3,2,0:T(8,128)(2,1)S(1)} %get-tuple-element.379, s32[]{:T(128)S(6)} %copy.82), kind=kOutput, calls=%fused_computation.158.clone.1 | convolution fusion | flops 140510208 | bytes 401412 | tf_op jit(solution)/shard_map/while/body/eval_jaxpr/sub | solution.py:93
  126.3 3.1 %fusion.153 = bf16[4,512,32]{1,2,0:T(8,128)(2,1)S(1)} fusion(bf16[1024,4,32]{0,2,1:T(8,128)(2,1)S(1)} %get-tuple-element.381, f32[4,512]{1,0:T(4,128)S(1)} %fusion.152, bf16[1024,4,32]{0,2,1:T(8,128)(2,1)S(1)} %get-tuple-element.380, bf16[8,512,4,32]{1,3,2,0:T(8,128)(2,1)S(1)} %get-tuple-element.379, s32[]{:T(128)S(6)} %copy.82), kind=kOutput, calls=%fused_computation.8.clone.1 | convolution fusion | flops 276892672 | bytes 794628 | tf_op jit(solution)/shard_map/while/body/eval_jaxpr/hqk,khd->qhd/dot_general | solution.py:95
  129.6 0.7 constant_dynamic-update-slice_fusion.2
  130.2 2.9 %fusion.152 = f32[4,512]{1,0:T(4,128)S(1)} fusion(bf16[1024,4,32]{0,2,1:T(8,128)(2,1)S(1)} %get-tuple-element.380, bf16[8,512,4,32]{1,3,2,0:T(8,128)(2,1)S(1)} %get-tuple-element.379, s32[]{:T(128)S(6)} %copy.82), kind=kOutput, calls=%fused_computation.158.clone.1 | convolution fusion | flops 140510208 | bytes 401412 | tf_op jit(solution)/shard_map/while/body/eval_jaxpr/sub | solution.py:93
  133.1 3.1 %fusion.153 = bf16[4,512,32]{1,2,0:T(8,128)(2,1)S(1)} fusion(bf16[1024,4,32]{0,2,1:T(8,128)(2,1)S(1)} %get-tuple-element.381, f32[4,512]{1,0:T(4,128)S(1)} %fusion.152, bf16[1024,4,32]{0,2,1:T(8,128)(2,1)S(1)} %get-tuple-element.380, bf16[8,512,4,32]{1,3,2,0:T(8,128)(2,1)S(1)} %get-tuple-element.379, s32[]{:T(128)S(6)} %copy.82), kind=kOutput, calls=%fused_computation.8.clone.1 | convolution fusion | flops 276892672 | bytes 794628 | tf_op jit(solution)/shard_map/while/body/eval_jaxpr/hqk,khd->qhd/dot_general | solution.py:95
  136.4 0.7 constant_dynamic-update-slice_fusion.2
  137.0 2.9 %fusion.152 = f32[4,512]{1,0:T(4,128)S(1)} fusion(bf16[1024,4,32]{0,2,1:T(8,128)(2,1)S(1)} %get-tuple-element.380, bf16[8,512,4,32]{1,3,2,0:T(8,128)(2,1)S(1)} %get-tuple-element.379, s32[]{:T(128)S(6)} %copy.82), kind=kOutput, calls=%fused_computation.158.clone.1 | convolution fusion | flops 140510208 | bytes 401412 | tf_op jit(solution)/shard_map/while/body/eval_jaxpr/sub | solution.py:93
  140.0 3.1 %fusion.153 = bf16[4,512,32]{1,2,0:T(8,128)(2,1)S(1)} fusion(bf16[1024,4,32]{0,2,1:T(8,128)(2,1)S(1)} %get-tuple-element.381, f32[4,512]{1,0:T(4,128)S(1)} %fusion.152, bf16[1024,4,32]{0,2,1:T(8,128)(2,1)S(1)} %get-tuple-element.380, bf16[8,512,4,32]{1,3,2,0:T(8,128)(2,1)S(1)} %get-tuple-element.379, s32[]{:T(128)S(6)} %copy.82), kind=kOutput, calls=%fused_computation.8.clone.1 | convolution fusion | flops 276892672 | bytes 794628 | tf_op jit(solution)/shard_map/while/body/eval_jaxpr/hqk,khd->qhd/dot_general | solution.py:95
  143.2 0.7 constant_dynamic-update-slice_fusion.2
  143.9 2.9 %fusion.152 = f32[4,512]{1,0:T(4,128)S(1)} fusion(bf16[1024,4,32]{0,2,1:T(8,128)(2,1)S(1)} %get-tuple-element.380, bf16[8,512,4,32]{1,3,2,0:T(8,128)(2,1)S(1)} %get-tuple-element.379, s32[]{:T(128)S(6)} %copy.82), kind=kOutput, calls=%fused_computation.158.clone.1 | convolution fusion | flops 140510208 | bytes 401412 | tf_op jit(solution)/shard_map/while/body/eval_jaxpr/sub | solution.py:93
  146.8 3.1 %fusion.153 = bf16[4,512,32]{1,2,0:T(8,128)(2,1)S(1)} fusion(bf16[1024,4,32]{0,2,1:T(8,128)(2,1)S(1)} %get-tuple-element.381, f32[4,512]{1,0:T(4,128)S(1)} %fusion.152, bf16[1024,4,32]{0,2,1:T(8,128)(2,1)S(1)} %get-tuple-element.380, bf16[8,512,4,32]{1,3,2,0:T(8,128)(2,1)S(1)} %get-tuple-element.379, s32[]{:T(128)S(6)} %copy.82), kind=kOutput, calls=%fused_computation.8.clone.1 | convolution fusion | flops 276892672 | bytes 794628 | tf_op jit(solution)/shard_map/while/body/eval_jaxpr/hqk,khd->qhd/dot_general | solution.py:95
  150.0 0.7 constant_dynamic-update-slice_fusion.2
  150.7 2.9 %fusion.152 = f32[4,512]{1,0:T(4,128)S(1)} fusion(bf16[1024,4,32]{0,2,1:T(8,128)(2,1)S(1)} %get-tuple-element.380, bf16[8,512,4,32]{1,3,2,0:T(8,128)(2,1)S(1)} %get-tuple-element.379, s32[]{:T(128)S(6)} %copy.82), kind=kOutput, calls=%fused_computation.158.clone.1 | convolution fusion | flops 140510208 | bytes 401412 | tf_op jit(solution)/shard_map/while/body/eval_jaxpr/sub | solution.py:93
  153.7 3.1 %fusion.153 = bf16[4,512,32]{1,2,0:T(8,128)(2,1)S(1)} fusion(bf16[1024,4,32]{0,2,1:T(8,128)(2,1)S(1)} %get-tuple-element.381, f32[4,512]{1,0:T(4,128)S(1)} %fusion.152, bf16[1024,4,32]{0,2,1:T(8,128)(2,1)S(1)} %get-tuple-element.380, bf16[8,512,4,32]{1,3,2,0:T(8,128)(2,1)S(1)} %get-tuple-element.379, s32[]{:T(128)S(6)} %copy.82), kind=kOutput, calls=%fused_computation.8.clone.1 | convolution fusion | flops 276892672 | bytes 794628 | tf_op jit(solution)/shard_map/while/body/eval_jaxpr/hqk,khd->qhd/dot_general | solution.py:95
  156.9 0.7 constant_dynamic-update-slice_fusion.2
  157.6 2.9 %fusion.152 = f32[4,512]{1,0:T(4,128)S(1)} fusion(bf16[1024,4,32]{0,2,1:T(8,128)(2,1)S(1)} %get-tuple-element.380, bf16[8,512,4,32]{1,3,2,0:T(8,128)(2,1)S(1)} %get-tuple-element.379, s32[]{:T(128)S(6)} %copy.82), kind=kOutput, calls=%fused_computation.158.clone.1 | convolution fusion | flops 140510208 | bytes 401412 | tf_op jit(solution)/shard_map/while/body/eval_jaxpr/sub | solution.py:93
  160.5 3.1 %fusion.153 = bf16[4,512,32]{1,2,0:T(8,128)(2,1)S(1)} fusion(bf16[1024,4,32]{0,2,1:T(8,128)(2,1)S(1)} %get-tuple-element.381, f32[4,512]{1,0:T(4,128)S(1)} %fusion.152, bf16[1024,4,32]{0,2,1:T(8,128)(2,1)S(1)} %get-tuple-element.380, bf16[8,512,4,32]{1,3,2,0:T(8,128)(2,1)S(1)} %get-tuple-element.379, s32[]{:T(128)S(6)} %copy.82), kind=kOutput, calls=%fused_computation.8.clone.1 | convolution fusion | flops 276892672 | bytes 794628 | tf_op jit(solution)/shard_map/while/body/eval_jaxpr/hqk,khd->qhd/dot_general | solution.py:95
  163.7 0.7 constant_dynamic-update-slice_fusion.2
  164.4 2.9 %fusion.152 = f32[4,512]{1,0:T(4,128)S(1)} fusion(bf16[1024,4,32]{0,2,1:T(8,128)(2,1)S(1)} %get-tuple-element.380, bf16[8,512,4,32]{1,3,2,0:T(8,128)(2,1)S(1)} %get-tuple-element.379, s32[]{:T(128)S(6)} %copy.82), kind=kOutput, calls=%fused_computation.158.clone.1 | convolution fusion | flops 140510208 | bytes 401412 | tf_op jit(solution)/shard_map/while/body/eval_jaxpr/sub | solution.py:93
  167.3 3.1 %fusion.153 = bf16[4,512,32]{1,2,0:T(8,128)(2,1)S(1)} fusion(bf16[1024,4,32]{0,2,1:T(8,128)(2,1)S(1)} %get-tuple-element.381, f32[4,512]{1,0:T(4,128)S(1)} %fusion.152, bf16[1024,4,32]{0,2,1:T(8,128)(2,1)S(1)} %get-tuple-element.380, bf16[8,512,4,32]{1,3,2,0:T(8,128)(2,1)S(1)} %get-tuple-element.379, s32[]{:T(128)S(6)} %copy.82), kind=kOutput, calls=%fused_computation.8.clone.1 | convolution fusion | flops 276892672 | bytes 794628 | tf_op jit(solution)/shard_map/while/body/eval_jaxpr/hqk,khd->qhd/dot_general | solution.py:95
  170.6 0.7 constant_dynamic-update-slice_fusion.2
  171.2 2.9 %fusion.152 = f32[4,512]{1,0:T(4,128)S(1)} fusion(bf16[1024,4,32]{0,2,1:T(8,128)(2,1)S(1)} %get-tuple-element.380, bf16[8,512,4,32]{1,3,2,0:T(8,128)(2,1)S(1)} %get-tuple-element.379, s32[]{:T(128)S(6)} %copy.82), kind=kOutput, calls=%fused_computation.158.clone.1 | convolution fusion | flops 140510208 | bytes 401412 | tf_op jit(solution)/shard_map/while/body/eval_jaxpr/sub | solution.py:93
  174.2 3.1 %fusion.153 = bf16[4,512,32]{1,2,0:T(8,128)(2,1)S(1)} fusion(bf16[1024,4,32]{0,2,1:T(8,128)(2,1)S(1)} %get-tuple-element.381, f32[4,512]{1,0:T(4,128)S(1)} %fusion.152, bf16[1024,4,32]{0,2,1:T(8,128)(2,1)S(1)} %get-tuple-element.380, bf16[8,512,4,32]{1,3,2,0:T(8,128)(2,1)S(1)} %get-tuple-element.379, s32[]{:T(128)S(6)} %copy.82), kind=kOutput, calls=%fused_computation.8.clone.1 | convolution fusion | flops 276892672 | bytes 794628 | tf_op jit(solution)/shard_map/while/body/eval_jaxpr/hqk,khd->qhd/dot_general | solution.py:95
  177.4 0.7 constant_dynamic-update-slice_fusion.2
  178.1 2.5 convolution_convert_fusion.1
  180.6 2.4 copy.70
  183.0 4.9 %all-to-all-start.2 = ((bf16[4,4,1024,128]{2,3,1,0:T(8,128)(2,1)}), bf16[4,4,1024,128]{2,3,1,0:T(8,128)(2,1)}, u32[]{:S(2)}, u32[]{:S(2)}) async-start(bf16[4,4,1024,128]{2,3,1,0:T(8,128)(2,1)} %bitcast.144), calls=%async_computation.2 | async-start | bytes 8388608 | tf_op jit(solution)/shard_map/all_to_all | solution.py:18
  187.9 1.3 constant_dynamic-slice_fusion.2
  189.2 3.2 %collective-permute-start = (bf16[2,1024,128]{1,2,0:T(8,128)(2,1)S(1)}, bf16[2,1024,128]{1,2,0:T(8,128)(2,1)S(1)}, u32[]{:S(2)}, u32[]{:S(2)}) collective-permute-start(bf16[2,1024,128]{1,2,0:T(8,128)(2,1)S(1)} %get-tuple-element.225), channel_id=1, source_target_pairs={{0,8},{8,16},{16,24},{24,32},{32,40},{40,48},{48,56},{56,64},{64,7... | collective-permute-start | bytes 1572872 | tf_op jit(solution)/shard_map/ppermute | solution.py:52
  192.4 1.5 collective-permute-start.1
  194.0 5.1 %collective-permute-done = bf16[2,1024,128]{1,2,0:T(8,128)(2,1)S(1)} collective-permute-done((bf16[2,1024,128]{1,2,0:T(8,128)(2,1)S(1)}, bf16[2,1024,128]{1,2,0:T(8,128)(2,1)S(1)}, u32[]{:S(2)}, u32[]{:S(2)}) %collective-permute-start) | collective-permute-done | bytes 524320 | tf_op jit(solution)/shard_map/ppermute | solution.py:52
  199.0 4.4 %collective-permute-done.1 = bf16[2,1024,128]{1,2,0:T(8,128)(2,1)S(1)} collective-permute-done((bf16[2,1024,128]{1,2,0:T(8,128)(2,1)S(1)}, bf16[2,1024,128]{1,2,0:T(8,128)(2,1)S(1)}, u32[]{:S(2)}, u32[]{:S(2)}) %collective-permute-start.1) | collective-permute-done | bytes 524320 | tf_op jit(solution)/shard_map/ppermute | solution.py:55
  203.5 2.9 %fusion.85 = f32[8,1028,128]{1,2,0:T(8,128)} fusion(bf16[2,1024,128]{1,2,0:T(8,128)(2,1)S(1)} %collective-permute-done.1, bf16[4,1024,128]{1,2,0:T(8,128)(2,1)S(1)} %get-tuple-element.389, bf16[2,1024,128]{1,2,0:T(8,128)(2,1)S(1)} %collective-permute-done), kind=kLoop, calls=%fused_computation.60 | loop fusion | flops 12632064 | bytes 6307840 | tf_op jit(solution)/shard_map/convert_element_type | solution.py:152
  206.3 24.3 %all-to-all-done.2 = bf16[4,4,1024,128]{2,3,1,0:T(8,128)(2,1)} async-done(((bf16[4,4,1024,128]{2,3,1,0:T(8,128)(2,1)}), bf16[4,4,1024,128]{2,3,1,0:T(8,128)(2,1)}, u32[]{:S(2)}, u32[]{:S(2)}) %all-to-all-start.2) | async-done | bytes 4194336 | tf_op jit(solution)/shard_map/all_to_all | solution.py:18
  230.6 3.6 %convert_reduce_fusion.1 = f32[4,1024,128]{1,2,0:T(8,128)S(1)} fusion(bf16[4,4,1024,128]{2,3,1,0:T(8,128)(2,1)} %all-to-all-done.2), kind=kLoop, calls=%fused_computation.48 | loop fusion | flops 3670016 | bytes 6291456 | tf_op jit(solution)/shard_map/reduce_sum | solution.py:19
  234.2 11.8 %fusion.88 = bf16[4,1024,128]{1,2,0:T(8,128)(2,1)S(1)} fusion(f32[8,1028,128]{1,2,0:T(8,128)S(1)} %copy-done.1, f32[4,1024,128]{1,2,0:T(8,128)S(1)} %convert_reduce_fusion.1, bf16[4,1024,128]{1,2,0:T(8,128)(2,1)S(1)} %copy-done.4, f32[128]{0:T(128)S(1)} %get-tuple-element.252, f32[128]{0:T(128)S(1)} %get-tuple-element.253, f32[128]{0:T(128)S(1)} %get-tuple-element.230, ...), kind=kLoop, calls=%fused_computation.64 | loop fusion | flops 27787264 | bytes 56635904 | tf_op jit(solution)/shard_map/convert_element_type | solution.py:162
  246.0 1.3 copy.50
  (56 shorter events, 1.8 us)
Async XLA Ops:
  6.5 171.5 %copy-start = (bf16[128,512]{1,0:T(8,128)(2,1)S(1)}, bf16[128,512]{1,0:T(8,128)(2,1)}, u32[]{:S(2)}) copy-start(bf16[128,512]{1,0:T(8,128)(2,1)} %param.21) | copy-start | bytes 393220
  6.5 2.4 copy-start.9
  6.5 2.4 copy-start.11
  6.5 2.4 copy-start.8
  6.5 53.2 %all-gather.2.cloned.1.call-start = ((), (), s32[]{:S(2)}) async-start(), calls=%async_computation.3 | async-start | bytes 5242880 | tf_op jit(solution)/shard_map/all_gather | solution.py:105
  59.8 3.4 %copy-start.2 = (bf16[4,1024,512]{1,2,0:T(8,128)(2,1)S(1)}, bf16[4,1024,512]{1,2,0:T(8,128)(2,1)}, u32[]{:S(2)}) copy-start(bf16[4,1024,512]{1,2,0:T(8,128)(2,1)} %all-gather.2.cloned.1.call-done) | copy-start | bytes 12582916
  63.2 1.1 copy-start.12
  66.1 1.9 copy-start.3
  75.1 15.5 %all-to-all-start = ((bf16[16,64,128]{2,1,0:T(8,128)(2,1)}), bf16[16,64,128]{2,1,0:T(8,128)(2,1)S(1)}, u32[]{:S(2)}, u32[]{:S(2)}) async-start(bf16[16,64,128]{2,1,0:T(8,128)(2,1)} %bitcast.6), calls=%async_computation | async-start | bytes 524288 | tf_op jit(solution)/shard_map/all_to_all | solution.py:18
  82.1 12.5 %copy-start.5 = (bf16[512,128]{1,0:T(8,128)(2,1)S(1)}, bf16[512,128]{1,0:T(8,128)(2,1)}, u32[]{:S(2)}) copy-start(bf16[512,128]{1,0:T(8,128)(2,1)} %param.18) | copy-start | bytes 393220
  91.3 9.0 %all-to-all-start.1 = ((bf16[4,64,128]{2,1,0:T(8,128)(2,1)}), bf16[4,64,128]{2,1,0:T(8,128)(2,1)S(1)}, u32[]{:S(2)}, u32[]{:S(2)}) async-start(bf16[4,64,128]{2,1,0:T(8,128)(2,1)} %broadcast_in_dim.70), calls=%async_computation.1 | async-start | bytes 131072 | tf_op jit(solution)/shard_map/all_to_all | solution.py:24
  98.6 1.6 copy-start.6
  98.6 1.8 copy-start.7
  183.0 47.6 %all-to-all-start.2 = ((bf16[4,4,1024,128]{2,3,1,0:T(8,128)(2,1)}), bf16[4,4,1024,128]{2,3,1,0:T(8,128)(2,1)}, u32[]{:S(2)}, u32[]{:S(2)}) async-start(bf16[4,4,1024,128]{2,3,1,0:T(8,128)(2,1)} %bitcast.144), calls=%async_computation.2 | async-start | bytes 8388608 | tf_op jit(solution)/shard_map/all_to_all | solution.py:18
  187.9 6.0 %copy-start.10 = (f32[25,128]{1,0:T(8,128)S(1)}, f32[25,128]{1,0:T(8,128)}, u32[]{:S(2)}) copy-start(f32[25,128]{1,0:T(8,128)} %param.22) | copy-start | bytes 38404
  189.2 9.8 %collective-permute-start = (bf16[2,1024,128]{1,2,0:T(8,128)(2,1)S(1)}, bf16[2,1024,128]{1,2,0:T(8,128)(2,1)S(1)}, u32[]{:S(2)}, u32[]{:S(2)}) collective-permute-start(bf16[2,1024,128]{1,2,0:T(8,128)(2,1)S(1)} %get-tuple-element.225), channel_id=1, source_target_pairs={{0,8},{8,16},{16,24},{24,32},{32,40},{40,48},{48,56},{56,64},{64,7... | collective-permute-start | bytes 1572872 | tf_op jit(solution)/shard_map/ppermute | solution.py:52
  192.4 11.1 %collective-permute-start.1 = (bf16[2,1024,128]{1,2,0:T(8,128)(2,1)S(1)}, bf16[2,1024,128]{1,2,0:T(8,128)(2,1)S(1)}, u32[]{:S(2)}, u32[]{:S(2)}) collective-permute-start(bf16[2,1024,128]{1,2,0:T(8,128)(2,1)S(1)} %get-tuple-element.226), channel_id=1, source_target_pairs={{8,0},{16,8},{24,16},{32,24},{40,32},{48,40},{56,48},{64,56},{72,6... | collective-permute-start | bytes 1572872 | tf_op jit(solution)/shard_map/ppermute | solution.py:55
  206.3 27.9 %copy-start.4 = (bf16[4,1024,128]{1,2,0:T(8,128)(2,1)S(1)}, bf16[4,1024,128]{1,2,0:T(8,128)(2,1)}, u32[]{:S(2)}) copy-start(bf16[4,1024,128]{1,2,0:T(8,128)(2,1)} %copy.36) | copy-start | bytes 3145732
  230.6 3.6 %copy-start.1 = (f32[8,1028,128]{1,2,0:T(8,128)S(1)}, f32[8,1028,128]{1,2,0:T(8,128)}, u32[]{:S(2)}) copy-start(f32[8,1028,128]{1,2,0:T(8,128)} %fusion.85) | copy-start | bytes 12632068
Sparse Core Ops, SparseCore 0:
  9.0 50.6 all-gather.1
where the time goes:
time: 255 us; the launch traced here: 254 us
  waiting for transfers between devices  87.5 us (34%)
  matrix products  60.5 us (24%)
  local copies, waits for them, and re-layouts  25.4 us (10%)
  other arithmetic  24.4 us (10%)
  blocking collectives  22.4 us (9%)
  starting transfers between devices  19.9 us (8%)
  between operations  13.7 us (5%)
    all_gather x1, waiting for transfers between devices, shards(): whole = lax.all_gather(tokens, 'head', axis=2, tiled=True)  50.7 us
    all_to_all x2, waiting for transfers between devices, summed_on_arrival(): blocks = lax.all_to_all(cut_along(x, dim, devices), axis, 0, 0, tiled=True)  26.5 us
    dot_general x8, matrix products, one_block(): jnp.einsum('hqk,khd->qhd', probs, value_heads, preferred_element_type=jnp...  24.8 us
    sub x8, matrix products, one_block(): expo = jnp.exp(scores - top)  23.4 us
    all_gather x1, blocking collectives, sent_together(): lax.all_gather(both, axis, axis=dim, tiled=True)  22.4 us
    all_to_all x2, starting transfers between devices, summed_on_arrival(): blocks = lax.all_to_all(cut_along(x, dim, devices), axis, 0, 0, tiled=True)  11.8 us
    convert_element_type x1, other arithmetic, shards(): return total.astype(jnp.bfloat16)  11.8 us
    dynamic_update_slice x16, local copies, waits for them, and re-layouts, attend(): return lax.map(one_block, blocks).reshape(count, width)  6.39 us
  transfers between devices with their start and end apart: 6, of which 6 were waited for; matrix products, arithmetic and copies ran while one was open for 6% of the time, Pallas kernels for 0%

commit v1 on v0

v1 whole, which is shorter than its diff:
```python
import functools

import jax
import jax.numpy as jnp
from jax import lax
from jax.experimental import pallas as pl
from jax.experimental.pallas import tpu as pltpu
from jax.sharding import PartitionSpec as P


HEADS = 16
KER = 5
EPS = 1e-05
F32 = jnp.float32
BF = jnp.bfloat16
ROW_BY_ROW = (((1,), (1,)), ((), ()))
COLUMN_BY_COLUMN = (((0,), (0,)), ((), ()))


def from_everyone(x, axis):
    copies = jnp.broadcast_to(x, (lax.axis_size(axis), *x.shape))
    return lax.all_to_all(copies, axis, split_axis=0, concat_axis=0, tiled=True)


def split_in_two(x):
    high = x.astype(BF)
    return high, (x - high.astype(F32)).astype(BF)


def split_in_three(x):
    high = x.astype(BF)
    rest = x - high.astype(F32)
    middle = rest.astype(BF)
    return high, middle, (rest - middle.astype(F32)).astype(BF)


def moments_kernel(tokens_ref, out_ref):
    rows, columns, channels = tokens_ref.shape
    ones = jnp.ones((8, channels), BF)
    average = jnp.full((channels, channels), 1.0 / channels, BF)
    for row in range(rows):
        block = tokens_ref[row]
        center = jnp.dot(block, average, preferred_element_type=F32)
        square = jnp.square(block.astype(F32) - center)
        high, low = split_in_two(square)
        total = lax.dot_general(ones, block, ROW_BY_ROW, preferred_element_type=F32)
        spread = lax.dot_general(ones, high, ROW_BY_ROW, preferred_element_type=F32)
        spread = spread + lax.dot_general(ones, low, ROW_BY_ROW, preferred_element_type=F32)
        at = pl.ds(row * columns, columns)
        for copy in range(out_ref.shape[0]):
            out_ref[copy, 0:1, at] = total[0:1]
            out_ref[copy, 1:2, at] = spread[0:1]


def local_moments(tokens, copies):
    rows, columns, _ = tokens.shape
    return pl.pallas_call(
        moments_kernel,
        out_shape=jax.ShapeDtypeStruct((copies, 2, rows * columns), F32),
        cost_estimate=pl.CostEstimate(flops=10**9, bytes_accessed=2**20, transcendentals=0),
        name="moments",
    )(tokens)


def normalize_sample_kernel(
    tokens_ref, moments_ref, gain_ref, table_ref, weight_ref, normed_ref, sampled_ref, planes
):
    rows, columns, channels = tokens_ref.shape
    devices = moments_ref.shape[0]
    sums = [moments_ref[d, 0:1, :] for d in range(devices)]
    width = channels * devices
    center = functools.reduce(jnp.add, sums) * (1.0 / width)
    spread = functools.reduce(jnp.add, [moments_ref[d, 1:2, :] for d in range(devices)])
    for d in range(devices):
        spread = spread + channels * jnp.square(sums[d] * (1.0 / channels) - center)
    factor = lax.rsqrt(spread * (1.0 / width) + EPS)
    pieces = [*split_in_three(center), *split_in_three(factor)]
    pieces += [jnp.zeros_like(pieces[0])] * 10
    stacked = jnp.concatenate([p.astype(F32) for p in pieces], axis=0).astype(BF)
    piece = lax.broadcasted_iota(jnp.int32, (16, 2 * channels), 0)
    lane = lax.broadcasted_iota(jnp.int32, (16, 2 * channels), 1)
    pick = jnp.where((piece < 6) & (piece // 3 == lane // channels), 1.0, 0.0).astype(BF)
    for row in range(rows):
        part = stacked[:, row * columns : (row + 1) * columns]
        spreadout = lax.dot_general(part, pick, COLUMN_BY_COLUMN, preferred_element_type=F32)
        values = tokens_ref[row].astype(F32) - spreadout[:, :channels]
        values = (values * spreadout[:, channels:] * gain_ref[...]).astype(BF)
        normed_ref[row] = values
        planes[:, row * channels : (row + 1) * channels] = values
    inner = jnp.dot(table_ref[...], planes[...], preferred_element_type=F32)
    total = None
    for row in range(rows):
        at = slice(row * channels, (row + 1) * channels)
        part = weight_ref[:, at].astype(F32) * inner[:, at]
        total = part if total is None else total + part
    sampled_ref[...] = total.astype(BF)


def normalize_and_sample(tokens, moments, gain, table, weight):
    rows, columns, channels = tokens.shape
    points = table.shape[0]
    return pl.pallas_call(
        normalize_sample_kernel,
        out_shape=(
            jax.ShapeDtypeStruct(tokens.shape, BF),
            jax.ShapeDtypeStruct((points, channels), BF),
        ),
        scratch_shapes=[pltpu.VMEM((columns, rows * channels), BF)],
        cost_estimate=pl.CostEstimate(flops=2 * 10**9, bytes_accessed=6 * 2**20, transcendentals=0),
        name="normalize_sample",
    )(tokens, moments, gain, table, weight)


def query_kernel(scale, place_ref, *refs):
    *row_refs, gain_ref, weight_ref, out_ref = refs
    groups = len(row_refs)
    channels = row_refs[0].shape[1]
    width = groups * channels
    parts = [ref[...].astype(F32) for ref in row_refs]
    center = sum(jnp.sum(p, axis=1, keepdims=True) for p in parts) * (1.0 / width)
    parts = [p - center for p in parts]
    spread = sum(jnp.sum(jnp.square(p), axis=1, keepdims=True) for p in parts) * (1.0 / width)
    factor = lax.rsqrt(spread + EPS)
    normed, lines = [], []
    for distance, part in enumerate(parts):
        source = lax.rem(place_ref[0] + (groups - distance), groups)
        normed.append((part * factor * gain_ref[pl.ds(source, 1), :]).astype(BF))
        line = pl.ds(pl.multiple_of(source * channels, channels), channels)
        lines.append(jnp.concatenate([weight_ref[g, line, :] for g in range(groups)], axis=1))
    normed = jnp.concatenate(normed, axis=1)
    weight = jnp.concatenate(lines, axis=0)
    query = jnp.dot(normed, weight, preferred_element_type=F32) * scale
    for g in range(groups):
        out_ref[g] = query[:, g * channels : (g + 1) * channels].astype(BF)


def query_of(place, row, gain, weight, columns, scale):
    groups = len(row)
    channels = row[0].shape[1]
    depth = weight.shape[2]
    block = 256
    return pl.pallas_call(
        functools.partial(query_kernel, scale),
        grid_spec=pltpu.PrefetchScalarGridSpec(
            num_scalar_prefetch=1,
            grid=(columns // block,),
            in_specs=[pl.BlockSpec((block, channels), lambda i, place: (i, 0))] * groups
            + [
                pl.BlockSpec(gain.shape, lambda i, place: (0, 0)),
                pl.BlockSpec((groups, None, depth, channels), lambda i, place: (0, 0, 0, 0)),
            ],
            out_specs=pl.BlockSpec((groups, block, channels), lambda i, place: (0, i, 0)),
        ),
        out_shape=jax.ShapeDtypeStruct((groups, columns, channels), BF),
        cost_estimate=pl.CostEstimate(flops=2 * 10**9, bytes_accessed=3 * 2**20, transcendentals=0),
        name="query",
    )(place, *row, gain, weight)


def key_value_kernel(blocks_ref, key_weight_ref, value_weight_ref, key_ref, value_ref, sampled):
    bands, groups, share, channels = blocks_ref.shape
    for b in range(bands):
        for g in range(groups):
            sampled[b * share : (b + 1) * share, g * channels : (g + 1) * channels] = blocks_ref[b, g]
    for g in range(groups):
        weight = jnp.concatenate([key_weight_ref[g], value_weight_ref[g]], axis=1)
        product = jnp.dot(sampled[...], weight, preferred_element_type=F32)
        key_ref[g] = product[:, :channels].astype(BF)
        value_ref[g] = product[:, channels:].astype(BF)


def keys_and_values(blocks, early, late):
    bands, groups, share, channels = blocks.shape
    depth = early.shape[2]
    out = jax.ShapeDtypeStruct((groups, bands * share, channels), BF)
    whole = pl.BlockSpec((groups, bands * share, channels), lambda i: (0, 0, 0))
    return pl.pallas_call(
        key_value_kernel,
        grid=(1,),
        in_specs=[
            pl.BlockSpec(blocks.shape, lambda i: (0, 0, 0, 0)),
            pl.BlockSpec((groups, None, depth, channels), lambda i: (0, 1, 0, 0)),
            pl.BlockSpec((groups, None, depth, channels), lambda i: (0, 0, 0, 0)),
        ],
        out_specs=(whole, whole),
        out_shape=(out, out),
        scratch_shapes=[pltpu.VMEM((bands * share, depth), BF)],
        cost_estimate=pl.CostEstimate(flops=2 * 10**9, bytes_accessed=4 * 2**20, transcendentals=0),
        name="key_value",
    )(blocks, early, late)


def attend_kernel(
    per_group, query_ref, key_ref, value_ref, weight_ref, out_ref, attended, joined
):
    groups, block, channels = query_ref.shape
    head = lax.broadcasted_iota(jnp.int32, (1, channels), 1) // (channels // per_group)
    zero = jnp.zeros((), BF)

    @pl.when(pl.program_id(0) == 0)
    def _():
        for g in range(groups):
            lines = slice(g * channels, (g + 1) * channels)
            for j in range(groups):
                at = slice(j * channels, (j + 1) * channels)
                joined[lines, at] = weight_ref[g, at, :]

    one = jnp.ones((), BF)
    for g in range(groups):
        total = jnp.zeros((block, 2 * channels), F32)
        for h in range(per_group):
            key = jnp.where(head == h, key_ref[g], zero)
            scores = lax.dot_general(query_ref[g], key, ROW_BY_ROW, preferred_element_type=F32)
            top = jnp.max(scores, axis=-1, keepdims=True)
            probs = jnp.exp2(scores - top).astype(BF)
            value = jnp.where(head == h, value_ref[g], zero)
            ones = jnp.broadcast_to(jnp.where(head == h, one, zero), value.shape)
            both = jnp.concatenate([value, ones], axis=1)
            total = total + jnp.dot(probs, both, preferred_element_type=F32)
        at = slice(g * channels, (g + 1) * channels)
        attended[:, at] = (total[:, :channels] / total[:, channels:]).astype(BF)
    projected = jnp.dot(attended[...], joined[...], preferred_element_type=F32)
    for g in range(groups):
        out_ref[g] = projected[:, g * channels : (g + 1) * channels].astype(BF)


def attend_and_project(query, key, value, weight, first, count):
    groups, _, channels = query.shape
    points = key.shape[1]
    block = 256
    width = groups * channels
    start = first // block
    whole = pl.BlockSpec(key.shape, lambda i: (0, 0, 0))
    return pl.pallas_call(
        functools.partial(attend_kernel, HEADS // groups),
        grid=(count // block,),
        in_specs=[
            pl.BlockSpec((groups, block, channels), lambda i: (0, i + start, 0)),
            whole,
            whole,
            pl.BlockSpec((groups, None, width, channels), lambda i: (0, 1, 0, 0)),
        ],
        out_specs=pl.BlockSpec((groups, block, channels), lambda i: (0, i, 0)),
        out_shape=jax.ShapeDtypeStruct((groups, count, channels), BF),
        scratch_shapes=[pltpu.VMEM((block, width), BF), pltpu.VMEM((width, width), BF)],
        cost_estimate=pl.CostEstimate(
            flops=4 * count * points * width, bytes_accessed=4 * 2**20, transcendentals=0
        ),
        name="attend",
    )(query, key, value, weight)


def convolve_kernel(low_ref, normed_ref, high_ref, tokens_ref, taps_ref, out_ref, padded):
    rows, columns, channels = normed_ref.shape
    margin = KER // 2
    pad = 8
    padded[:, 0:pad, :] = jnp.zeros((rows + 2 * margin, pad, channels), F32)
    padded[:, pad + columns :, :] = jnp.zeros((rows + 2 * margin, pad, channels), F32)
    padded[0:margin, pad : pad + columns, :] = low_ref[...].astype(F32)
    padded[margin : margin + rows, pad : pad + columns, :] = normed_ref[...].astype(F32)
    padded[margin + rows :, pad : pad + columns, :] = high_ref[...].astype(F32)
    taps = taps_ref[...]
    strip = 8

    def one_strip(index, carry):
        start = pl.multiple_of(index * strip, strip)
        totals = [tokens_ref[r, pl.ds(start, strip), :].astype(F32) for r in range(rows)]
        for second in range(KER):
            for line in range(rows + 2 * margin):
                values = padded[line, pl.ds(start + pad - margin + second, strip), :]
                for r in range(rows):
                    first = line - r
                    if 0 <= first < KER:
                        tap = first * KER + second
                        totals[r] = totals[r] + taps[tap : tap + 1, :] * values
        for r in range(rows):
            out_ref[r, pl.ds(start, strip), :] = totals[r]
        return carry

    lax.fori_loop(0, columns // strip, one_strip, 0)


def convolve(low, normed, high, tokens, taps):
    rows, columns, channels = normed.shape
    return pl.pallas_call(
        convolve_kernel,
        out_shape=jax.ShapeDtypeStruct(normed.shape, F32),
        scratch_shapes=[pltpu.VMEM((rows + 2 * (KER // 2), columns + 16, channels), F32)],
        cost_estimate=pl.CostEstimate(
            flops=10**9, bytes_accessed=6 * 2**20, transcendentals=0
        ),
        name="convolve",
    )(low, normed, high, tokens, taps)


def column_table(corner_col, col_left, col_right, columns):
    positions = lax.broadcasted_iota(jnp.int32, (1, columns), 1)
    zero = jnp.zeros((), BF)
    left = jnp.where(positions == corner_col[:, None], col_left[:, None], zero)
    right = jnp.where(positions == corner_col[:, None] + 1, col_right[:, None], zero)
    return left + right


def row_weights(corner_row, row_top, row_bottom, band_start, rows, channels):
    grid_rows = band_start + lax.broadcasted_iota(jnp.int32, (1, rows * channels), 1) // channels
    zero = jnp.zeros((), BF)
    top = jnp.where(grid_rows == corner_row[:, None], row_top[:, None], zero)
    bottom = jnp.where(grid_rows == corner_row[:, None] + 1, row_bottom[:, None], zero)
    return top + bottom


def body(
    tokens, corner_row, corner_col, fraction, w_query, w_key, w_value, w_out, conv_kernel, norm_gain
):
    rows, columns, channels = tokens.shape
    groups = lax.axis_size("head")
    bands = lax.axis_size("band")
    width = groups * channels
    points = corner_row.shape[0]
    share = points // bands

    place = lax.axis_index("head")
    core = lax.axis_index("dp")
    moments = local_moments(tokens, groups)
    moments = lax.all_to_all(moments, "head", 0, 0, tiled=True)
    stacked_out = [w_out[:, g * channels : (g + 1) * channels] for g in range(groups)]
    first = jnp.concatenate([w_query, w_key], axis=0)
    second = jnp.concatenate([w_value, *stacked_out], axis=0)
    half = jnp.where(core == 0, first, second)
    bulk = [
        jnp.concatenate(
            [
                lax.dynamic_index_in_dim(
                    tokens, lax.rem(place + distance, groups), 0, keepdims=False
                ),
                half,
            ],
            axis=0,
        )
        for distance in range(1, groups)
    ]
    arrived = []
    for distance in (2, 1, 3):
        ring = [(i, (i + distance) % groups) for i in range(groups)]
        arrived.append((distance, lax.ppermute(bulk[distance - 1], "head", ring)))
    arrived = [block for _, block in sorted(arrived, key=lambda item: item[0])]
    other = [lax.ppermute(a[columns:], "dp", [(0, 1), (1, 0)]) for a in arrived]
    depth = w_query.shape[0]
    early = [first] + [jnp.where(core == 0, a[columns:], o) for a, o in zip(arrived, other)]
    late = [second] + [jnp.where(core == 0, o, a[columns:]) for a, o in zip(arrived, other)]
    early = jnp.stack(early).reshape(groups, 2, depth, channels)
    late = jnp.stack(late).reshape(groups, 2, depth, channels)
    own_row = lax.dynamic_index_in_dim(tokens, place, 0, keepdims=False)

    row_top = (1.0 - fraction[0]).astype(BF)
    row_bottom = fraction[0].astype(BF)
    col_left = (1.0 - fraction[1]).astype(BF)
    col_right = fraction[1].astype(BF)
    table = column_table(corner_col, col_left, col_right, columns)
    weight = row_weights(
        corner_row, row_top, row_bottom, lax.axis_index("band") * rows, rows, channels
    )
    gain = norm_gain.reshape(groups, channels)
    gain_here = lax.dynamic_slice_in_dim(gain, lax.axis_index("head"), 1, 0)
    normed, partial = normalize_and_sample(tokens, moments, gain_here, table, weight)

    parts = lax.all_to_all(partial.reshape(bands, share, channels), "band", 0, 0, tiled=True)
    forward = [(i, i + 1) for i in range(bands - 1)]
    backward = [(target, source) for source, target in forward]
    margin = KER // 2
    low = lax.ppermute(normed[rows - margin :], "band", forward)
    high = lax.ppermute(normed[:margin], "band", backward)
    piece = jnp.sum(parts.astype(F32), axis=0).astype(BF)
    blocks = from_everyone(piece, ("band", "head")).reshape(bands, groups, share, channels)

    size = width // HEADS
    scale = 1.4426950408889634 / size**0.5
    query = query_of(place.reshape(1), [own_row, *arrived], gain, early, columns, scale)
    base = convolve(low, normed, high, tokens, conv_kernel)
    key, value = keys_and_values(blocks, early, late)
    chunks = 2
    count = columns // chunks
    returned = []
    for chunk in range(chunks):
        projected = attend_and_project(query, key, value, late, chunk * count, count)
        returned.append(lax.all_to_all(projected, "head", 0, 0, tiled=True))
    projected = jnp.concatenate(returned, axis=1)
    return (base + projected.astype(F32)).astype(BF)


def solution(mesh):
    return jax.shard_map(
        body,
        mesh=mesh,
        in_specs=(
            P(("dp", "band"), None, "head"),
            P("dp"),
            P("dp"),
            P(None, "dp"),
            P(None, "head"),
            P(None, "head"),
            P(None, "head"),
            P("head", None),
            P(None, "head"),
            P(),
        ),
        out_specs=P(("dp", "band"), None, "head"),
        check_vma=False,
    )
```

time: 255 us -> 130 us (0.51)
  waiting for transfers between devices: 87.5 us -> 15.8 us
  matrix products: 60.5 us -> 0 us
  Pallas kernels: 0 us -> 53.6 us
  blocking collectives: 22.4 us -> 0 us
  starting transfers between devices: 19.9 us -> 39.8 us
  local copies, waits for them, and re-layouts: 25.4 us -> 8.57 us
  between operations: 13.7 us -> 0.29 us
  other arithmetic: 24.4 us -> 11.2 us
    pallas_call x0 -> x7, Pallas kernels: none -> 53.6 us  [the longest x2 27.7 us: attend_and_project(): pl.pallas_call(functools.partial(attend_kernel, HEADS // groups), grid=(c...]
    all_gather x1 -> x0, waiting for transfers between devices: 50.7 us -> none  [shards(): whole = lax.all_gather(tokens, 'head', axis=2, tiled=True)]
    dot_general x16 -> x0, matrix products: 37.1 us -> none  [the longest x8 24.8 us: one_block(): jnp.einsum('hqk,khd->qhd', probs, value_heads, preferred_element_type=jnp...]
    all_to_all x2 -> x4, waiting for transfers between devices: 26.5 us -> 2.05 us  [the longest x1 2.04 us: body(): lax.all_to_all(partial.reshape(bands, share, channels), 'band', 0, 0, til...]
    sub x8 -> x0, matrix products: 23.4 us -> none  [one_block(): expo = jnp.exp(scores - top)]
    all_gather x1 -> x0, blocking collectives: 22.4 us -> none  [sent_together(): lax.all_gather(both, axis, axis=dim, tiled=True)]
    convert_element_type x5 -> x2, other arithmetic: 16.3 us -> 2.82 us  [the longest x1 2.77 us: body(): return (base + projected.astype(F32)).astype(BF)]
    all_to_all x2 -> x4, starting transfers between devices: 11.8 us -> 20.7 us  [the longest x2 8.22 us: body(): returned.append(lax.all_to_all(projected, 'head', 0, 0, tiled=True))]
  transfers between devices with their start and end apart: 6 -> 13, of which waited for: 6 -> 4; matrix products, arithmetic and copies ran while one was open for 6% -> 11% of each run, Pallas kernels for 0% -> 25%
where the time goes in v1:
time: 130 us; the launch traced here: 129 us
  Pallas kernels  53.6 us (41%)
  starting transfers between devices  39.8 us (31%)
  waiting for transfers between devices  15.8 us (12%)
  other arithmetic  11.2 us (9%)
  local copies, waits for them, and re-layouts  8.57 us (7%)
    pallas_call x2, Pallas kernels, attend_and_project(): pl.pallas_call(functools.partial(attend_kernel, HEADS // groups), grid=(c...  27.7 us
    pallas_call x1, Pallas kernels, convolve(): pl.pallas_call(convolve_kernel, out_shape=jax.ShapeDtypeStruct(normed.sha...  8.73 us
    all_to_all x2, starting transfers between devices, body(): returned.append(lax.all_to_all(projected, 'head', 0, 0, tiled=True))  8.22 us
    all_to_all x1, waiting for transfers between devices, from_everyone(): return lax.all_to_all(copies, axis, split_axis=0, concat_axis=0, tiled=True)  8.18 us
    all_to_all x1, starting transfers between devices, body(): lax.all_to_all(partial.reshape(bands, share, channels), 'band', 0, 0, til...  7.87 us
    all_to_all x1, starting transfers between devices, from_everyone(): return lax.all_to_all(copies, axis, split_axis=0, concat_axis=0, tiled=True)  7.04 us
    ppermute x3, waiting for transfers between devices, body(): arrived.append((distance, lax.ppermute(bulk[distance - 1], 'head', ring)))  5.37 us
    ppermute x3, starting transfers between devices, body(): arrived.append((distance, lax.ppermute(bulk[distance - 1], 'head', ring)))  5.02 us
  transfers between devices with their start and end apart: 13, of which 4 were waited for; matrix products, arithmetic and copies ran while one was open for 11% of the time, Pallas kernels for 25%

profile of v1, /device:TPU:0, one launch (start us, length us, event | category | flops | bytes accessed | tf_op | source)
XLA Modules:
  0.0 129.2 jit_solution(4416948215869651287)
XLA Ops:
  0.0 3.5 %moments.1 = f32[4,2,4096]{2,1,0:T(2,128)} custom-call(bf16[4,1024,128]{2,1,0:T(8,128)(2,1)} %tokens_ref.5), custom_call_target="tpu_custom_call" | custom-call | flops 1000000000 | bytes 1048576 | tf_op jit(solution)/shard_map/moments/pallas_call | solution.py:57
  3.5 4.6 %all-to-all-start = ((f32[4,2,4096]{2,1,0:T(2,128)}), f32[4,2,4096]{2,1,0:T(2,128)S(1)}, u32[]{:S(2)}, u32[]{:S(2)}) async-start(f32[4,2,4096]{2,1,0:T(2,128)} %moments.1), calls=%async_computation | async-start | bytes 262144 | tf_op jit(solution)/shard_map/all_to_all | solution.py:325
  8.1 0.0 copy-done.6
  8.1 0.0 copy-done.7
  8.1 0.0 copy-done.8
  8.2 0.0 copy-done.9
  8.3 0.0 copy-done
  8.3 0.0 copy-start.12
  8.3 0.0 copy-start.11
  8.3 0.0 copy-start.13
  8.3 0.8 dynamic-slice_bitcast_fusion
  9.1 0.1 pad_maximum_fusion.2
  9.2 3.3 %collective-permute-start.4 = (bf16[2048,128]{1,0:T(8,128)(2,1)S(1)}, bf16[2048,128]{1,0:T(8,128)(2,1)S(1)}, u32[]{:S(2)}, u32[]{:S(2)}) collective-permute-start(bf16[2048,128]{1,0:T(8,128)(2,1)S(1)} %get-tuple-element.29), channel_id=1, source_target_pairs={{0,6},{2,0},{4,2},{6,4},{1,7},{3,1},{5,3},{7,5},{8,14},{10,8},{12,... | collective-permute-start | bytes 1572872 | tf_op jit(solution)/shard_map/ppermute | solution.py:345
  12.5 0.9 collective-permute-start.3
  13.4 0.9 collective-permute-start.2
  14.2 0.0 copy-done.12
  14.2 0.0 copy-done.11
  14.3 0.0 copy-done.13
  14.3 0.1 convert_reduce_fusion.1
  14.3 2.2 %fusion.2.table_ref = bf16[1024,1024]{1,0:T(8,128)(2,1)} fusion(s32[1024]{0:T(1024)S(1)} %broadcast_add_fusion.1, s32[1024]{0:T(1024)S(1)} %copy-done.11, bf16[1024]{0:T(1024)(128)(2,1)S(1)} %get-tuple-element.14, bf16[1024]{0:T(1024)(128)(2,1)S(1)} %get-tuple-element.16), kind=kLoop, calls=%fused_computation.4 | loop fusion | flops 8388608 | bytes 2109440 | tf_op jit(solution)/shard_map/add | solution.py:301
  16.5 1.7 %fusion.3.weight_ref = bf16[1024,512]{1,0:T(8,128)(2,1)} fusion(s32[512]{0:T(512)S(1)} %fusion.4, s32[1024]{0:T(1024)S(1)} %broadcast_add_fusion, s32[1024]{0:T(1024)S(1)} %copy-done.12, bf16[1024]{0:T(1024)(128)(2,1)S(1)} %get-tuple-element.15, bf16[1024]{0:T(1024)(128)(2,1)S(1)} %get-tuple-element.13), kind=kLoop, calls=%fused_computation.8 | loop fusion | flops 2621440 | bytes 1062912 | tf_op jit(solution)/shard_map/add | solution.py:309
  18.2 1.2 constant_dynamic-slice_fusion.gain_ref
  19.4 0.0 all-to-all-done.moments_ref
  19.4 0.7 copy-done.10
  20.1 4.9 %normalize_sample.1 = (bf16[4,1024,128]{2,1,0:T(8,128)(2,1)}, bf16[1024,128]{1,0:T(8,128)(2,1)}) custom-call(bf16[4,1024,128]{2,1,0:T(8,128)(2,1)} %tokens_ref.5, f32[4,2,4096]{2,1,0:T(2,128)} %copy-done.10, f32[1,128]{1,0:T(1,128)} %constant_dynamic-slice_fusion.gain_ref, bf16[1024,1024]{1,0:T(8,128)(2,1)} %fusion.2.table_ref, ...), custom_call_target="tpu_custom_call" | custom-call | flops 2000000000 | bytes 6291456 | tf_op jit(solution)/shard_map/normalize_sample/pallas_call | solution.py:102
  25.0 7.9 %all-to-all-start.1 = ((bf16[16,64,128]{2,1,0:T(8,128)(2,1)}), bf16[16,64,128]{2,1,0:T(8,128)(2,1)S(1)}, u32[]{:S(2)}, u32[]{:S(2)}) async-start(bf16[16,64,128]{2,1,0:T(8,128)(2,1)} %bitcast.29), calls=%async_computation.1 | async-start | bytes 524288 | tf_op jit(solution)/shard_map/all_to_all | solution.py:367
  32.8 5.4 %collective-permute-done.2.refs_1_ = bf16[2048,128]{1,0:T(8,128)(2,1)} collective-permute-done((bf16[2048,128]{1,0:T(8,128)(2,1)S(1)}, bf16[2048,128]{1,0:T(8,128)(2,1)}, u32[]{:S(2)}, u32[]{:S(2)}) %collective-permute-start.2) | collective-permute-done | bytes 524320 | tf_op jit(solution)/shard_map/ppermute | solution.py:345
  38.2 1.0 slice.52
  39.2 0.1 collective-permute-start.5
  39.3 2.0 %all-to-all-done.1 = bf16[16,64,128]{2,1,0:T(8,128)(2,1)S(1)} async-done(((bf16[16,64,128]{2,1,0:T(8,128)(2,1)}), bf16[16,64,128]{2,1,0:T(8,128)(2,1)S(1)}, u32[]{:S(2)}, u32[]{:S(2)}) %all-to-all-start.1) | async-done | bytes 262176 | tf_op jit(solution)/shard_map/all_to_all | solution.py:367
  41.3 1.2 broadcast_in_dim.53
  42.6 7.0 %all-to-all-start.2 = ((bf16[64,64,128]{2,1,0:T(8,128)(2,1)}), bf16[64,64,128]{2,1,0:T(8,128)(2,1)S(1)}, u32[]{:S(2)}, u32[]{:S(2)}) async-start(bf16[64,64,128]{2,1,0:T(8,128)(2,1)} %broadcast_in_dim.53), calls=%async_computation.2 | async-start | bytes 2097152 | tf_op jit(solution)/shard_map/all_to_all | solution.py:22
  49.6 0.0 collective-permute-done.4.refs_3_
  49.6 0.0 copy-start.5
  49.7 0.3 collective-permute-start.7
  49.9 0.0 collective-permute-done.3.refs_2_
  50.0 1.0 slice.53
  50.9 0.6 collective-permute-start.6
  51.5 0.0 collective-permute-done.5
  51.5 1.1 broadcast_select_fusion.2
  52.6 0.0 collective-permute-done.7
  52.6 0.1 collective-permute-done.6
  52.7 1.0 broadcast_select_fusion
  53.8 1.1 pad_maximum_fusion.1.value_weight_ref.weight_ref
  54.9 1.1 pad_maximum_fusion.refs_5_.key_weight_ref
  56.0 4.7 %query.1.query_ref = bf16[4,1024,128]{2,1,0:T(8,128)(2,1)} custom-call(s32[1]{0:T(128)} %bitcast.1.place_ref, bf16[1024,128]{1,0:T(8,128)(2,1)} %get-tuple-element.19.refs_0_, bf16[2048,128]{1,0:T(8,128)(2,1)} %collective-permute-done.2.refs_1_, bf16[2048,128]{1,0:T(8,128)(2,1)} %collective-permute-done.3.refs_2_, bf16[2048,128]{1,0:T(8,128)(2,1)} %copy-done.5, ...), custom_call_target="tpu_custom_call" | custom-call | flops 2000000000 | bytes 3145728 | tf_op jit(solution)/shard_map/query/pallas_call | solution.py:142
  60.6 8.2 %all-to-all-done.2 = bf16[64,64,128]{2,1,0:T(8,128)(2,1)S(1)} async-done(((bf16[64,64,128]{2,1,0:T(8,128)(2,1)}), bf16[64,64,128]{2,1,0:T(8,128)(2,1)S(1)}, u32[]{:S(2)}, u32[]{:S(2)}) %all-to-all-start.2) | async-done | bytes 1048608 | tf_op jit(solution)/shard_map/all_to_all | solution.py:22
  68.8 1.0 copy-done.2
  69.8 4.2 %key_value.1 = (bf16[4,1024,128]{2,1,0:T(8,128)(2,1)}, bf16[4,1024,128]{2,1,0:T(8,128)(2,1)}) custom-call(bf16[16,4,64,128]{3,2,1,0:T(8,128)(2,1)} %bitcast.22, bf16[4,2,512,128]{3,2,1,0:T(8,128)(2,1)} %pad_maximum_fusion.refs_5_.key_weight_ref, bf16[4,2,512,128]{3,2,1,0:T(8,128)(2,1)} %pad_maximum_fusion.1.value_weight_ref.weight_ref), custom_call_target="tpu_custom_call" | custom-call | flops 2000000000 | bytes 4194304 | tf_op jit(solution)/shard_map/key_value/pallas_call | solution.py:177
  74.0 13.9 %attend.2 = bf16[4,512,128]{2,1,0:T(8,128)(2,1)} custom-call(bf16[4,1024,128]{2,1,0:T(8,128)(2,1)} %query.1.query_ref, bf16[4,1024,128]{2,1,0:T(8,128)(2,1)} %get-tuple-element.11.key_ref, bf16[4,1024,128]{2,1,0:T(8,128)(2,1)} %get-tuple-element.12.value_ref, bf16[4,2,512,128]{3,2,1,0:T(8,128)(2,1)} %pad_maximum_fusion.1.value_weight_ref.weight_ref), custom_call_target="tpu_custom_call" | custom-call | flops 1073741824 | bytes 4194304 | tf_op jit(solution)/shard_map/attend/pallas_call | solution.py:234
  87.9 3.5 %all-to-all-start.3 = ((bf16[4,512,128]{2,1,0:T(8,128)(2,1)}), bf16[4,512,128]{2,1,0:T(8,128)(2,1)S(1)}, u32[]{:S(2)}, u32[]{:S(2)}) async-start(bf16[4,512,128]{2,1,0:T(8,128)(2,1)} %attend.2), calls=%async_computation.3 | async-start | bytes 1048576 | tf_op jit(solution)/shard_map/all_to_all | solution.py:386
  91.4 0.1 fusion.8
  91.4 1.3 %collective-permute-start.1 = (bf16[2,1024,128]{2,1,0:T(8,128)(2,1)S(1)}, bf16[2,1024,128]{2,1,0:T(8,128)(2,1)S(1)}, u32[]{:S(2)}, u32[]{:S(2)}) collective-permute-start(bf16[2,1024,128]{2,1,0:T(8,128)(2,1)S(1)} %get-tuple-element.21), channel_id=1, source_target_pairs={{8,0},{16,8},{24,16},{32,24},{40,32},{48,40},{56,48},{64,56},{72,6... | collective-permute-start | bytes 1572872 | tf_op jit(solution)/shard_map/ppermute | solution.py:372
  92.7 4.8 %collective-permute-start = (bf16[2,1024,128]{2,1,0:T(8,128)(2,1)S(1)}, bf16[2,1024,128]{2,1,0:T(8,128)(2,1)S(1)}, u32[]{:S(2)}, u32[]{:S(2)}) collective-permute-start(bf16[2,1024,128]{2,1,0:T(8,128)(2,1)S(1)} %get-tuple-element.22), channel_id=1, source_target_pairs={{0,8},{8,16},{16,24},{24,32},{32,40},{40,48},{48,56},{56,64},{64,7... | collective-permute-start | bytes 1572872 | tf_op jit(solution)/shard_map/ppermute | solution.py:371
  97.5 13.8 %attend.3 = bf16[4,512,128]{2,1,0:T(8,128)(2,1)} custom-call(bf16[4,1024,128]{2,1,0:T(8,128)(2,1)} %query.1.query_ref, bf16[4,1024,128]{2,1,0:T(8,128)(2,1)} %get-tuple-element.11.key_ref, bf16[4,1024,128]{2,1,0:T(8,128)(2,1)} %get-tuple-element.12.value_ref, bf16[4,2,512,128]{3,2,1,0:T(8,128)(2,1)} %pad_maximum_fusion.1.value_weight_ref.weight_ref), custom_call_target="tpu_custom_call" | custom-call | flops 1073741824 | bytes 4194304 | tf_op jit(solution)/shard_map/attend/pallas_call | solution.py:234
  111.4 0.0 all-to-all-done.3
  111.4 4.7 %all-to-all-start.4 = ((bf16[4,512,128]{2,1,0:T(8,128)(2,1)}), bf16[4,512,128]{2,1,0:T(8,128)(2,1)S(1)}, u32[]{:S(2)}, u32[]{:S(2)}) async-start(bf16[4,512,128]{2,1,0:T(8,128)(2,1)} %attend.3), calls=%async_computation.4 | async-start | bytes 1048576 | tf_op jit(solution)/shard_map/all_to_all | solution.py:386
  116.1 0.0 collective-permute-done.1.high_ref
  116.1 0.0 collective-permute-done.low_ref
  116.1 0.8 copy-done.3
  116.9 0.8 copy-done.4
  117.7 8.7 %convolve.1 = f32[4,1024,128]{2,1,0:T(8,128)} custom-call(bf16[2,1024,128]{2,1,0:T(8,128)(2,1)} %copy-done.4, bf16[4,1024,128]{2,1,0:T(8,128)(2,1)} %get-tuple-element.9.normed_ref, bf16[2,1024,128]{2,1,0:T(8,128)(2,1)} %copy-done.3, bf16[4,1024,128]{2,1,0:T(8,128)(2,1)} %tokens_ref.5, f32[25,128]{1,0:T(8,128)} %taps_ref.1), custom_call_target="tpu_custom_call" | custom-call | flops 1000000000 | bytes 6291456 | tf_op jit(solution)/shard_map/convolve/pallas_call | solution.py:285
  126.4 0.0 all-to-all-done.4
  126.4 2.8 %add_convert_fusion = bf16[4,1024,128]{2,1,0:T(8,128)(2,1)} fusion(f32[4,1024,128]{2,1,0:T(8,128)} %convolve.1, bf16[4,512,128]{2,1,0:T(8,128)(2,1)S(1)} %all-to-all-done.4, bf16[4,512,128]{2,1,0:T(8,128)(2,1)S(1)} %all-to-all-done.3), kind=kLoop, calls=%fused_computation.5 | loop fusion | flops 3145728 | bytes 4194304 | tf_op jit(solution)/shard_map/convert_element_type | solution.py:388
  (25 shorter events, 0.2 us)
Async XLA Ops:
  0.0 8.3 %copy-start = (bf16[4,1024,128]{2,1,0:T(8,128)(2,1)S(1)}, bf16[4,1024,128]{2,1,0:T(8,128)(2,1)}, u32[]{:S(2)}) copy-start(bf16[4,1024,128]{2,1,0:T(8,128)(2,1)} %tokens_ref.5) | copy-start | bytes 3145732
  0.0 8.1 %copy-start.6 = (bf16[512,128]{1,0:T(8,128)(2,1)S(1)}, bf16[512,128]{1,0:T(8,128)(2,1)}, u32[]{:S(2)}) copy-start(bf16[512,128]{1,0:T(8,128)(2,1)} %param.14) | copy-start | bytes 393220
  0.0 8.1 %copy-start.7 = (bf16[512,128]{1,0:T(8,128)(2,1)S(1)}, bf16[512,128]{1,0:T(8,128)(2,1)}, u32[]{:S(2)}) copy-start(bf16[512,128]{1,0:T(8,128)(2,1)} %param.16) | copy-start | bytes 393220
  0.0 8.1 %copy-start.8 = (bf16[128,512]{1,0:T(8,128)(2,1)S(1)}, bf16[128,512]{1,0:T(8,128)(2,1)}, u32[]{:S(2)}) copy-start(bf16[128,512]{1,0:T(8,128)(2,1)} %param.17) | copy-start | bytes 393220
  0.0 8.2 %copy-start.9 = (bf16[512,128]{1,0:T(8,128)(2,1)S(1)}, bf16[512,128]{1,0:T(8,128)(2,1)}, u32[]{:S(2)}) copy-start(bf16[512,128]{1,0:T(8,128)(2,1)} %param.15) | copy-start | bytes 393220
  3.5 15.9 %all-to-all-start = ((f32[4,2,4096]{2,1,0:T(2,128)}), f32[4,2,4096]{2,1,0:T(2,128)S(1)}, u32[]{:S(2)}, u32[]{:S(2)}) async-start(f32[4,2,4096]{2,1,0:T(2,128)} %moments.1), calls=%async_computation | async-start | bytes 262144 | tf_op jit(solution)/shard_map/all_to_all | solution.py:325
  8.3 5.9 %copy-start.12 = (s32[1024]{0:T(1024)S(1)}, s32[1024]{0:T(1024)}, u32[]{:S(2)}) copy-start(s32[1024]{0:T(1024)} %param.11) | copy-start | bytes 12292
  8.3 5.9 %copy-start.11 = (s32[1024]{0:T(1024)S(1)}, s32[1024]{0:T(1024)}, u32[]{:S(2)}) copy-start(s32[1024]{0:T(1024)} %param.12) | copy-start | bytes 12292
  8.3 6.0 %copy-start.13 = (f32[2,1024]{1,0:T(2,128)S(1)}, f32[2,1024]{1,0:T(2,128)}, u32[]{:S(2)}) copy-start(f32[2,1024]{1,0:T(2,128)} %param.13) | copy-start | bytes 24580
  9.2 40.4 %collective-permute-start.4 = (bf16[2048,128]{1,0:T(8,128)(2,1)S(1)}, bf16[2048,128]{1,0:T(8,128)(2,1)S(1)}, u32[]{:S(2)}, u32[]{:S(2)}) collective-permute-start(bf16[2048,128]{1,0:T(8,128)(2,1)S(1)} %get-tuple-element.29), channel_id=1, source_target_pairs={{0,6},{2,0},{4,2},{6,4},{1,7},{3,1},{5,3},{7,5},{8,14},{10,8},{12,... | collective-permute-start | bytes 1572872 | tf_op jit(solution)/shard_map/ppermute | solution.py:345
  12.5 37.4 %collective-permute-start.3 = (bf16[2048,128]{1,0:T(8,128)(2,1)S(1)}, bf16[2048,128]{1,0:T(8,128)(2,1)}, u32[]{:S(2)}, u32[]{:S(2)}) collective-permute-start(bf16[2048,128]{1,0:T(8,128)(2,1)S(1)} %get-tuple-element.30), channel_id=1, source_target_pairs={{0,4},{2,6},{4,0},{6,2},{1,5},{3,7},{5,1},{7,3},{8,12},{10,14},{12... | collective-permute-start | bytes 1572872 | tf_op jit(solution)/shard_map/ppermute | solution.py:345
  13.4 24.8 %collective-permute-start.2 = (bf16[2048,128]{1,0:T(8,128)(2,1)S(1)}, bf16[2048,128]{1,0:T(8,128)(2,1)}, u32[]{:S(2)}, u32[]{:S(2)}) collective-permute-start(bf16[2048,128]{1,0:T(8,128)(2,1)S(1)} %get-tuple-element.31), channel_id=1, source_target_pairs={{0,2},{2,4},{4,6},{6,0},{1,3},{3,5},{5,7},{7,1},{8,10},{10,12},{12... | collective-permute-start | bytes 1572872 | tf_op jit(solution)/shard_map/ppermute | solution.py:345
  19.4 0.7 copy-start.10
  25.0 16.3 %all-to-all-start.1 = ((bf16[16,64,128]{2,1,0:T(8,128)(2,1)}), bf16[16,64,128]{2,1,0:T(8,128)(2,1)S(1)}, u32[]{:S(2)}, u32[]{:S(2)}) async-start(bf16[16,64,128]{2,1,0:T(8,128)(2,1)} %bitcast.29), calls=%async_computation.1 | async-start | bytes 524288 | tf_op jit(solution)/shard_map/all_to_all | solution.py:367
  39.2 12.3 %collective-permute-start.5 = (bf16[1024,128]{1,0:T(8,128)(2,1)S(1)}, bf16[1024,128]{1,0:T(8,128)(2,1)}, u32[]{:S(2)}, u32[]{:S(2)}) collective-permute-start(bf16[1024,128]{1,0:T(8,128)(2,1)S(1)} %slice.52), channel_id=1, source_target_pairs={{0,1},{1,0},{2,3},{3,2},{4,5},{5,4},{6,7},{7,6},{8,9},{9,8},{10,11... | collective-permute-start | bytes 786440 | tf_op jit(solution)/shard_map/ppermute | solution.py:347
  42.6 26.2 %all-to-all-start.2 = ((bf16[64,64,128]{2,1,0:T(8,128)(2,1)}), bf16[64,64,128]{2,1,0:T(8,128)(2,1)S(1)}, u32[]{:S(2)}, u32[]{:S(2)}) async-start(bf16[64,64,128]{2,1,0:T(8,128)(2,1)} %broadcast_in_dim.53), calls=%async_computation.2 | async-start | bytes 2097152 | tf_op jit(solution)/shard_map/all_to_all | solution.py:22
  49.6 4.1 %copy-start.5 = (bf16[2048,128]{1,0:T(8,128)(2,1)}, bf16[2048,128]{1,0:T(8,128)(2,1)S(1)}, u32[]{:S(2)}) copy-start(bf16[2048,128]{1,0:T(8,128)(2,1)S(1)} %collective-permute-done.4.refs_3_) | copy-start | bytes 1572868
  49.7 2.9 %collective-permute-start.7 = (bf16[1024,128]{1,0:T(8,128)(2,1)S(1)}, bf16[1024,128]{1,0:T(8,128)(2,1)S(1)}, u32[]{:S(2)}, u32[]{:S(2)}) collective-permute-start(bf16[1024,128]{1,0:T(8,128)(2,1)S(1)} %slice.54), channel_id=1, source_target_pairs={{0,1},{1,0},{2,3},{3,2},{4,5},{5,4},{6,7},{7,6},{8,9},{9,8},{10,11... | collective-permute-start | bytes 786440 | tf_op jit(solution)/shard_map/ppermute | solution.py:347
  50.9 1.8 %collective-permute-start.6 = (bf16[1024,128]{1,0:T(8,128)(2,1)S(1)}, bf16[1024,128]{1,0:T(8,128)(2,1)S(1)}, u32[]{:S(2)}, u32[]{:S(2)}) collective-permute-start(bf16[1024,128]{1,0:T(8,128)(2,1)S(1)} %slice.53), channel_id=1, source_target_pairs={{0,1},{1,0},{2,3},{3,2},{4,5},{5,4},{6,7},{7,6},{8,9},{9,8},{10,11... | collective-permute-start | bytes 786440 | tf_op jit(solution)/shard_map/ppermute | solution.py:347
  68.8 1.0 copy-start.2
  74.0 17.4 %copy-start.1 = (bf16[4,1024,128]{2,1,0:T(8,128)(2,1)S(1)}, bf16[4,1024,128]{2,1,0:T(8,128)(2,1)}, u32[]{:S(2)}) copy-start(bf16[4,1024,128]{2,1,0:T(8,128)(2,1)} %get-tuple-element.9.normed_ref) | copy-start | bytes 3145732
  87.9 23.5 %all-to-all-start.3 = ((bf16[4,512,128]{2,1,0:T(8,128)(2,1)}), bf16[4,512,128]{2,1,0:T(8,128)(2,1)S(1)}, u32[]{:S(2)}, u32[]{:S(2)}) async-start(bf16[4,512,128]{2,1,0:T(8,128)(2,1)} %attend.2), calls=%async_computation.3 | async-start | bytes 1048576 | tf_op jit(solution)/shard_map/all_to_all | solution.py:386
  91.4 24.7 %collective-permute-start.1 = (bf16[2,1024,128]{2,1,0:T(8,128)(2,1)S(1)}, bf16[2,1024,128]{2,1,0:T(8,128)(2,1)S(1)}, u32[]{:S(2)}, u32[]{:S(2)}) collective-permute-start(bf16[2,1024,128]{2,1,0:T(8,128)(2,1)S(1)} %get-tuple-element.21), channel_id=1, source_target_pairs={{8,0},{16,8},{24,16},{32,24},{40,32},{48,40},{56,48},{64,56},{72,6... | collective-permute-start | bytes 1572872 | tf_op jit(solution)/shard_map/ppermute | solution.py:372
  92.7 23.4 %collective-permute-start = (bf16[2,1024,128]{2,1,0:T(8,128)(2,1)S(1)}, bf16[2,1024,128]{2,1,0:T(8,128)(2,1)S(1)}, u32[]{:S(2)}, u32[]{:S(2)}) collective-permute-start(bf16[2,1024,128]{2,1,0:T(8,128)(2,1)S(1)} %get-tuple-element.22), channel_id=1, source_target_pairs={{0,8},{8,16},{16,24},{24,32},{32,40},{40,48},{48,56},{56,64},{64,7... | collective-permute-start | bytes 1572872 | tf_op jit(solution)/shard_map/ppermute | solution.py:371
  111.4 15.1 %all-to-all-start.4 = ((bf16[4,512,128]{2,1,0:T(8,128)(2,1)}), bf16[4,512,128]{2,1,0:T(8,128)(2,1)S(1)}, u32[]{:S(2)}, u32[]{:S(2)}) async-start(bf16[4,512,128]{2,1,0:T(8,128)(2,1)} %attend.3), calls=%async_computation.4 | async-start | bytes 1048576 | tf_op jit(solution)/shard_map/all_to_all | solution.py:386
  116.1 0.8 copy-start.3
  116.9 0.8 copy-start.4

commit v2 on v1

v2 whole, which is shorter than its diff:
```python
import functools

import jax
import jax.numpy as jnp
from jax import lax
from jax.experimental import pallas as pl
from jax.experimental.pallas import tpu as pltpu
from jax.sharding import PartitionSpec as P


HEADS = 16
KER = 5
EPS = 1e-05
F32 = jnp.float32
BF = jnp.bfloat16
ROW_BY_ROW = (((1,), (1,)), ((), ()))
COLUMN_BY_COLUMN = (((0,), (0,)), ((), ()))


def split_in_three(x):
    high = x.astype(BF)
    rest = x - high.astype(F32)
    middle = rest.astype(BF)
    return high, middle, (rest - middle.astype(F32)).astype(BF)


def moments_kernel(tokens_ref, out_ref):
    rows, columns, channels = tokens_ref.shape
    half = lax.broadcasted_iota(jnp.int32, (8, 2 * channels), 1) // channels
    pick = jnp.where(half == lax.broadcasted_iota(jnp.int32, (8, 2 * channels), 0), 1.0, 0.0)
    pick = pick.astype(BF)
    average = jnp.full((channels, channels), 1.0 / channels, BF)
    for row in range(rows):
        block = tokens_ref[row]
        center = jnp.dot(block, average, preferred_element_type=F32)
        square = jnp.square(block.astype(F32) - center).astype(BF)
        both = jnp.concatenate([block, square], axis=1)
        facts = lax.dot_general(pick, both, ROW_BY_ROW, preferred_element_type=F32)
        at = pl.ds(row * columns, columns)
        for copy in range(out_ref.shape[0]):
            out_ref[copy, :, at] = facts[0:2]


def local_moments(tokens, copies):
    rows, columns, _ = tokens.shape
    return pl.pallas_call(
        moments_kernel,
        out_shape=jax.ShapeDtypeStruct((copies, 2, rows * columns), F32),
        cost_estimate=pl.CostEstimate(flops=10**9, bytes_accessed=2**20, transcendentals=0),
        name="moments",
    )(tokens)


def tables_kernel(band_ref, row_ref, column_ref, fraction_ref, table_ref, weight_ref):
    _, columns = table_ref.shape
    rows = weight_ref.shape[1] // 128
    lines = row_ref[...]
    start = band_ref[0] * rows
    column = column_ref[...]
    vertical = fraction_ref[0:1, :]
    horizontal = fraction_ref[1:2, :]
    top = (1.0 - vertical).astype(BF).astype(F32)
    bottom = vertical.astype(BF).astype(F32)
    coarse = (column // 8) * 8
    facts = [
        coarse.astype(F32),
        (column - coarse).astype(F32),
        (1.0 - horizontal).astype(BF).astype(F32),
        horizontal.astype(BF).astype(F32),
    ]
    for r in range(rows):
        here = jnp.where(lines == start + r, top, 0.0)
        facts.append(here + jnp.where(lines + 1 == start + r, bottom, 0.0))
    facts += [jnp.zeros_like(facts[0])] * (16 - len(facts))
    facts = jnp.concatenate(facts, axis=0).astype(BF)
    kinds = 3 + rows
    fact = lax.broadcasted_iota(jnp.int32, (16, kinds * 128), 0)
    kind = lax.broadcasted_iota(jnp.int32, (16, kinds * 128), 1) // 128
    pick = (jnp.maximum(fact - 1, 0) == kind) & (fact < kinds + 1)
    spread = lax.dot_general(
        facts,
        jnp.where(pick, 1.0, 0.0).astype(BF),
        COLUMN_BY_COLUMN,
        preferred_element_type=F32,
    )
    weight_ref[...] = spread[:, 3 * 128 :].astype(BF)
    middle = spread[:, :128]
    left, right = spread[:, 128:256], spread[:, 256:384]
    lane = lax.broadcasted_iota(jnp.int32, (1, 128), 1).astype(F32)
    for block in range(columns // 128):
        offset = lane + float(block * 128) - middle
        values = jnp.where(offset == 0.0, left, jnp.where(offset == 1.0, right, 0.0))
        table_ref[:, block * 128 : (block + 1) * 128] = values.astype(BF)


def tables(band, corner_row, corner_col, fraction, columns, rows):
    points = corner_row.shape[0]
    vmem = pl.BlockSpec(memory_space=pltpu.VMEM)
    return pl.pallas_call(
        tables_kernel,
        in_specs=[pl.BlockSpec(memory_space=pltpu.SMEM), vmem, vmem, vmem],
        out_specs=(vmem, vmem),
        out_shape=(
            jax.ShapeDtypeStruct((points, columns), BF),
            jax.ShapeDtypeStruct((points, rows * 128), BF),
        ),
        cost_estimate=pl.CostEstimate(flops=10**9, bytes_accessed=3 * 2**20, transcendentals=0),
        name="tables",
    )(band, corner_row.reshape(1, points), corner_col.reshape(1, points), fraction)


def normalize_sample_kernel(
    place_ref,
    gain_ref,
    tokens_hbm,
    moments_hbm,
    table_hbm,
    weight_hbm,
    normed_hbm,
    low_hbm,
    high_hbm,
    sampled_ref,
    tokens,
    moments,
    table,
    weights,
    normed,
    planes,
    arrive,
    leave,
):
    fetches = []
    for index, (source, target) in enumerate(
        ((moments_hbm, moments), (tokens_hbm, tokens), (table_hbm, table), (weight_hbm, weights))
    ):
        fetches.append(pltpu.make_async_copy(source, target, arrive.at[index]))
        fetches[-1].start()
    rows, columns, channels = tokens.shape
    devices = moments.shape[0]
    fetches[0].wait()
    sums = [moments[d, 0:1, :] for d in range(devices)]
    width = channels * devices
    center = functools.reduce(jnp.add, sums) * (1.0 / width)
    spread = functools.reduce(jnp.add, [moments[d, 1:2, :] for d in range(devices)])
    for d in range(devices):
        spread = spread + channels * jnp.square(sums[d] * (1.0 / channels) - center)
    factor = lax.rsqrt(spread * (1.0 / width) + EPS)
    pieces = [*split_in_three(center), *split_in_three(factor)]
    pieces += [jnp.zeros_like(pieces[0])] * 10
    stacked = jnp.concatenate([p.astype(F32) for p in pieces], axis=0).astype(BF)
    piece = lax.broadcasted_iota(jnp.int32, (16, 2 * channels), 0)
    lane = lax.broadcasted_iota(jnp.int32, (16, 2 * channels), 1)
    pick = jnp.where((piece < 6) & (piece // 3 == lane // channels), 1.0, 0.0).astype(BF)
    gain = gain_ref[pl.ds(place_ref[0], 1), :]
    margin = KER // 2
    fetches[1].wait()
    stores = []

    def send(source, target):
        stores.append(pltpu.make_async_copy(source, target, leave.at[len(stores)]))
        stores[-1].start()

    for row in range(rows):
        part = stacked[:, row * columns : (row + 1) * columns]
        spreadout = lax.dot_general(part, pick, COLUMN_BY_COLUMN, preferred_element_type=F32)
        values = tokens[row].astype(F32) - spreadout[:, :channels]
        values = (values * spreadout[:, channels:] * gain).astype(BF)
        normed[row] = values
        planes[:, row * channels : (row + 1) * channels] = values
    send(normed, normed_hbm)
    send(normed.at[pl.ds(rows - margin, margin)], low_hbm)
    send(normed.at[pl.ds(0, margin)], high_hbm)
    fetches[2].wait()
    inner = jnp.dot(table[...], planes[...], preferred_element_type=F32)
    fetches[3].wait()
    total = None
    for row in range(rows):
        at = slice(row * channels, (row + 1) * channels)
        part = weights[:, at].astype(F32) * inner[:, at]
        total = part if total is None else total + part
    sampled_ref[...] = total.astype(BF)
    for store in stores:
        store.wait()


def normalize_and_sample(place, gain, tokens, moments, table, weight):
    rows, columns, channels = tokens.shape
    points = table.shape[0]
    vmem = pl.BlockSpec(memory_space=pltpu.VMEM)
    anywhere = pl.BlockSpec(memory_space=pl.ANY)
    edge = jax.ShapeDtypeStruct((KER // 2, columns, channels), BF)
    return pl.pallas_call(
        normalize_sample_kernel,
        in_specs=[pl.BlockSpec(memory_space=pltpu.SMEM), vmem] + [anywhere] * 4,
        out_specs=(anywhere, anywhere, anywhere, vmem),
        out_shape=(
            jax.ShapeDtypeStruct(tokens.shape, BF),
            edge,
            edge,
            jax.ShapeDtypeStruct((points, channels), BF),
        ),
        scratch_shapes=[
            pltpu.VMEM(tokens.shape, BF),
            pltpu.VMEM(moments.shape, F32),
            pltpu.VMEM(table.shape, BF),
            pltpu.VMEM(weight.shape, BF),
            pltpu.VMEM(tokens.shape, BF),
            pltpu.VMEM((columns, rows * channels), BF),
            pltpu.SemaphoreType.DMA((4,)),
            pltpu.SemaphoreType.DMA((3,)),
        ],
        cost_estimate=pl.CostEstimate(flops=2 * 10**9, bytes_accessed=6 * 2**20, transcendentals=0),
        name="normalize_sample",
    )(place, gain, tokens, moments, table, weight)


def query_kernel(scale, groups, place_ref, *refs):
    row_refs, refs = refs[:groups], refs[groups:]
    gain_ref, own_ref, *rest = refs
    near_refs, far_refs, (out_ref,) = rest[: groups - 1], rest[groups - 1 : -1], rest[-1:]
    channels = row_refs[0].shape[1]
    width = groups * channels
    place, core = place_ref[0], place_ref[1]
    parts = [ref[...].astype(F32) for ref in row_refs]
    center = sum(jnp.sum(p, axis=1, keepdims=True) for p in parts) * (1.0 / width)
    parts = [p - center for p in parts]
    spread = sum(jnp.sum(jnp.square(p), axis=1, keepdims=True) for p in parts) * (1.0 / width)
    factor = lax.rsqrt(spread + EPS)
    normed, lines = [], []
    for distance, part in enumerate(parts):
        source = lax.rem(place + (groups - distance), groups)
        normed.append((part * factor * gain_ref[pl.ds(source, 1), :]).astype(BF))
        half = near_refs[0].shape[0]
        at = pl.multiple_of(source * channels, channels)
        inside = pl.ds(pl.multiple_of(lax.rem(at, half), channels), channels)
        mine = at // half == core
        line = [own_ref[pl.ds(at, channels), :]]
        for near, far in zip(near_refs, far_refs):
            line.append(jnp.where(mine, near[inside, :], far[inside, :]))
        lines.append(jnp.concatenate(line, axis=1))
    query = jnp.dot(
        jnp.concatenate(normed, axis=1),
        jnp.concatenate(lines, axis=0),
        preferred_element_type=F32,
    )
    for g in range(groups):
        out_ref[g] = (query[:, g * channels : (g + 1) * channels] * scale).astype(BF)


def weight_specs(which, groups, ahead, depth, channels):
    half = depth // 2
    own = pl.BlockSpec((None, depth, channels), lambda *_: (which, 0, 0))
    near = pl.BlockSpec((half, channels), lambda *_: (ahead // half + which, 0))
    far = pl.BlockSpec((half, channels), lambda *_: (which, 0))
    return [own, *[near] * (groups - 1), *[far] * (groups - 1)]


def query_of(place, row, gain, weights, columns, scale):
    own, near, far = weights
    groups = len(row)
    channels = row[0].shape[1]
    depth = own.shape[1]
    block = 256
    return pl.pallas_call(
        functools.partial(query_kernel, scale, groups),
        grid_spec=pltpu.PrefetchScalarGridSpec(
            num_scalar_prefetch=1,
            grid=(columns // block,),
            in_specs=[pl.BlockSpec((block, channels), lambda i, place: (i, 0))] * groups
            + [pl.BlockSpec(gain.shape, lambda i, place: (0, 0))]
            + weight_specs(0, groups, columns, depth, channels),
            out_specs=pl.BlockSpec((groups, block, channels), lambda i, place: (0, i, 0)),
        ),
        out_shape=jax.ShapeDtypeStruct((groups, columns, channels), BF),
        cost_estimate=pl.CostEstimate(flops=2 * 10**9, bytes_accessed=3 * 2**20, transcendentals=0),
        name="query",
    )(place, *row, gain, own, *near, *far)


def attend_kernel(per_group, first, start, block, place_ref, query_hbm, *refs):
    if first:
        blocks_hbm, own_hbm, *refs = refs
    else:
        key_hbm, value_hbm, own_hbm, *refs = refs
    groups, _, channels = query_hbm.shape
    others = groups - 1
    near_hbm, far_hbm, refs = refs[:others], refs[others : 2 * others], refs[2 * others :]
    if first:
        out_ref, key_hbm, value_hbm, query, keys, values, joined, arrive, leave, *refs = refs
        sampled, pairs = refs
    else:
        out_ref, query, keys, values, joined, arrive = refs
    core = place_ref[1]
    width = groups * channels
    half = width // 2
    count = query.shape[1]
    fetches = []

    def fetch(source, target):
        copy = pltpu.make_async_copy(source, target, arrive.at[len(fetches)])
        copy.start()
        fetches.append(copy)
        return copy

    def wait(copies):
        for copy in copies:
            copy.wait()

    def columns_of(g):
        return pl.ds(g * channels, channels)

    if first:
        gathered = [
            fetch(blocks_hbm.at[:, g], sampled.at[:, :, columns_of(g)]) for g in range(groups)
        ]
        paired = [
            [fetch(own_hbm.at[1 + side], pairs.at[0, :, columns_of(side)]) for side in range(2)]
        ]
        for g in range(1, groups):
            paired.append([])
            for side in range(2):
                for half_hbm, at in ((near_hbm[g - 1], core), (far_hbm[g - 1], 1 - core)):
                    lines = pl.ds(pl.multiple_of(at * half, half), half)
                    ahead = half_hbm.shape[0] - 4 * half
                    source = half_hbm.at[pl.ds(ahead + (1 + side) * half, half)]
                    paired[g].append(fetch(source, pairs.at[g, lines, columns_of(side)]))
    asked = fetch(query_hbm.at[:, pl.ds(start, count)], query)
    if not first:
        made = [
            [fetch(key_hbm.at[g], keys.at[g]), fetch(value_hbm.at[g], values.at[g])]
            for g in range(groups)
        ]
    joins = []
    for j in range(groups):
        source = own_hbm.at[3, columns_of(j)]
        joins.append(fetch(source, joined.at[columns_of(0), columns_of(j)]))
    per_half = groups // 2
    for g in range(1, groups):
        for j in range(per_half):
            for half_hbm, at in ((near_hbm[g - 1], core), (far_hbm[g - 1], 1 - core)):
                lanes = pl.ds(pl.multiple_of((at * per_half + j) * channels, channels), channels)
                ahead = half_hbm.shape[0] - half
                source = half_hbm.at[pl.ds(ahead + j * channels, channels)]
                joins.append(fetch(source, joined.at[columns_of(g), lanes]))

    if first:
        stores = []
        wait(gathered)
        points = sampled[...].reshape(keys.shape[1], width)
        for g in range(groups):
            wait(paired[g])
            product = jnp.dot(points, pairs[g], preferred_element_type=F32)
            keys[g] = product[:, :channels].astype(BF)
            values[g] = product[:, channels:].astype(BF)
        for source, target in ((keys, key_hbm), (values, value_hbm)):
            stores.append(pltpu.make_async_copy(source, target, leave.at[len(stores)]))
            stores[-1].start()

    else:
        for copies in made:
            wait(copies)
    asked.wait()
    wait(joins)
    head = lax.broadcasted_iota(jnp.int32, (1, channels), 1) // (channels // per_group)
    zero = jnp.zeros((), BF)
    one = jnp.ones((), BF)

    def one_block(index, carry):
        lines = pl.ds(pl.multiple_of(index * block, block), block)
        attended = []
        for g in range(groups):
            total = jnp.zeros((block, 2 * channels), F32)
            for h in range(per_group):
                key = jnp.where(head == h, keys[g], zero)
                scores = lax.dot_general(
                    query[g, lines, :], key, ROW_BY_ROW, preferred_element_type=F32
                )
                top = jnp.max(scores, axis=-1, keepdims=True)
                probs = jnp.exp2(scores - top).astype(BF)
                value = jnp.where(head == h, values[g], zero)
                ones = jnp.broadcast_to(jnp.where(head == h, one, zero), value.shape)
                both = jnp.concatenate([value, ones], axis=1)
                total = total + jnp.dot(probs, both, preferred_element_type=F32)
            attended.append((total[:, :channels] / total[:, channels:]).astype(BF))
        whole = jnp.concatenate(attended, axis=1)
        projected = jnp.dot(whole, joined[...], preferred_element_type=F32)
        for g in range(groups):
            out_ref[g, lines, :] = projected[:, g * channels : (g + 1) * channels].astype(BF)
        return carry

    lax.fori_loop(0, count // block, one_block, 0)
    if first:
        wait(stores)


def attend_and_project(place, query, source, weights, start, count, block):
    own, near, far = weights
    groups, _, channels = query.shape
    first = len(source) == 1
    width = groups * channels
    points = source[0].size // width
    vmem = pl.BlockSpec(memory_space=pltpu.VMEM)
    anywhere = pl.BlockSpec(memory_space=pl.ANY)
    out_specs, out_shape = vmem, jax.ShapeDtypeStruct((groups, count, channels), BF)
    operands = [query, *source, own, *near, *far]
    pair = (groups, points, channels)
    scratch = [
        pltpu.VMEM((groups, count, channels), BF),
        pltpu.VMEM(pair, BF),
        pltpu.VMEM(pair, BF),
        pltpu.VMEM((width, width), BF),
        pltpu.SemaphoreType.DMA((64,)),
    ]
    if first:
        made = jax.ShapeDtypeStruct(pair, BF)
        out_specs, out_shape = (vmem, anywhere, anywhere), (out_shape, made, made)
        bands, _, share, _ = source[0].shape
        scratch += [
            pltpu.SemaphoreType.DMA((2,)),
            pltpu.VMEM((bands, share, width), BF),
            pltpu.VMEM((groups, width, 2 * channels), BF),
        ]
    return pl.pallas_call(
        functools.partial(attend_kernel, HEADS // groups, first, start, block),
        in_specs=[pl.BlockSpec(memory_space=pltpu.SMEM)] + [anywhere] * len(operands),
        out_specs=out_specs,
        out_shape=out_shape,
        scratch_shapes=scratch,
        cost_estimate=pl.CostEstimate(
            flops=4 * count * points * width, bytes_accessed=4 * 2**20, transcendentals=0
        ),
        name="attend",
    )(place, *operands)


def convolve_kernel(low_ref, normed_ref, high_ref, tokens_ref, taps_ref, out_ref, padded):
    rows, columns, channels = normed_ref.shape
    margin = KER // 2
    pad = 8

    @pl.when(pl.program_id(0) == 0)
    def _():
        padded[:, 0:pad, :] = jnp.zeros((rows + 2 * margin, pad, channels), F32)
        padded[:, pad + columns :, :] = jnp.zeros((rows + 2 * margin, pad, channels), F32)
        padded[0:margin, pad : pad + columns, :] = low_ref[...].astype(F32)
        padded[margin : margin + rows, pad : pad + columns, :] = normed_ref[...].astype(F32)
        padded[margin + rows :, pad : pad + columns, :] = high_ref[...].astype(F32)

    taps = taps_ref[...]
    strip = 16
    span = tokens_ref.shape[1]
    begin = pl.program_id(0) * span

    def one_strip(index, carry):
        inside = pl.multiple_of(index * strip, strip)
        start = pl.multiple_of(begin + inside, strip)
        totals = [tokens_ref[r, pl.ds(inside, strip), :].astype(F32) for r in range(rows)]
        for second in range(KER):
            for line in range(rows + 2 * margin):
                values = padded[line, pl.ds(start + pad - margin + second, strip), :]
                for r in range(rows):
                    first = line - r
                    if 0 <= first < KER:
                        tap = first * KER + second
                        totals[r] = totals[r] + taps[tap : tap + 1, :] * values
        for r in range(rows):
            out_ref[r, pl.ds(inside, strip), :] = totals[r]
        return carry

    lax.fori_loop(0, span // strip, one_strip, 0)


def convolve(low, normed, high, tokens, taps):
    rows, columns, channels = normed.shape
    span = columns // 4
    piece = pl.BlockSpec((rows, span, channels), lambda i: (0, i, 0))
    edge = pl.BlockSpec(low.shape, lambda i: (0, 0, 0))
    return pl.pallas_call(
        convolve_kernel,
        grid=(columns // span,),
        in_specs=[
            edge,
            pl.BlockSpec(normed.shape, lambda i: (0, 0, 0)),
            edge,
            piece,
            pl.BlockSpec(taps.shape, lambda i: (0, 0)),
        ],
        out_specs=piece,
        out_shape=jax.ShapeDtypeStruct(normed.shape, F32),
        scratch_shapes=[pltpu.VMEM((rows + 2 * (KER // 2), columns + 16, channels), F32)],
        cost_estimate=pl.CostEstimate(flops=10**9, bytes_accessed=6 * 2**20, transcendentals=0),
        name="convolve",
    )(low, normed, high, tokens, taps)


def body(
    tokens, corner_row, corner_col, fraction, w_query, w_key, w_value, w_out, conv_kernel, norm_gain
):
    rows, columns, channels = tokens.shape
    groups = lax.axis_size("head")
    bands = lax.axis_size("band")
    width = groups * channels
    points = corner_row.shape[0]
    share = points // bands

    head = lax.axis_index("head")
    core = lax.axis_index("dp")
    place = jnp.stack([head, core])
    moments = local_moments(tokens, groups)
    moments = lax.all_to_all(moments, "head", 0, 0, tiled=True)
    depth = w_query.shape[0]
    out_blocks = [w_out[:, g * channels : (g + 1) * channels] for g in range(groups)]
    own = jnp.stack([w_query, w_key, w_value, jnp.concatenate(out_blocks, axis=0)])
    half = lax.dynamic_slice_in_dim(own, core * (depth // 2), depth // 2, 1)
    half = half.reshape(2 * depth, channels)

    def to_all_heads(blocks):
        arrived = {}
        for distance in (2, 1, 3):
            ring = [(i, (i + distance) % groups) for i in range(groups)]
            arrived[distance] = lax.ppermute(blocks[distance], "head", ring)
        return [arrived[distance] for distance in range(1, groups)]

    token_rows = [
        lax.dynamic_index_in_dim(tokens, (head + distance) % groups, 0, keepdims=False)
        for distance in range(groups)
    ]
    bulk = [jnp.concatenate([rows_out, half], axis=0) for rows_out in token_rows]
    near = to_all_heads(bulk)
    token_rows = [token_rows[0], *near]
    far = [lax.ppermute(a[columns:], "dp", [(0, 1), (1, 0)]) for a in near]
    weights = (own, near, far)
    gain = norm_gain.reshape(groups, channels)

    table, weight = tables(
        lax.axis_index("band").reshape(1), corner_row, corner_col, fraction, columns, rows
    )
    normed, low, high, partial = normalize_and_sample(place, gain, tokens, moments, table, weight)

    parts = lax.all_to_all(partial.reshape(bands, share, channels), "band", 0, 0, tiled=True)
    forward = [(i, i + 1) for i in range(bands - 1)]
    backward = [(target, source) for source, target in forward]
    low = lax.ppermute(low, "band", forward)
    high = lax.ppermute(high, "band", backward)
    piece = jnp.sum(parts.astype(F32), axis=0).astype(BF)
    copies = jnp.broadcast_to(piece, (bands * groups, *piece.shape))
    blocks = lax.all_to_all(copies, ("band", "head"), 0, 0, tiled=True)
    blocks = blocks.reshape(bands, groups, share, channels)

    size = width // HEADS
    scale = 1.4426950408889634 / size**0.5
    query = query_of(place, token_rows, gain, weights, columns, scale)
    base = convolve(low, normed, high, tokens, conv_kernel)
    half_way = columns // 2
    chunks = ((0, half_way, half_way // 2), (half_way, half_way, half_way // 2))
    returned = []
    source = (blocks,)
    for chunk, (start, count, block) in enumerate(chunks):
        projected = attend_and_project(place, query, source, weights, start, count, block)
        if chunk == 0:
            projected, *source = projected
        returned.append(lax.all_to_all(projected, "head", 0, 0, tiled=True))
    projected = jnp.concatenate(returned, axis=1)
    return (base + projected.astype(F32)).astype(BF)


def solution(mesh):
    return jax.shard_map(
        body,
        mesh=mesh,
        in_specs=(
            P(("dp", "band"), None, "head"),
            P("dp"),
            P("dp"),
            P(None, "dp"),
            P(None, "head"),
            P(None, "head"),
            P(None, "head"),
            P("head", None),
            P(None, "head"),
            P(),
        ),
        out_specs=P(("dp", "band"), None, "head"),
        check_vma=False,
    )
```

time: 130 us -> 148 us (1.14)
  the two profiles are of different devices: /device:TPU:0 before, /device:TPU:4 now
where the time goes in v2:
time: 148 us
  Pallas kernels  57.2 us (39%)
  starting transfers between devices  42.1 us (28%)
  waiting for transfers between devices  38.7 us (26%)
  local copies, waits for them, and re-layouts  5.46 us (4%)
  other arithmetic  3.79 us (3%)
    pallas_call x2, Pallas kernels, attend_and_project(): pl.pallas_call(functools.partial(attend_kernel, HEADS // groups, first, s...  32.5 us
    ppermute x3, waiting for transfers between devices, to_all_heads(): arrived[distance] = lax.ppermute(blocks[distance], 'head', ring)  29.7 us
    all_to_all x1, starting transfers between devices, body(): lax.all_to_all(partial.reshape(bands, share, channels), 'band', 0, 0, til...  8.3 us
    all_to_all x2, starting transfers between devices, body(): returned.append(lax.all_to_all(projected, 'head', 0, 0, tiled=True))  8.24 us
    all_to_all x1, starting transfers between devices, body(): blocks = lax.all_to_all(copies, ('band', 'head'), 0, 0, tiled=True)  8.04 us
    pallas_call x1, Pallas kernels, convolve(): pl.pallas_call(convolve_kernel, grid=(columns // span,), in_specs=[edge,...  7.44 us
    all_to_all x1, waiting for transfers between devices, body(): lax.all_to_all(partial.reshape(bands, share, channels), 'band', 0, 0, til...  5.54 us
    pallas_call x1, Pallas kernels, query_of(): pl.pallas_call(functools.partial(query_kernel, scale, groups), grid_spec=...  5.38 us
  transfers between devices with their start and end apart: 13, of which 7 were waited for; matrix products, arithmetic and copies ran while one was open for 1% of the time, Pallas kernels for 21%

profile of v2, /device:TPU:4, one launch (start us, length us, event | category | flops | bytes accessed | tf_op | source)
XLA Modules:
  0.0 147.6 jit_solution(10113140834284482771)
XLA Ops:
  0.0 0.0 copy-start.11
  0.0 0.0 copy-start.15
  0.0 3.2 %moments.1 = f32[4,2,4096]{2,1,0:T(2,128)} custom-call(bf16[4,1024,128]{2,1,0:T(8,128)(2,1)} %tokens_ref.3), custom_call_target="tpu_custom_call" | custom-call | flops 1000000000 | bytes 1048576 | tf_op jit(solution)/shard_map/moments/pallas_call | solution.py:46
  3.2 4.5 %all-to-all-start = ((f32[4,2,4096]{2,1,0:T(2,128)}), f32[4,2,4096]{2,1,0:T(2,128)S(1)}, u32[]{:S(2)}, u32[]{:S(2)}) async-start(f32[4,2,4096]{2,1,0:T(2,128)} %moments.1), calls=%async_computation | async-start | bytes 262144 | tf_op jit(solution)/shard_map/all_to_all | solution.py:510
  7.7 0.0 copy-done.11
  7.8 0.0 copy-done.13
  7.8 0.0 copy-done.14
  7.8 0.0 copy-done.15
  7.8 0.1 pad_maximum_fusion.3.refs_5_.refs_1_.refs_2_
  7.9 0.0 copy-start
  7.9 0.8 pad_add_fusion.place_ref
  8.7 3.7 %tables.1 = (bf16[1024,1024]{1,0:T(8,128)(2,1)}, bf16[1024,512]{1,0:T(8,128)(2,1)}) custom-call(s32[1]{0:T(128)} %bitcast.3.band_ref, s32[1,1024]{1,0:T(1,128)} %bitcast.28, s32[1,1024]{1,0:T(1,128)} %bitcast.29, f32[2,1024]{1,0:T(2,128)} %fraction_ref.1), custom_call_target="tpu_custom_call" | custom-call | flops 1000000000 | bytes 3145728 | tf_op jit(solution)/shard_map/tables/pallas_call | solution.py:99
  12.3 1.4 all-to-all-done.moments_hbm
  13.7 0.7 copy-done.12
  14.4 5.0 %normalize_sample.1 = (bf16[4,1024,128]{2,1,0:T(8,128)(2,1)}, bf16[2,1024,128]{2,1,0:T(8,128)(2,1)}, bf16[2,1024,128]{2,1,0:T(8,128)(2,1)}, bf16[1024,128]{1,0:T(8,128)(2,1)}) custom-call(s32[2]{0:T(128)} %pad_add_fusion.place_ref, f32[4,128]{1,0:T(4,128)} %bitcast.30, bf16[4,1024,128]{2,1,0:T(8,128)(2,1)} %tokens_ref.3, f32[4,2,4096]{2,1,0:T(2,128)} %copy-done.12, ...), custom_call_target="tpu_custom_call" | custom-call | flops 2000000000 | bytes 6291456 | tf_op jit(solution)/shard_map/normalize_sample/pallas_call | solution.py:192
  19.4 8.3 %all-to-all-start.1 = ((bf16[16,64,128]{2,1,0:T(8,128)(2,1)}), bf16[16,64,128]{2,1,0:T(8,128)(2,1)S(1)}, u32[]{:S(2)}, u32[]{:S(2)}) async-start(bf16[16,64,128]{2,1,0:T(8,128)(2,1)} %bitcast.24), calls=%async_computation.1 | async-start | bytes 524288 | tf_op jit(solution)/shard_map/all_to_all | solution.py:540
  27.7 0.0 copy-done
  27.7 0.0 copy-done.1
  27.8 0.8 dynamic-slice_bitcast_fusion
  28.5 5.5 %all-to-all-done.1 = bf16[16,64,128]{2,1,0:T(8,128)(2,1)S(1)} async-done(((bf16[16,64,128]{2,1,0:T(8,128)(2,1)}), bf16[16,64,128]{2,1,0:T(8,128)(2,1)S(1)}, u32[]{:S(2)}, u32[]{:S(2)}) %all-to-all-start.1) | async-done | bytes 262176 | tf_op jit(solution)/shard_map/all_to_all | solution.py:540
  34.1 1.2 broadcast_in_dim.3
  35.4 8.0 %all-to-all-start.2 = ((bf16[64,64,128]{2,1,0:T(8,128)(2,1)}), bf16[64,64,128]{2,1,0:T(8,128)(2,1)S(1)}, u32[]{:S(2)}, u32[]{:S(2)}) async-start(bf16[64,64,128]{2,1,0:T(8,128)(2,1)} %broadcast_in_dim.3), calls=%async_computation.2 | async-start | bytes 2097152 | tf_op jit(solution)/shard_map/all_to_all | solution.py:547
  43.4 0.1 pad_maximum_fusion
  43.5 2.8 %collective-permute-start.4 = (bf16[2048,128]{1,0:T(8,128)(2,1)S(1)}, bf16[2048,128]{1,0:T(8,128)(2,1)S(1)}, u32[]{:S(2)}, u32[]{:S(2)}) collective-permute-start(bf16[2048,128]{1,0:T(8,128)(2,1)S(1)} %get-tuple-element.27), channel_id=1, source_target_pairs={{0,6},{2,0},{4,2},{6,4},{1,7},{3,1},{5,3},{7,5},{8,14},{10,8},{12,... | collective-permute-start | bytes 1572872 | tf_op jit(solution)/shard_map/ppermute | solution.py:521
  46.3 0.8 collective-permute-start.3
  47.1 0.9 collective-permute-start.2
  48.0 18.4 %collective-permute-done.4.refs_3_.refs_8_.refs_4_.refs_5_ = bf16[2048,128]{1,0:T(8,128)(2,1)S(1)} collective-permute-done((bf16[2048,128]{1,0:T(8,128)(2,1)S(1)}, bf16[2048,128]{1,0:T(8,128)(2,1)S(1)}, u32[]{:S(2)}, u32[]{:S(2)}) %collective-permute-start.4) | collective-permute-done | bytes 524320 | tf_op jit(solution)/shard_map/ppermute | solution.py:521
  66.4 0.1 collective-permute-start.7
  66.5 1.2 collective-permute-done.3.refs_2_.refs_7_.refs_3_.refs_4_
  67.7 0.1 collective-permute-start.6
  67.8 10.2 %collective-permute-done.2.refs_1_.refs_6_.refs_2_.refs_3_ = bf16[2048,128]{1,0:T(8,128)(2,1)S(1)} collective-permute-done((bf16[2048,128]{1,0:T(8,128)(2,1)S(1)}, bf16[2048,128]{1,0:T(8,128)(2,1)S(1)}, u32[]{:S(2)}, u32[]{:S(2)}) %collective-permute-start.2) | collective-permute-done | bytes 524320 | tf_op jit(solution)/shard_map/ppermute | solution.py:521
  78.0 0.3 collective-permute-start.5
  78.3 0.0 collective-permute-done.7.refs_11_.refs_7_.refs_8_
  78.3 0.0 copy-start.6
  78.3 0.0 collective-permute-done.6.refs_10_.refs_6_.refs_7_
  78.3 0.0 copy-start.7
  78.3 1.5 %collective-permute-done.5.refs_9_.refs_5_.refs_6_ = bf16[1024,128]{1,0:T(8,128)(2,1)S(1)} collective-permute-done((bf16[1024,128]{1,0:T(8,128)(2,1)S(1)}, bf16[1024,128]{1,0:T(8,128)(2,1)S(1)}, u32[]{:S(2)}, u32[]{:S(2)}) %collective-permute-start.5) | collective-permute-done | bytes 262176 | tf_op jit(solution)/shard_map/ppermute | solution.py:531
  79.8 0.0 copy-done.3
  79.8 0.0 copy-done.4
  79.8 0.0 copy-done.5
  79.8 0.0 copy-done.6
  79.8 0.0 copy-done.7
  79.8 0.7 copy-done.8
  80.5 5.4 %query.1.query_hbm = bf16[4,1024,128]{2,1,0:T(8,128)(2,1)} custom-call(s32[2]{0:T(128)} %pad_add_fusion.place_ref, bf16[1024,128]{1,0:T(8,128)(2,1)} %get-tuple-element.25.refs_0_, bf16[2048,128]{1,0:T(8,128)(2,1)} %copy-done.5, bf16[2048,128]{1,0:T(8,128)(2,1)} %copy-done.4, bf16[2048,128]{1,0:T(8,128)(2,1)} %copy-done.3, f32[4,128]{1,0:T(4,128)} %bitcast.31, ...), custom_call_target="tpu_custom_call" | custom-call | flops 2000000000 | bytes 3145728 | tf_op jit(solution)/shard_map/query/pallas_call | solution.py:264
  85.9 0.0 all-to-all-done.2
  85.9 0.0 copy-start.2
  85.9 1.0 copy-done.2
  86.9 17.5 %attend.2 = (bf16[4,512,128]{2,1,0:T(8,128)(2,1)}, bf16[4,1024,128]{2,1,0:T(8,128)(2,1)}, bf16[4,1024,128]{2,1,0:T(8,128)(2,1)}) custom-call(s32[2]{0:T(128)} %pad_add_fusion.place_ref, bf16[4,1024,128]{2,1,0:T(8,128)(2,1)} %query.1.query_hbm, bf16[16,4,64,128]{3,2,1,0:T(8,128)(2,1)} %bitcast.22, bf16[4,512,128]{2,1,0:T(8,128)(2,1)} %copy-done, ...), custom_call_target="tpu_custom_call" | custom-call | flops 1073741824 | bytes 4194304 | tf_op jit(solution)/shard_map/attend/pallas_call | solution.py:423
  104.4 3.5 %all-to-all-start.3 = ((bf16[4,512,128]{2,1,0:T(8,128)(2,1)}), bf16[4,512,128]{2,1,0:T(8,128)(2,1)S(1)}, u32[]{:S(2)}, u32[]{:S(2)}) async-start(bf16[4,512,128]{2,1,0:T(8,128)(2,1)} %get-tuple-element.20), calls=%async_computation.3 | async-start | bytes 1048576 | tf_op jit(solution)/shard_map/all_to_all | solution.py:562
  107.9 0.0 copy-done.17
  107.9 3.4 %collective-permute-start = (bf16[2,1024,128]{2,1,0:T(8,128)(2,1)S(1)}, bf16[2,1024,128]{2,1,0:T(8,128)(2,1)S(1)}, u32[]{:S(2)}, u32[]{:S(2)}) collective-permute-start(bf16[2,1024,128]{2,1,0:T(8,128)(2,1)S(1)} %copy-done.17), channel_id=1, source_target_pairs={{0,8},{8,16},{16,24},{24,32},{32,40},{40,48},{48,56},{56,64},{64,7... | collective-permute-start | bytes 1572872 | tf_op jit(solution)/shard_map/ppermute | solution.py:543
  111.3 0.0 copy-done.16
  111.3 4.8 %collective-permute-start.1 = (bf16[2,1024,128]{2,1,0:T(8,128)(2,1)S(1)}, bf16[2,1024,128]{2,1,0:T(8,128)(2,1)S(1)}, u32[]{:S(2)}, u32[]{:S(2)}) collective-permute-start(bf16[2,1024,128]{2,1,0:T(8,128)(2,1)S(1)} %copy-done.16), channel_id=1, source_target_pairs={{8,0},{16,8},{24,16},{32,24},{40,32},{48,40},{56,48},{64,56},{72,6... | collective-permute-start | bytes 1572872 | tf_op jit(solution)/shard_map/ppermute | solution.py:544
  116.1 15.0 %attend.3 = bf16[4,512,128]{2,1,0:T(8,128)(2,1)} custom-call(s32[2]{0:T(128)} %pad_add_fusion.place_ref, bf16[4,1024,128]{2,1,0:T(8,128)(2,1)} %query.1.query_hbm, bf16[4,1024,128]{2,1,0:T(8,128)(2,1)} %get-tuple-element.21.refs_0_, bf16[4,1024,128]{2,1,0:T(8,128)(2,1)} %get-tuple-element.22.refs_1_, bf16[4,512,128]{2,1,0:T(8,128)(2,1)} %copy-done, ...), custom_call_target="tpu_custom_call" | custom-call | flops 1073741824 | bytes 4194304 | tf_op jit(solution)/shard_map/attend/pallas_call | solution.py:423
  131.1 0.0 all-to-all-done.3
  131.1 4.8 %all-to-all-start.4 = ((bf16[4,512,128]{2,1,0:T(8,128)(2,1)}), bf16[4,512,128]{2,1,0:T(8,128)(2,1)S(1)}, u32[]{:S(2)}, u32[]{:S(2)}) async-start(bf16[4,512,128]{2,1,0:T(8,128)(2,1)} %attend.3), calls=%async_computation.4 | async-start | bytes 1048576 | tf_op jit(solution)/shard_map/all_to_all | solution.py:562
  135.9 0.0 collective-permute-done.low_ref
  135.9 0.0 collective-permute-done.1.high_ref
  135.9 0.0 copy-start.10
  135.9 0.8 copy-done.9
  136.7 0.2 copy-done.10
  136.8 7.4 %convolve.1 = f32[4,1024,128]{2,1,0:T(8,128)} custom-call(bf16[2,1024,128]{2,1,0:T(8,128)(2,1)} %copy-done.9, bf16[4,1024,128]{2,1,0:T(8,128)(2,1)} %get-tuple-element.17.normed_ref, bf16[2,1024,128]{2,1,0:T(8,128)(2,1)} %copy-done.10, bf16[4,1024,128]{2,1,0:T(8,128)(2,1)} %tokens_ref.3, f32[25,128]{1,0:T(8,128)} %taps_ref.1), custom_call_target="tpu_custom_call" | custom-call | flops 1000000000 | bytes 6291456 | tf_op jit(solution)/shard_map/convolve/pallas_call | solution.py:478
  144.3 0.5 all-to-all-done.4
  144.8 2.8 %add_convert_fusion = bf16[4,1024,128]{2,1,0:T(8,128)(2,1)} fusion(f32[4,1024,128]{2,1,0:T(8,128)} %convolve.1, bf16[4,512,128]{2,1,0:T(8,128)(2,1)S(1)} %all-to-all-done.4, bf16[4,512,128]{2,1,0:T(8,128)(2,1)S(1)} %all-to-all-done.3), kind=kLoop, calls=%fused_computation | loop fusion | flops 3145728 | bytes 4194304 | tf_op jit(solution)/shard_map/convert_element_type | solution.py:564
  (18 shorter events, 0.2 us)
Async XLA Ops:
  0.0 7.7 %copy-start.11 = (bf16[128,512]{1,0:T(8,128)(2,1)S(1)}, bf16[128,512]{1,0:T(8,128)(2,1)}, u32[]{:S(2)}) copy-start(bf16[128,512]{1,0:T(8,128)(2,1)} %param.17) | copy-start | bytes 393220
  0.0 7.8 %copy-start.13 = (bf16[512,128]{1,0:T(8,128)(2,1)S(1)}, bf16[512,128]{1,0:T(8,128)(2,1)}, u32[]{:S(2)}) copy-start(bf16[512,128]{1,0:T(8,128)(2,1)} %param.16) | copy-start | bytes 393220
  0.0 7.8 %copy-start.14 = (bf16[512,128]{1,0:T(8,128)(2,1)S(1)}, bf16[512,128]{1,0:T(8,128)(2,1)}, u32[]{:S(2)}) copy-start(bf16[512,128]{1,0:T(8,128)(2,1)} %param.15) | copy-start | bytes 393220
  0.0 7.8 %copy-start.15 = (bf16[512,128]{1,0:T(8,128)(2,1)S(1)}, bf16[512,128]{1,0:T(8,128)(2,1)}, u32[]{:S(2)}) copy-start(bf16[512,128]{1,0:T(8,128)(2,1)} %param.14) | copy-start | bytes 393220
  3.2 10.5 %all-to-all-start = ((f32[4,2,4096]{2,1,0:T(2,128)}), f32[4,2,4096]{2,1,0:T(2,128)S(1)}, u32[]{:S(2)}, u32[]{:S(2)}) async-start(f32[4,2,4096]{2,1,0:T(2,128)} %moments.1), calls=%async_computation | async-start | bytes 262144 | tf_op jit(solution)/shard_map/all_to_all | solution.py:510
  7.9 19.8 %copy-start = (bf16[4,512,128]{2,1,0:T(8,128)(2,1)}, bf16[4,512,128]{2,1,0:T(8,128)(2,1)S(1)}, u32[]{:S(2)}) copy-start(bf16[4,512,128]{2,1,0:T(8,128)(2,1)S(1)} %pad_maximum_fusion.3.refs_5_.refs_1_.refs_2_) | copy-start | bytes 1572868
  13.7 0.7 copy-start.12
  14.3 13.4 %copy-start.1 = (bf16[4,1024,128]{2,1,0:T(8,128)(2,1)S(1)}, bf16[4,1024,128]{2,1,0:T(8,128)(2,1)}, u32[]{:S(2)}) copy-start(bf16[4,1024,128]{2,1,0:T(8,128)(2,1)} %tokens_ref.3) | copy-start | bytes 3145732
  19.4 14.7 %all-to-all-start.1 = ((bf16[16,64,128]{2,1,0:T(8,128)(2,1)}), bf16[16,64,128]{2,1,0:T(8,128)(2,1)S(1)}, u32[]{:S(2)}, u32[]{:S(2)}) async-start(bf16[16,64,128]{2,1,0:T(8,128)(2,1)} %bitcast.24), calls=%async_computation.1 | async-start | bytes 524288 | tf_op jit(solution)/shard_map/all_to_all | solution.py:540
  35.4 50.5 %all-to-all-start.2 = ((bf16[64,64,128]{2,1,0:T(8,128)(2,1)}), bf16[64,64,128]{2,1,0:T(8,128)(2,1)S(1)}, u32[]{:S(2)}, u32[]{:S(2)}) async-start(bf16[64,64,128]{2,1,0:T(8,128)(2,1)} %broadcast_in_dim.3), calls=%async_computation.2 | async-start | bytes 2097152 | tf_op jit(solution)/shard_map/all_to_all | solution.py:547
  43.5 22.9 %collective-permute-start.4 = (bf16[2048,128]{1,0:T(8,128)(2,1)S(1)}, bf16[2048,128]{1,0:T(8,128)(2,1)S(1)}, u32[]{:S(2)}, u32[]{:S(2)}) collective-permute-start(bf16[2048,128]{1,0:T(8,128)(2,1)S(1)} %get-tuple-element.27), channel_id=1, source_target_pairs={{0,6},{2,0},{4,2},{6,4},{1,7},{3,1},{5,3},{7,5},{8,14},{10,8},{12,... | collective-permute-start | bytes 1572872 | tf_op jit(solution)/shard_map/ppermute | solution.py:521
  46.3 21.4 %collective-permute-start.3 = (bf16[2048,128]{1,0:T(8,128)(2,1)S(1)}, bf16[2048,128]{1,0:T(8,128)(2,1)S(1)}, u32[]{:S(2)}, u32[]{:S(2)}) collective-permute-start(bf16[2048,128]{1,0:T(8,128)(2,1)S(1)} %get-tuple-element.28), channel_id=1, source_target_pairs={{0,4},{2,6},{4,0},{6,2},{1,5},{3,7},{5,1},{7,3},{8,12},{10,14},{12... | collective-permute-start | bytes 1572872 | tf_op jit(solution)/shard_map/ppermute | solution.py:521
  47.1 30.8 %collective-permute-start.2 = (bf16[2048,128]{1,0:T(8,128)(2,1)S(1)}, bf16[2048,128]{1,0:T(8,128)(2,1)S(1)}, u32[]{:S(2)}, u32[]{:S(2)}) collective-permute-start(bf16[2048,128]{1,0:T(8,128)(2,1)S(1)} %get-tuple-element.29), channel_id=1, source_target_pairs={{0,2},{2,4},{4,6},{6,0},{1,3},{3,5},{5,7},{7,1},{8,10},{10,12},{12... | collective-permute-start | bytes 1572872 | tf_op jit(solution)/shard_map/ppermute | solution.py:521
  66.4 13.4 %copy-start.3 = (bf16[2048,128]{1,0:T(8,128)(2,1)}, bf16[2048,128]{1,0:T(8,128)(2,1)S(1)}, u32[]{:S(2)}) copy-start(bf16[2048,128]{1,0:T(8,128)(2,1)S(1)} %collective-permute-done.4.refs_3_.refs_8_.refs_4_.refs_5_) | copy-start | bytes 1572868
  66.4 11.9 %collective-permute-start.7 = (bf16[1024,128]{1,0:T(8,128)(2,1)S(1)}, bf16[1024,128]{1,0:T(8,128)(2,1)S(1)}, u32[]{:S(2)}, u32[]{:S(2)}) collective-permute-start(bf16[1024,128]{1,0:T(8,128)(2,1)S(1)} %slice.30), channel_id=1, source_target_pairs={{0,1},{1,0},{2,3},{3,2},{4,5},{5,4},{6,7},{7,6},{8,9},{9,8},{10,11... | collective-permute-start | bytes 786440 | tf_op jit(solution)/shard_map/ppermute | solution.py:531
  67.7 12.1 %copy-start.4 = (bf16[2048,128]{1,0:T(8,128)(2,1)}, bf16[2048,128]{1,0:T(8,128)(2,1)S(1)}, u32[]{:S(2)}) copy-start(bf16[2048,128]{1,0:T(8,128)(2,1)S(1)} %collective-permute-done.3.refs_2_.refs_7_.refs_3_.refs_4_) | copy-start | bytes 1572868
  67.7 10.6 %collective-permute-start.6 = (bf16[1024,128]{1,0:T(8,128)(2,1)S(1)}, bf16[1024,128]{1,0:T(8,128)(2,1)S(1)}, u32[]{:S(2)}, u32[]{:S(2)}) collective-permute-start(bf16[1024,128]{1,0:T(8,128)(2,1)S(1)} %slice.29), channel_id=1, source_target_pairs={{0,1},{1,0},{2,3},{3,2},{4,5},{5,4},{6,7},{7,6},{8,9},{9,8},{10,11... | collective-permute-start | bytes 786440 | tf_op jit(solution)/shard_map/ppermute | solution.py:531
  78.0 1.8 %copy-start.5 = (bf16[2048,128]{1,0:T(8,128)(2,1)}, bf16[2048,128]{1,0:T(8,128)(2,1)S(1)}, u32[]{:S(2)}) copy-start(bf16[2048,128]{1,0:T(8,128)(2,1)S(1)} %collective-permute-done.2.refs_1_.refs_6_.refs_2_.refs_3_) | copy-start | bytes 1572868
  78.0 1.8 %collective-permute-start.5 = (bf16[1024,128]{1,0:T(8,128)(2,1)S(1)}, bf16[1024,128]{1,0:T(8,128)(2,1)S(1)}, u32[]{:S(2)}, u32[]{:S(2)}) collective-permute-start(bf16[1024,128]{1,0:T(8,128)(2,1)S(1)} %slice.28), channel_id=1, source_target_pairs={{0,1},{1,0},{2,3},{3,2},{4,5},{5,4},{6,7},{7,6},{8,9},{9,8},{10,11... | collective-permute-start | bytes 786440 | tf_op jit(solution)/shard_map/ppermute | solution.py:531
  78.3 1.5 %copy-start.6 = (bf16[1024,128]{1,0:T(8,128)(2,1)}, bf16[1024,128]{1,0:T(8,128)(2,1)S(1)}, u32[]{:S(2)}) copy-start(bf16[1024,128]{1,0:T(8,128)(2,1)S(1)} %collective-permute-done.7.refs_11_.refs_7_.refs_8_) | copy-start | bytes 786436
  78.3 1.5 %copy-start.7 = (bf16[1024,128]{1,0:T(8,128)(2,1)}, bf16[1024,128]{1,0:T(8,128)(2,1)S(1)}, u32[]{:S(2)}) copy-start(bf16[1024,128]{1,0:T(8,128)(2,1)S(1)} %collective-permute-done.6.refs_10_.refs_6_.refs_7_) | copy-start | bytes 786436
  79.8 0.7 copy-start.8
  85.9 1.0 copy-start.2
  86.9 21.0 %copy-start.17 = (bf16[2,1024,128]{2,1,0:T(8,128)(2,1)S(1)}, bf16[2,1024,128]{2,1,0:T(8,128)(2,1)}, u32[]{:S(2)}) copy-start(bf16[2,1024,128]{2,1,0:T(8,128)(2,1)} %get-tuple-element.16) | copy-start | bytes 1572868
  86.9 24.4 %copy-start.16 = (bf16[2,1024,128]{2,1,0:T(8,128)(2,1)S(1)}, bf16[2,1024,128]{2,1,0:T(8,128)(2,1)}, u32[]{:S(2)}) copy-start(bf16[2,1024,128]{2,1,0:T(8,128)(2,1)} %get-tuple-element.18) | copy-start | bytes 1572868
  104.4 26.7 %all-to-all-start.3 = ((bf16[4,512,128]{2,1,0:T(8,128)(2,1)}), bf16[4,512,128]{2,1,0:T(8,128)(2,1)S(1)}, u32[]{:S(2)}, u32[]{:S(2)}) async-start(bf16[4,512,128]{2,1,0:T(8,128)(2,1)} %get-tuple-element.20), calls=%async_computation.3 | async-start | bytes 1048576 | tf_op jit(solution)/shard_map/all_to_all | solution.py:562
  107.9 28.0 %collective-permute-start = (bf16[2,1024,128]{2,1,0:T(8,128)(2,1)S(1)}, bf16[2,1024,128]{2,1,0:T(8,128)(2,1)S(1)}, u32[]{:S(2)}, u32[]{:S(2)}) collective-permute-start(bf16[2,1024,128]{2,1,0:T(8,128)(2,1)S(1)} %copy-done.17), channel_id=1, source_target_pairs={{0,8},{8,16},{16,24},{24,32},{32,40},{40,48},{48,56},{56,64},{64,7... | collective-permute-start | bytes 1572872 | tf_op jit(solution)/shard_map/ppermute | solution.py:543
  111.3 24.6 %collective-permute-start.1 = (bf16[2,1024,128]{2,1,0:T(8,128)(2,1)S(1)}, bf16[2,1024,128]{2,1,0:T(8,128)(2,1)S(1)}, u32[]{:S(2)}, u32[]{:S(2)}) collective-permute-start(bf16[2,1024,128]{2,1,0:T(8,128)(2,1)S(1)} %copy-done.16), channel_id=1, source_target_pairs={{8,0},{16,8},{24,16},{32,24},{40,32},{48,40},{56,48},{64,56},{72,6... | collective-permute-start | bytes 1572872 | tf_op jit(solution)/shard_map/ppermute | solution.py:544
  131.1 13.7 %all-to-all-start.4 = ((bf16[4,512,128]{2,1,0:T(8,128)(2,1)}), bf16[4,512,128]{2,1,0:T(8,128)(2,1)S(1)}, u32[]{:S(2)}, u32[]{:S(2)}) async-start(bf16[4,512,128]{2,1,0:T(8,128)(2,1)} %attend.3), calls=%async_computation.4 | async-start | bytes 1048576 | tf_op jit(solution)/shard_map/all_to_all | solution.py:562
  135.9 0.8 copy-start.9
  135.9 1.0 copy-start.10

commit v3 on v2

--- a/solution.py
+++ b/solution.py
@@ -24,10 +24,30 @@
     return high, middle, (rest - middle.astype(F32)).astype(BF)
 
 
-def moments_kernel(tokens_ref, out_ref):
+def moments_kernel(
+    place_ref, tokens_ref, query_ref, key_ref, value_ref, out_weight_ref, moments_ref, own_ref, *refs
+):
+    *bulk_hbm, half, leave = refs
     rows, columns, channels = tokens_ref.shape
-    half = lax.broadcasted_iota(jnp.int32, (8, 2 * channels), 1) // channels
-    pick = jnp.where(half == lax.broadcasted_iota(jnp.int32, (8, 2 * channels), 0), 1.0, 0.0)
+    depth = query_ref.shape[0]
+    for index, ref in enumerate((query_ref, key_ref, value_ref)):
+        own_ref[index] = ref[...]
+    for g in range(rows):
+        at = slice(g * channels, (g + 1) * channels)
+        own_ref[3, at, :] = out_weight_ref[:, at]
+    cut = depth // 2
+    lines = pl.ds(pl.multiple_of(place_ref[1] * cut, cut), cut)
+    for index in range(4):
+        half[index * cut : (index + 1) * cut, :] = own_ref[index, lines, :]
+    stores = []
+    for distance, target in enumerate(bulk_hbm, 1):
+        row = lax.rem(place_ref[0] + distance, rows)
+        for source, start in ((tokens_ref.at[row], 0), (half, columns)):
+            place = target.at[pl.ds(start, source.shape[0])]
+            stores.append(pltpu.make_async_copy(source, place, leave.at[len(stores)]))
+            stores[-1].start()
+    side = lax.broadcasted_iota(jnp.int32, (8, 2 * channels), 1) // channels
+    pick = jnp.where(side == lax.broadcasted_iota(jnp.int32, (8, 2 * channels), 0), 1.0, 0.0)
     pick = pick.astype(BF)
     average = jnp.full((channels, channels), 1.0 / channels, BF)
     for row in range(rows):
@@ -37,25 +57,42 @@
         both = jnp.concatenate([block, square], axis=1)
         facts = lax.dot_general(pick, both, ROW_BY_ROW, preferred_element_type=F32)
         at = pl.ds(row * columns, columns)
-        for copy in range(out_ref.shape[0]):
-            out_ref[copy, :, at] = facts[0:2]
-
-
-def local_moments(tokens, copies):
-    rows, columns, _ = tokens.shape
-    return pl.pallas_call(
+        for copy in range(moments_ref.shape[0]):
+            moments_ref[copy, :, at] = facts[0:2]
+    for store in stores:
+        store.wait()
+
+
+def moments_and_bulk(place, tokens, w_query, w_key, w_value, w_out, copies):
+    rows, columns, channels = tokens.shape
+    depth = w_query.shape[0]
+    vmem = pl.BlockSpec(memory_space=pltpu.VMEM)
+    anywhere = pl.BlockSpec(memory_space=pl.ANY)
+    bulk = jax.ShapeDtypeStruct((columns + 2 * depth, channels), BF)
+    moments, own, *bulk = pl.pallas_call(
         moments_kernel,
-        out_shape=jax.ShapeDtypeStruct((copies, 2, rows * columns), F32),
+        in_specs=[pl.BlockSpec(memory_space=pltpu.SMEM)] + [vmem] * 5,
+        out_specs=(vmem, vmem, *[anywhere] * (copies - 1)),
+        out_shape=(
+            jax.ShapeDtypeStruct((copies, 2, rows * columns), F32),
+            jax.ShapeDtypeStruct((4, depth, channels), BF),
+            *[bulk] * (copies - 1),
+        ),
+        scratch_shapes=[
+            pltpu.VMEM((2 * depth, channels), BF),
+            pltpu.SemaphoreType.DMA((2 * copies,)),
+        ],
         cost_estimate=pl.CostEstimate(flops=10**9, bytes_accessed=2**20, transcendentals=0),
         name="moments",
-    )(tokens)
-
-
-def tables_kernel(band_ref, row_ref, column_ref, fraction_ref, table_ref, weight_ref):
+    )(place, tokens, w_query, w_key, w_value, w_out)
+    return moments, own, bulk
+
+
+def make_tables(band, row_ref, column_ref, fraction_ref, table_ref, weight_ref):
     _, columns = table_ref.shape
     rows = weight_ref.shape[1] // 128
     lines = row_ref[...]
-    start = band_ref[0] * rows
+    start = band * rows
     column = column_ref[...]
     vertical = fraction_ref[0:1, :]
     horizontal = fraction_ref[1:2, :]
@@ -93,29 +130,14 @@
         table_ref[:, block * 128 : (block + 1) * 128] = values.astype(BF)
 
 
-def tables(band, corner_row, corner_col, fraction, columns, rows):
-    points = corner_row.shape[0]
-    vmem = pl.BlockSpec(memory_space=pltpu.VMEM)
-    return pl.pallas_call(
-        tables_kernel,
-        in_specs=[pl.BlockSpec(memory_space=pltpu.SMEM), vmem, vmem, vmem],
-        out_specs=(vmem, vmem),
-        out_shape=(
-            jax.ShapeDtypeStruct((points, columns), BF),
-            jax.ShapeDtypeStruct((points, rows * 128), BF),
-        ),
-        cost_estimate=pl.CostEstimate(flops=10**9, bytes_accessed=3 * 2**20, transcendentals=0),
-        name="tables",
-    )(band, corner_row.reshape(1, points), corner_col.reshape(1, points), fraction)
-
-
 def normalize_sample_kernel(
     place_ref,
     gain_ref,
+    row_ref,
+    column_ref,
+    fraction_ref,
     tokens_hbm,
     moments_hbm,
-    table_hbm,
-    weight_hbm,
     normed_hbm,
     low_hbm,
     high_hbm,
@@ -131,12 +153,13 @@
 ):
     fetches = []
     for index, (source, target) in enumerate(
-        ((moments_hbm, moments), (tokens_hbm, tokens), (table_hbm, table), (weight_hbm, weights))
+        ((moments_hbm, moments), (tokens_hbm, tokens))
     ):
         fetches.append(pltpu.make_async_copy(source, target, arrive.at[index]))
         fetches[-1].start()
     rows, columns, channels = tokens.shape
     devices = moments.shape[0]
+    make_tables(place_ref[2], row_ref, column_ref, fraction_ref, table, weights)
     fetches[0].wait()
     sums = [moments[d, 0:1, :] for d in range(devices)]
     width = channels * devices
@@ -170,9 +193,7 @@
     send(normed, normed_hbm)
     send(normed.at[pl.ds(rows - margin, margin)], low_hbm)
     send(normed.at[pl.ds(0, margin)], high_hbm)
-    fetches[2].wait()
     inner = jnp.dot(table[...], planes[...], preferred_element_type=F32)
-    fetches[3].wait()
     total = None
     for row in range(rows):
         at = slice(row * channels, (row + 1) * channels)
@@ -183,15 +204,15 @@
         store.wait()
 
 
-def normalize_and_sample(place, gain, tokens, moments, table, weight):
+def normalize_and_sample(place, gain, corner_row, corner_col, fraction, tokens, moments):
     rows, columns, channels = tokens.shape
-    points = table.shape[0]
+    points = corner_row.shape[0]
     vmem = pl.BlockSpec(memory_space=pltpu.VMEM)
     anywhere = pl.BlockSpec(memory_space=pl.ANY)
     edge = jax.ShapeDtypeStruct((KER // 2, columns, channels), BF)
     return pl.pallas_call(
         normalize_sample_kernel,
-        in_specs=[pl.BlockSpec(memory_space=pltpu.SMEM), vmem] + [anywhere] * 4,
+        in_specs=[pl.BlockSpec(memory_space=pltpu.SMEM)] + [vmem] * 4 + [anywhere] * 2,
         out_specs=(anywhere, anywhere, anywhere, vmem),
         out_shape=(
             jax.ShapeDtypeStruct(tokens.shape, BF),
@@ -202,16 +223,24 @@
         scratch_shapes=[
             pltpu.VMEM(tokens.shape, BF),
             pltpu.VMEM(moments.shape, F32),
-            pltpu.VMEM(table.shape, BF),
-            pltpu.VMEM(weight.shape, BF),
+            pltpu.VMEM((points, columns), BF),
+            pltpu.VMEM((points, rows * channels), BF),
             pltpu.VMEM(tokens.shape, BF),
             pltpu.VMEM((columns, rows * channels), BF),
-            pltpu.SemaphoreType.DMA((4,)),
+            pltpu.SemaphoreType.DMA((2,)),
             pltpu.SemaphoreType.DMA((3,)),
         ],
         cost_estimate=pl.CostEstimate(flops=2 * 10**9, bytes_accessed=6 * 2**20, transcendentals=0),
         name="normalize_sample",
-    )(place, gain, tokens, moments, table, weight)
+    )(
+        place,
+        gain,
+        corner_row.reshape(1, points),
+        corner_col.reshape(1, points),
+        fraction,
+        tokens,
+        moments,
+    )
 
 
 def query_kernel(scale, groups, place_ref, *refs):
@@ -258,7 +287,7 @@
 def query_of(place, row, gain, weights, columns, scale):
     own, near, far = weights
     groups = len(row)
-    channels = row[0].shape[1]
+    channels = own.shape[2]
     depth = own.shape[1]
     block = 256
     return pl.pallas_call(
@@ -266,7 +295,8 @@
         grid_spec=pltpu.PrefetchScalarGridSpec(
             num_scalar_prefetch=1,
             grid=(columns // block,),
-            in_specs=[pl.BlockSpec((block, channels), lambda i, place: (i, 0))] * groups
+            in_specs=[pl.BlockSpec((None, block, channels), lambda i, place: (place[0], i, 0))]
+            + [pl.BlockSpec((block, channels), lambda i, place: (i, 0))] * (groups - 1)
             + [pl.BlockSpec(gain.shape, lambda i, place: (0, 0))]
             + weight_specs(0, groups, columns, depth, channels),
             out_specs=pl.BlockSpec((groups, block, channels), lambda i, place: (0, i, 0)),
@@ -433,12 +463,16 @@
     )(place, *operands)
 
 
-def convolve_kernel(low_ref, normed_ref, high_ref, tokens_ref, taps_ref, out_ref, padded):
+def convolve_kernel(
+    low_ref, normed_ref, high_ref, tokens_ref, added_ref, taps_ref, mixed_ref, base_ref, padded
+):
     rows, columns, channels = normed_ref.shape
     margin = KER // 2
     pad = 8
-
-    @pl.when(pl.program_id(0) == 0)
+    step = pl.program_id(0)
+    finished = pl.num_programs(0) // 2
+
+    @pl.when(step == 0)
     def _():
         padded[:, 0:pad, :] = jnp.zeros((rows + 2 * margin, pad, channels), F32)
         padded[:, pad + columns :, :] = jnp.zeros((rows + 2 * margin, pad, channels), F32)
@@ -449,54 +483,68 @@
     taps = taps_ref[...]
     strip = 16
     span = tokens_ref.shape[1]
-    begin = pl.program_id(0) * span
-
-    def one_strip(index, carry):
-        inside = pl.multiple_of(index * strip, strip)
-        start = pl.multiple_of(begin + inside, strip)
-        totals = [tokens_ref[r, pl.ds(inside, strip), :].astype(F32) for r in range(rows)]
-        for second in range(KER):
-            for line in range(rows + 2 * margin):
-                values = padded[line, pl.ds(start + pad - margin + second, strip), :]
-                for r in range(rows):
-                    first = line - r
-                    if 0 <= first < KER:
-                        tap = first * KER + second
-                        totals[r] = totals[r] + taps[tap : tap + 1, :] * values
-        for r in range(rows):
-            out_ref[r, pl.ds(inside, strip), :] = totals[r]
-        return carry
-
-    lax.fori_loop(0, span // strip, one_strip, 0)
-
-
-def convolve(low, normed, high, tokens, taps):
+    begin = step * span
+
+    def convolve_into(out_ref, added):
+        def one_strip(index, carry):
+            inside = pl.multiple_of(index * strip, strip)
+            at = pl.ds(inside, strip)
+            start = pl.multiple_of(begin + inside, strip)
+            totals = [tokens_ref[r, at, :].astype(F32) for r in range(rows)]
+            if added:
+                totals = [t + added_ref[r, at, :].astype(F32) for r, t in enumerate(totals)]
+            for second in range(KER):
+                for line in range(rows + 2 * margin):
+                    values = padded[line, pl.ds(start + pad - margin + second, strip), :]
+                    for r in range(rows):
+                        first = line - r
+                        if 0 <= first < KER:
+                            tap = first * KER + second
+                            totals[r] = totals[r] + taps[tap : tap + 1, :] * values
+            for r in range(rows):
+                out_ref[r, at, :] = totals[r].astype(out_ref.dtype)
+            return carry
+
+        lax.fori_loop(0, span // strip, one_strip, 0)
+
+    @pl.when(step < finished)
+    def _():
+        convolve_into(mixed_ref, True)
+
+    @pl.when(step >= finished)
+    def _():
+        convolve_into(base_ref, False)
+
+
+def convolve(low, normed, high, tokens, added, taps):
     rows, columns, channels = normed.shape
-    span = columns // 4
+    steps = 4
+    span = columns // steps
+    last = steps // 2 - 1
+    whole = pl.BlockSpec(normed.shape, lambda i: (0, 0, 0))
     piece = pl.BlockSpec((rows, span, channels), lambda i: (0, i, 0))
+    front = pl.BlockSpec((rows, span, channels), lambda i: (0, jnp.minimum(i, last), 0))
+    back = pl.BlockSpec((rows, span, channels), lambda i: (0, jnp.maximum(i - last - 1, 0), 0))
     edge = pl.BlockSpec(low.shape, lambda i: (0, 0, 0))
     return pl.pallas_call(
         convolve_kernel,
-        grid=(columns // span,),
-        in_specs=[
-            edge,
-            pl.BlockSpec(normed.shape, lambda i: (0, 0, 0)),
-            edge,
-            piece,
-            pl.BlockSpec(taps.shape, lambda i: (0, 0)),
-        ],
-        out_specs=piece,
-        out_shape=jax.ShapeDtypeStruct(normed.shape, F32),
+        grid=(steps,),
+        in_specs=[edge, whole, edge, piece, front, pl.BlockSpec(taps.shape, lambda i: (0, 0))],
+        out_specs=(front, back),
+        out_shape=(
+            jax.ShapeDtypeStruct(normed.shape, BF),
+            jax.ShapeDtypeStruct((rows, columns // 2, channels), F32),
+        ),
         scratch_shapes=[pltpu.VMEM((rows + 2 * (KER // 2), columns + 16, channels), F32)],
         cost_estimate=pl.CostEstimate(flops=10**9, bytes_accessed=6 * 2**20, transcendentals=0),
         name="convolve",
-    )(low, normed, high, tokens, taps)
+    )(low, normed, high, tokens, added, taps)
 
 
 def body(
     tokens, corner_row, corner_col, fraction, w_query, w_key, w_value, w_out, conv_kernel, norm_gain
 ):
-    rows, columns, channels = tokens.shape
+    _, columns, channels = tokens.shape
     groups = lax.axis_size("head")
     bands = lax.axis_size("band")
     width = groups * channels
@@ -505,14 +553,11 @@
 
     head = lax.axis_index("head")
     core = lax.axis_index("dp")
-    place = jnp.stack([head, core])
-    moments = local_moments(tokens, groups)
+    place = jnp.stack([head, core, lax.axis_index("band")])
+    moments, own, bulk = moments_and_bulk(
+        place, tokens, w_query, w_key, w_value, w_out, groups
+    )
     moments = lax.all_to_all(moments, "head", 0, 0, tiled=True)
-    depth = w_query.shape[0]
-    out_blocks = [w_out[:, g * channels : (g + 1) * channels] for g in range(groups)]
-    own = jnp.stack([w_query, w_key, w_value, jnp.concatenate(out_blocks, axis=0)])
-    half = lax.dynamic_slice_in_dim(own, core * (depth // 2), depth // 2, 1)
-    half = half.reshape(2 * depth, channels)
 
     def to_all_heads(blocks):
         arrived = {}
@@ -521,21 +566,15 @@
             arrived[distance] = lax.ppermute(blocks[distance], "head", ring)
         return [arrived[distance] for distance in range(1, groups)]
 
-    token_rows = [
-        lax.dynamic_index_in_dim(tokens, (head + distance) % groups, 0, keepdims=False)
-        for distance in range(groups)
-    ]
-    bulk = [jnp.concatenate([rows_out, half], axis=0) for rows_out in token_rows]
-    near = to_all_heads(bulk)
-    token_rows = [token_rows[0], *near]
+    near = to_all_heads([None, *bulk])
+    token_rows = [tokens, *near]
     far = [lax.ppermute(a[columns:], "dp", [(0, 1), (1, 0)]) for a in near]
     weights = (own, near, far)
     gain = norm_gain.reshape(groups, channels)
 
-    table, weight = tables(
-        lax.axis_index("band").reshape(1), corner_row, corner_col, fraction, columns, rows
+    normed, low, high, partial = normalize_and_sample(
+        place, gain, corner_row, corner_col, fraction, tokens, moments
     )
-    normed, low, high, partial = normalize_and_sample(place, gain, tokens, moments, table, weight)
 
     parts = lax.all_to_all(partial.reshape(bands, share, channels), "band", 0, 0, tiled=True)
     forward = [(i, i + 1) for i in range(bands - 1)]
@@ -550,7 +589,6 @@
     size = width // HEADS
     scale = 1.4426950408889634 / size**0.5
     query = query_of(place, token_rows, gain, weights, columns, scale)
-    base = convolve(low, normed, high, tokens, conv_kernel)
     half_way = columns // 2
     chunks = ((0, half_way, half_way // 2), (half_way, half_way, half_way // 2))
     returned = []
@@ -560,8 +598,9 @@
         if chunk == 0:
             projected, *source = projected
         returned.append(lax.all_to_all(projected, "head", 0, 0, tiled=True))
-    projected = jnp.concatenate(returned, axis=1)
-    return (base + projected.astype(F32)).astype(BF)
+    mixed, base = convolve(low, normed, high, tokens, returned[0], conv_kernel)
+    rest = (base + returned[1].astype(F32)).astype(BF)
+    return lax.dynamic_update_slice_in_dim(mixed, rest, half_way, 1)
 
 
 def solution(mesh):

time: 148 us -> 150 us (1.014)
  the two profiles are of different devices: /device:TPU:4 before, /device:TPU:10 now
where the time goes in v3:
time: 150 us; the launch traced here: 149 us
  Pallas kernels  55.3 us (37%)
  starting transfers between devices  31.4 us (21%)
  waiting for transfers between devices  29.5 us (20%)
  blocking collectives  24.7 us (16%)
  local copies, waits for them, and re-layouts  4.74 us (3%)
  other arithmetic  2.77 us (2%)
    pallas_call x2, Pallas kernels, attend_and_project(): pl.pallas_call(functools.partial(attend_kernel, HEADS // groups, first, s...  32.3 us
    ppermute x3, waiting for transfers between devices, to_all_heads(): arrived[distance] = lax.ppermute(blocks[distance], 'head', ring)  28 us
    all_to_all x1, blocking collectives, body(): lax.all_to_all(partial.reshape(bands, share, channels), 'band', 0, 0, til...  15.1 us
    all_to_all x2, starting transfers between devices, body(): returned.append(lax.all_to_all(projected, 'head', 0, 0, tiled=True))  10.5 us
    all_to_all x1, blocking collectives, body(): moments = lax.all_to_all(moments, 'head', 0, 0, tiled=True)  9.55 us
    pallas_call x1, Pallas kernels, convolve(): pl.pallas_call(convolve_kernel, grid=(steps,), in_specs=[edge, whole, edg...  7.79 us
    all_to_all x1, starting transfers between devices, body(): blocks = lax.all_to_all(copies, ('band', 'head'), 0, 0, tiled=True)  7.53 us
    pallas_call x1, Pallas kernels, query_of(): pl.pallas_call(functools.partial(query_kernel, scale, groups), grid_spec=...  5.4 us
  transfers between devices with their start and end apart: 11, of which 4 were waited for; matrix products, arithmetic and copies ran while one was open for 0% of the time, Pallas kernels for 19%

profile of v3, /device:TPU:10, one launch (start us, length us, event | category | flops | bytes accessed | tf_op | source)
XLA Modules:
  0.0 148.7 jit_solution(11929660905438396950)
XLA Ops:
  0.0 0.6 pad_add_fusion.place_ref
  0.6 4.6 %moments.1 = (f32[4,2,4096]{2,1,0:T(2,128)}, bf16[4,512,128]{2,1,0:T(8,128)(2,1)}, bf16[2048,128]{1,0:T(8,128)(2,1)}, bf16[2048,128]{1,0:T(8,128)(2,1)}, bf16[2048,128]{1,0:T(8,128)(2,1)}) custom-call(s32[3]{0:T(128)} %pad_add_fusion.place_ref, bf16[4,1024,128]{2,1,0:T(8,128)(2,1)} %tokens_ref.3, bf16[512,128]{1,0:T(8,128)(2,1)} %query_ref.1, ...), custom_call_target="tpu_custom_call" | custom-call | flops 1000000000 | bytes 1048576 | tf_op jit(solution)/shard_map/moments/pallas_call | solution.py:72
  5.2 9.5 %all_to_all.25.moments_hbm = f32[4,2,4096]{2,1,0:T(2,128)} all-to-all(f32[4,2,4096]{2,1,0:T(2,128)} %get-tuple-element.19), channel_id=1, replica_groups=mesh['band'=16,'head'=4,'dp'=2] {'head'}, dimensions={0} | all-to-all | bytes 262144 | tf_op jit(solution)/shard_map/all_to_all | solution.py:560
  14.8 5.3 %normalize_sample.1 = (bf16[4,1024,128]{2,1,0:T(8,128)(2,1)}, bf16[2,1024,128]{2,1,0:T(8,128)(2,1)}, bf16[2,1024,128]{2,1,0:T(8,128)(2,1)}, bf16[1024,128]{1,0:T(8,128)(2,1)}) custom-call(s32[3]{0:T(128)} %pad_add_fusion.place_ref, f32[4,128]{1,0:T(4,128)} %bitcast.12, s32[1,1024]{1,0:T(1,128)} %bitcast.10, s32[1,1024]{1,0:T(1,128)} %bitcast.11, ...), custom_call_target="tpu_custom_call" | custom-call | flops 2000000000 | bytes 6291456 | tf_op jit(solution)/shard_map/normalize_sample/pallas_call | solution.py:213
  20.0 15.1 %all_to_all.26 = bf16[16,64,128]{2,1,0:T(8,128)(2,1)S(1)} all-to-all(bf16[16,64,128]{2,1,0:T(8,128)(2,1)} %bitcast.9), channel_id=1, replica_groups=mesh['band'=16,'head'=4,'dp'=2] {'band'}, dimensions={0} | all-to-all | bytes 524288 | tf_op jit(solution)/shard_map/all_to_all | solution.py:579
  35.2 1.2 broadcast_in_dim.3
  36.4 0.0 copy-start.14
  36.4 0.0 copy-start.11
  36.4 0.0 copy-start.10
  36.4 7.5 %all-to-all-start.2 = ((bf16[64,64,128]{2,1,0:T(8,128)(2,1)}), bf16[64,64,128]{2,1,0:T(8,128)(2,1)S(1)}, u32[]{:S(2)}, u32[]{:S(2)}) async-start(bf16[64,64,128]{2,1,0:T(8,128)(2,1)} %broadcast_in_dim.3), calls=%async_computation.2 | async-start | bytes 2097152 | tf_op jit(solution)/shard_map/all_to_all | solution.py:586
  44.0 0.0 copy-done.14
  44.0 1.5 %collective-permute-start.2 = (bf16[2048,128]{1,0:T(8,128)(2,1)S(1)}, bf16[2048,128]{1,0:T(8,128)(2,1)S(1)}, u32[]{:S(2)}, u32[]{:S(2)}) collective-permute-start(bf16[2048,128]{1,0:T(8,128)(2,1)S(1)} %copy-done.14), channel_id=1, source_target_pairs={{0,2},{2,4},{4,6},{6,0},{1,3},{3,5},{5,7},{7,1},{8,10},{10,12},{12... | collective-permute-start | bytes 1572872 | tf_op jit(solution)/shard_map/ppermute | solution.py:566
  45.5 0.0 copy-done.11
  45.5 1.2 collective-permute-start.3
  46.7 0.0 copy-done.10
  46.7 2.1 %collective-permute-start.4 = (bf16[2048,128]{1,0:T(8,128)(2,1)S(1)}, bf16[2048,128]{1,0:T(8,128)(2,1)S(1)}, u32[]{:S(2)}, u32[]{:S(2)}) collective-permute-start(bf16[2048,128]{1,0:T(8,128)(2,1)S(1)} %copy-done.10), channel_id=1, source_target_pairs={{0,6},{2,0},{4,2},{6,4},{1,7},{3,1},{5,3},{7,5},{8,14},{10,8},{12,... | collective-permute-start | bytes 1572872 | tf_op jit(solution)/shard_map/ppermute | solution.py:566
  48.8 17.3 %collective-permute-done.2.refs_1_.refs_6_.refs_2_.refs_3_ = bf16[2048,128]{1,0:T(8,128)(2,1)S(1)} collective-permute-done((bf16[2048,128]{1,0:T(8,128)(2,1)S(1)}, bf16[2048,128]{1,0:T(8,128)(2,1)S(1)}, u32[]{:S(2)}, u32[]{:S(2)}) %collective-permute-start.2) | collective-permute-done | bytes 524320 | tf_op jit(solution)/shard_map/ppermute | solution.py:566
  66.1 0.0 copy-start.1
  66.1 0.1 collective-permute-start.5
  66.2 1.2 collective-permute-done.3.refs_2_.refs_7_.refs_3_.refs_4_
  67.4 0.0 copy-start.2
  67.4 0.0 copy-done.1
  67.4 0.1 collective-permute-start.6
  67.5 9.4 %collective-permute-done.4.refs_3_.refs_8_.refs_4_.refs_5_ = bf16[2048,128]{1,0:T(8,128)(2,1)S(1)} collective-permute-done((bf16[2048,128]{1,0:T(8,128)(2,1)S(1)}, bf16[2048,128]{1,0:T(8,128)(2,1)S(1)}, u32[]{:S(2)}, u32[]{:S(2)}) %collective-permute-start.4) | collective-permute-done | bytes 524320 | tf_op jit(solution)/shard_map/ppermute | solution.py:566
  77.0 0.0 copy-start.3
  77.0 0.0 copy-done.2
  77.0 0.3 collective-permute-start.7
  77.3 0.0 collective-permute-done.5.refs_9_.refs_5_.refs_6_
  77.3 0.0 copy-start.4
  77.3 0.0 collective-permute-done.6.refs_10_.refs_6_.refs_7_
  77.3 0.0 copy-start.5
  77.3 1.5 collective-permute-done.7.refs_11_.refs_7_.refs_8_
  78.8 0.0 copy-start.6
  78.8 0.0 copy-done.3
  78.8 0.0 copy-done.4
  78.8 0.0 copy-done.5
  78.8 0.7 copy-done.6
  79.5 5.4 %query.1.query_hbm = bf16[4,1024,128]{2,1,0:T(8,128)(2,1)} custom-call(s32[3]{0:T(128)} %pad_add_fusion.place_ref, bf16[4,1024,128]{2,1,0:T(8,128)(2,1)} %tokens_ref.3, bf16[2048,128]{1,0:T(8,128)(2,1)} %copy-done.1, bf16[2048,128]{1,0:T(8,128)(2,1)} %copy-done.2, bf16[2048,128]{1,0:T(8,128)(2,1)} %copy-done.3, f32[4,128]{1,0:T(4,128)} %bitcast.13, ...), custom_call_target="tpu_custom_call" | custom-call | flops 2000000000 | bytes 3145728 | tf_op jit(solution)/shard_map/query/pallas_call | solution.py:293
  84.9 0.0 all-to-all-done.2
  84.9 0.0 copy-start
  84.9 1.0 copy-done
  85.9 17.3 %attend.2 = (bf16[4,512,128]{2,1,0:T(8,128)(2,1)}, bf16[4,1024,128]{2,1,0:T(8,128)(2,1)}, bf16[4,1024,128]{2,1,0:T(8,128)(2,1)}) custom-call(s32[3]{0:T(128)} %pad_add_fusion.place_ref, bf16[4,1024,128]{2,1,0:T(8,128)(2,1)} %query.1.query_hbm, bf16[16,4,64,128]{3,2,1,0:T(8,128)(2,1)} %bitcast.8, ...), custom_call_target="tpu_custom_call" | custom-call | flops 1073741824 | bytes 4194304 | tf_op jit(solution)/shard_map/attend/pallas_call | solution.py:453
  103.2 0.0 copy-start.9
  103.3 0.0 copy-start.8
  103.3 5.7 %all-to-all-start.3 = ((bf16[4,512,128]{2,1,0:T(8,128)(2,1)}), bf16[4,512,128]{2,1,0:T(8,128)(2,1)S(1)}, u32[]{:S(2)}, u32[]{:S(2)}) async-start(bf16[4,512,128]{2,1,0:T(8,128)(2,1)} %get-tuple-element.28), calls=%async_computation.3 | async-start | bytes 1048576 | tf_op jit(solution)/shard_map/all_to_all | solution.py:600
  109.0 0.0 copy-done.9
  109.0 3.4 %collective-permute-start = (bf16[2,1024,128]{2,1,0:T(8,128)(2,1)S(1)}, bf16[2,1024,128]{2,1,0:T(8,128)(2,1)S(1)}, u32[]{:S(2)}, u32[]{:S(2)}) collective-permute-start(bf16[2,1024,128]{2,1,0:T(8,128)(2,1)S(1)} %copy-done.9), channel_id=1, source_target_pairs={{0,8},{8,16},{16,24},{24,32},{32,40},{40,48},{48,56},{56,64},{64,7... | collective-permute-start | bytes 1572872 | tf_op jit(solution)/shard_map/ppermute | solution.py:582
  112.4 0.0 copy-done.8
  112.5 4.7 %collective-permute-start.1 = (bf16[2,1024,128]{2,1,0:T(8,128)(2,1)S(1)}, bf16[2,1024,128]{2,1,0:T(8,128)(2,1)S(1)}, u32[]{:S(2)}, u32[]{:S(2)}) collective-permute-start(bf16[2,1024,128]{2,1,0:T(8,128)(2,1)S(1)} %copy-done.8), channel_id=1, source_target_pairs={{8,0},{16,8},{24,16},{32,24},{40,32},{48,40},{56,48},{64,56},{72,6... | collective-permute-start | bytes 1572872 | tf_op jit(solution)/shard_map/ppermute | solution.py:583
  117.2 14.9 %attend.3 = bf16[4,512,128]{2,1,0:T(8,128)(2,1)} custom-call(s32[3]{0:T(128)} %pad_add_fusion.place_ref, bf16[4,1024,128]{2,1,0:T(8,128)(2,1)} %query.1.query_hbm, bf16[4,1024,128]{2,1,0:T(8,128)(2,1)} %get-tuple-element.31.refs_0_, bf16[4,1024,128]{2,1,0:T(8,128)(2,1)} %get-tuple-element.32.refs_1_, ...), custom_call_target="tpu_custom_call" | custom-call | flops 1073741824 | bytes 4194304 | tf_op jit(solution)/shard_map/attend/pallas_call | solution.py:453
  132.2 0.0 all-to-all-done.3.added_ref
  132.2 0.0 copy-start.7
  132.2 0.8 copy-done.7
  133.0 4.8 %all-to-all-start.4 = ((bf16[4,512,128]{2,1,0:T(8,128)(2,1)}), bf16[4,512,128]{2,1,0:T(8,128)(2,1)S(1)}, u32[]{:S(2)}, u32[]{:S(2)}) async-start(bf16[4,512,128]{2,1,0:T(8,128)(2,1)} %attend.3), calls=%async_computation.4 | async-start | bytes 1048576 | tf_op jit(solution)/shard_map/all_to_all | solution.py:600
  137.8 0.0 collective-permute-done.low_ref
  137.8 0.0 copy-start.12
  137.8 0.0 collective-permute-done.1.high_ref
  137.8 0.0 copy-start.13
  137.8 0.8 copy-done.12
  138.6 0.2 copy-done.13
  138.8 7.8 %convolve.1 = (bf16[4,1024,128]{2,1,0:T(8,128)(2,1)}, f32[4,512,128]{2,1,0:T(8,128)}) custom-call(bf16[2,1024,128]{2,1,0:T(8,128)(2,1)} %copy-done.12, bf16[4,1024,128]{2,1,0:T(8,128)(2,1)} %get-tuple-element.21.normed_ref, bf16[2,1024,128]{2,1,0:T(8,128)(2,1)} %copy-done.13, bf16[4,1024,128]{2,1,0:T(8,128)(2,1)} %tokens_ref.3, ...), custom_call_target="tpu_custom_call" | custom-call | flops 1000000000 | bytes 6291456 | tf_op jit(solution)/shard_map/convolve/pallas_call | solution.py:529
  146.5 0.0 all-to-all-done.4
  146.5 2.1 %fusion = bf16[4,1024,128]{2,1,0:T(8,128)(2,1)} fusion(bf16[4,1024,128]{2,1,0:T(8,128)(2,1)} %get-tuple-element.29, f32[4,512,128]{2,1,0:T(8,128)} %get-tuple-element.30, bf16[4,512,128]{2,1,0:T(8,128)(2,1)S(1)} %all-to-all-done.4), kind=kLoop, calls=%fused_computation.1 | loop fusion | flops 786432 | bytes 2097152 | tf_op jit(solution)/shard_map/dynamic_update_slice | solution.py:603
  (4 shorter events, 0.1 us)
Async XLA Ops:
  36.4 7.5 %copy-start.14 = (bf16[2048,128]{1,0:T(8,128)(2,1)S(1)}, bf16[2048,128]{1,0:T(8,128)(2,1)}, u32[]{:S(2)}) copy-start(bf16[2048,128]{1,0:T(8,128)(2,1)} %get-tuple-element.23) | copy-start | bytes 1572868
  36.4 9.1 %copy-start.11 = (bf16[2048,128]{1,0:T(8,128)(2,1)S(1)}, bf16[2048,128]{1,0:T(8,128)(2,1)}, u32[]{:S(2)}) copy-start(bf16[2048,128]{1,0:T(8,128)(2,1)} %get-tuple-element.24) | copy-start | bytes 1572868
  36.4 10.3 %copy-start.10 = (bf16[2048,128]{1,0:T(8,128)(2,1)S(1)}, bf16[2048,128]{1,0:T(8,128)(2,1)}, u32[]{:S(2)}) copy-start(bf16[2048,128]{1,0:T(8,128)(2,1)} %get-tuple-element.25) | copy-start | bytes 1572868
  36.4 48.5 %all-to-all-start.2 = ((bf16[64,64,128]{2,1,0:T(8,128)(2,1)}), bf16[64,64,128]{2,1,0:T(8,128)(2,1)S(1)}, u32[]{:S(2)}, u32[]{:S(2)}) async-start(bf16[64,64,128]{2,1,0:T(8,128)(2,1)} %broadcast_in_dim.3), calls=%async_computation.2 | async-start | bytes 2097152 | tf_op jit(solution)/shard_map/all_to_all | solution.py:586
  44.0 22.1 %collective-permute-start.2 = (bf16[2048,128]{1,0:T(8,128)(2,1)S(1)}, bf16[2048,128]{1,0:T(8,128)(2,1)S(1)}, u32[]{:S(2)}, u32[]{:S(2)}) collective-permute-start(bf16[2048,128]{1,0:T(8,128)(2,1)S(1)} %copy-done.14), channel_id=1, source_target_pairs={{0,2},{2,4},{4,6},{6,0},{1,3},{3,5},{5,7},{7,1},{8,10},{10,12},{12... | collective-permute-start | bytes 1572872 | tf_op jit(solution)/shard_map/ppermute | solution.py:566
  45.5 21.9 %collective-permute-start.3 = (bf16[2048,128]{1,0:T(8,128)(2,1)S(1)}, bf16[2048,128]{1,0:T(8,128)(2,1)S(1)}, u32[]{:S(2)}, u32[]{:S(2)}) collective-permute-start(bf16[2048,128]{1,0:T(8,128)(2,1)S(1)} %copy-done.11), channel_id=1, source_target_pairs={{0,4},{2,6},{4,0},{6,2},{1,5},{3,7},{5,1},{7,3},{8,12},{10,14},{12... | collective-permute-start | bytes 1572872 | tf_op jit(solution)/shard_map/ppermute | solution.py:566
  46.7 30.3 %collective-permute-start.4 = (bf16[2048,128]{1,0:T(8,128)(2,1)S(1)}, bf16[2048,128]{1,0:T(8,128)(2,1)S(1)}, u32[]{:S(2)}, u32[]{:S(2)}) collective-permute-start(bf16[2048,128]{1,0:T(8,128)(2,1)S(1)} %copy-done.10), channel_id=1, source_target_pairs={{0,6},{2,0},{4,2},{6,4},{1,7},{3,1},{5,3},{7,5},{8,14},{10,8},{12,... | collective-permute-start | bytes 1572872 | tf_op jit(solution)/shard_map/ppermute | solution.py:566
  66.1 1.3 copy-start.1
  66.1 11.2 %collective-permute-start.5 = (bf16[1024,128]{1,0:T(8,128)(2,1)S(1)}, bf16[1024,128]{1,0:T(8,128)(2,1)S(1)}, u32[]{:S(2)}, u32[]{:S(2)}) collective-permute-start(bf16[1024,128]{1,0:T(8,128)(2,1)S(1)} %slice.12), channel_id=1, source_target_pairs={{0,1},{1,0},{2,3},{3,2},{4,5},{5,4},{6,7},{7,6},{8,9},{9,8},{10,11... | collective-permute-start | bytes 786440 | tf_op jit(solution)/shard_map/ppermute | solution.py:571
  67.4 9.6 %copy-start.2 = (bf16[2048,128]{1,0:T(8,128)(2,1)}, bf16[2048,128]{1,0:T(8,128)(2,1)S(1)}, u32[]{:S(2)}) copy-start(bf16[2048,128]{1,0:T(8,128)(2,1)S(1)} %collective-permute-done.3.refs_2_.refs_7_.refs_3_.refs_4_) | copy-start | bytes 1572868
  67.4 9.9 %collective-permute-start.6 = (bf16[1024,128]{1,0:T(8,128)(2,1)S(1)}, bf16[1024,128]{1,0:T(8,128)(2,1)S(1)}, u32[]{:S(2)}, u32[]{:S(2)}) collective-permute-start(bf16[1024,128]{1,0:T(8,128)(2,1)S(1)} %slice.13), channel_id=1, source_target_pairs={{0,1},{1,0},{2,3},{3,2},{4,5},{5,4},{6,7},{7,6},{8,9},{9,8},{10,11... | collective-permute-start | bytes 786440 | tf_op jit(solution)/shard_map/ppermute | solution.py:571
  77.0 1.8 %copy-start.3 = (bf16[2048,128]{1,0:T(8,128)(2,1)}, bf16[2048,128]{1,0:T(8,128)(2,1)S(1)}, u32[]{:S(2)}) copy-start(bf16[2048,128]{1,0:T(8,128)(2,1)S(1)} %collective-permute-done.4.refs_3_.refs_8_.refs_4_.refs_5_) | copy-start | bytes 1572868
  77.0 1.8 %collective-permute-start.7 = (bf16[1024,128]{1,0:T(8,128)(2,1)S(1)}, bf16[1024,128]{1,0:T(8,128)(2,1)S(1)}, u32[]{:S(2)}, u32[]{:S(2)}) collective-permute-start(bf16[1024,128]{1,0:T(8,128)(2,1)S(1)} %slice.14), channel_id=1, source_target_pairs={{0,1},{1,0},{2,3},{3,2},{4,5},{5,4},{6,7},{7,6},{8,9},{9,8},{10,11... | collective-permute-start | bytes 786440 | tf_op jit(solution)/shard_map/ppermute | solution.py:571
  77.3 1.5 %copy-start.4 = (bf16[1024,128]{1,0:T(8,128)(2,1)}, bf16[1024,128]{1,0:T(8,128)(2,1)S(1)}, u32[]{:S(2)}) copy-start(bf16[1024,128]{1,0:T(8,128)(2,1)S(1)} %collective-permute-done.5.refs_9_.refs_5_.refs_6_) | copy-start | bytes 786436
  77.3 1.5 %copy-start.5 = (bf16[1024,128]{1,0:T(8,128)(2,1)}, bf16[1024,128]{1,0:T(8,128)(2,1)S(1)}, u32[]{:S(2)}) copy-start(bf16[1024,128]{1,0:T(8,128)(2,1)S(1)} %collective-permute-done.6.refs_10_.refs_6_.refs_7_) | copy-start | bytes 786436
  78.8 0.7 copy-start.6
  84.9 1.0 copy-start
  103.2 5.8 %copy-start.9 = (bf16[2,1024,128]{2,1,0:T(8,128)(2,1)S(1)}, bf16[2,1024,128]{2,1,0:T(8,128)(2,1)}, u32[]{:S(2)}) copy-start(bf16[2,1024,128]{2,1,0:T(8,128)(2,1)} %get-tuple-element.20) | copy-start | bytes 1572868
  103.3 9.2 %copy-start.8 = (bf16[2,1024,128]{2,1,0:T(8,128)(2,1)S(1)}, bf16[2,1024,128]{2,1,0:T(8,128)(2,1)}, u32[]{:S(2)}) copy-start(bf16[2,1024,128]{2,1,0:T(8,128)(2,1)} %get-tuple-element.22) | copy-start | bytes 1572868
  103.3 28.9 %all-to-all-start.3 = ((bf16[4,512,128]{2,1,0:T(8,128)(2,1)}), bf16[4,512,128]{2,1,0:T(8,128)(2,1)S(1)}, u32[]{:S(2)}, u32[]{:S(2)}) async-start(bf16[4,512,128]{2,1,0:T(8,128)(2,1)} %get-tuple-element.28), calls=%async_computation.3 | async-start | bytes 1048576 | tf_op jit(solution)/shard_map/all_to_all | solution.py:600
  109.0 28.8 %collective-permute-start = (bf16[2,1024,128]{2,1,0:T(8,128)(2,1)S(1)}, bf16[2,1024,128]{2,1,0:T(8,128)(2,1)S(1)}, u32[]{:S(2)}, u32[]{:S(2)}) collective-permute-start(bf16[2,1024,128]{2,1,0:T(8,128)(2,1)S(1)} %copy-done.9), channel_id=1, source_target_pairs={{0,8},{8,16},{16,24},{24,32},{32,40},{40,48},{48,56},{56,64},{64,7... | collective-permute-start | bytes 1572872 | tf_op jit(solution)/shard_map/ppermute | solution.py:582
  112.5 25.3 %collective-permute-start.1 = (bf16[2,1024,128]{2,1,0:T(8,128)(2,1)S(1)}, bf16[2,1024,128]{2,1,0:T(8,128)(2,1)S(1)}, u32[]{:S(2)}, u32[]{:S(2)}) collective-permute-start(bf16[2,1024,128]{2,1,0:T(8,128)(2,1)S(1)} %copy-done.8), channel_id=1, source_target_pairs={{8,0},{16,8},{24,16},{32,24},{40,32},{48,40},{56,48},{64,56},{72,6... | collective-permute-start | bytes 1572872 | tf_op jit(solution)/shard_map/ppermute | solution.py:583
  132.2 0.8 copy-start.7
  133.0 13.6 %all-to-all-start.4 = ((bf16[4,512,128]{2,1,0:T(8,128)(2,1)}), bf16[4,512,128]{2,1,0:T(8,128)(2,1)S(1)}, u32[]{:S(2)}, u32[]{:S(2)}) async-start(bf16[4,512,128]{2,1,0:T(8,128)(2,1)} %attend.3), calls=%async_computation.4 | async-start | bytes 1048576 | tf_op jit(solution)/shard_map/all_to_all | solution.py:600
  137.8 0.8 copy-start.12
  137.8 1.0 copy-start.13

commit v4 on v3

--- a/solution.py
+++ b/solution.py
@@ -25,27 +25,42 @@
 
 
 def moments_kernel(
-    place_ref, tokens_ref, query_ref, key_ref, value_ref, out_weight_ref, moments_ref, own_ref, *refs
+    tokens_hbm, query_hbm, key_hbm, value_hbm, out_weight_hbm, moments_ref, own_hbm, *refs
 ):
-    *bulk_hbm, half, leave = refs
+    *bulk_hbm, tokens_ref, own, half, arrive, leave = refs
     rows, columns, channels = tokens_ref.shape
-    depth = query_ref.shape[0]
-    for index, ref in enumerate((query_ref, key_ref, value_ref)):
-        own_ref[index] = ref[...]
+    depth = query_hbm.shape[0]
+    fetches = []
+
+    def fetch(source, target):
+        fetches.append(pltpu.make_async_copy(source, target, arrive.at[len(fetches)]))
+        fetches[-1].start()
+
+    for row in range(rows):
+        fetch(tokens_hbm.at[row], tokens_ref.at[row])
+    for index, source in enumerate((query_hbm, key_hbm, value_hbm)):
+        fetch(source, own.at[index])
     for g in range(rows):
-        at = slice(g * channels, (g + 1) * channels)
-        own_ref[3, at, :] = out_weight_ref[:, at]
+        at = pl.ds(g * channels, channels)
+        fetch(out_weight_hbm.at[:, at], own.at[3, at])
+    for waited in fetches:
+        waited.wait()
+    stores = []
+
+    def send(source, target):
+        stores.append(pltpu.make_async_copy(source, target, leave.at[len(stores)]))
+        stores[-1].start()
+
+    send(own, own_hbm)
+    for distance, target in enumerate(bulk_hbm, 1):
+        row = lax.rem(lax.axis_index("head") + distance, rows)
+        send(tokens_ref.at[row], target.at[pl.ds(0, columns)])
     cut = depth // 2
-    lines = pl.ds(pl.multiple_of(place_ref[1] * cut, cut), cut)
+    lines = pl.ds(pl.multiple_of(lax.axis_index("dp") * cut, cut), cut)
     for index in range(4):
-        half[index * cut : (index + 1) * cut, :] = own_ref[index, lines, :]
-    stores = []
-    for distance, target in enumerate(bulk_hbm, 1):
-        row = lax.rem(place_ref[0] + distance, rows)
-        for source, start in ((tokens_ref.at[row], 0), (half, columns)):
-            place = target.at[pl.ds(start, source.shape[0])]
-            stores.append(pltpu.make_async_copy(source, place, leave.at[len(stores)]))
-            stores[-1].start()
+        half[index * cut : (index + 1) * cut, :] = own[index, lines, :]
+    for target in bulk_hbm:
+        send(half, target.at[pl.ds(columns, 2 * depth)])
     side = lax.broadcasted_iota(jnp.int32, (8, 2 * channels), 1) // channels
     pick = jnp.where(side == lax.broadcasted_iota(jnp.int32, (8, 2 * channels), 0), 1.0, 0.0)
     pick = pick.astype(BF)
@@ -63,7 +78,7 @@
         store.wait()
 
 
-def moments_and_bulk(place, tokens, w_query, w_key, w_value, w_out, copies):
+def moments_and_bulk(tokens, w_query, w_key, w_value, w_out, copies):
     rows, columns, channels = tokens.shape
     depth = w_query.shape[0]
     vmem = pl.BlockSpec(memory_space=pltpu.VMEM)
@@ -71,20 +86,23 @@
     bulk = jax.ShapeDtypeStruct((columns + 2 * depth, channels), BF)
     moments, own, *bulk = pl.pallas_call(
         moments_kernel,
-        in_specs=[pl.BlockSpec(memory_space=pltpu.SMEM)] + [vmem] * 5,
-        out_specs=(vmem, vmem, *[anywhere] * (copies - 1)),
+        in_specs=[anywhere] * 5,
+        out_specs=(vmem, anywhere, *[anywhere] * (copies - 1)),
         out_shape=(
             jax.ShapeDtypeStruct((copies, 2, rows * columns), F32),
             jax.ShapeDtypeStruct((4, depth, channels), BF),
             *[bulk] * (copies - 1),
         ),
         scratch_shapes=[
+            pltpu.VMEM(tokens.shape, BF),
+            pltpu.VMEM((4, depth, channels), BF),
             pltpu.VMEM((2 * depth, channels), BF),
-            pltpu.SemaphoreType.DMA((2 * copies,)),
+            pltpu.SemaphoreType.DMA((2 * rows + 3,)),
+            pltpu.SemaphoreType.DMA((2 * copies - 1,)),
         ],
         cost_estimate=pl.CostEstimate(flops=10**9, bytes_accessed=2**20, transcendentals=0),
         name="moments",
-    )(place, tokens, w_query, w_key, w_value, w_out)
+    )(tokens, w_query, w_key, w_value, w_out)
     return moments, own, bulk
 
 
@@ -131,7 +149,6 @@
 
 
 def normalize_sample_kernel(
-    place_ref,
     gain_ref,
     row_ref,
     column_ref,
@@ -159,7 +176,7 @@
         fetches[-1].start()
     rows, columns, channels = tokens.shape
     devices = moments.shape[0]
-    make_tables(place_ref[2], row_ref, column_ref, fraction_ref, table, weights)
+    make_tables(lax.axis_index("band"), row_ref, column_ref, fraction_ref, table, weights)
     fetches[0].wait()
     sums = [moments[d, 0:1, :] for d in range(devices)]
     width = channels * devices
@@ -174,7 +191,7 @@
     piece = lax.broadcasted_iota(jnp.int32, (16, 2 * channels), 0)
     lane = lax.broadcasted_iota(jnp.int32, (16, 2 * channels), 1)
     pick = jnp.where((piece < 6) & (piece // 3 == lane // channels), 1.0, 0.0).astype(BF)
-    gain = gain_ref[pl.ds(place_ref[0], 1), :]
+    gain = gain_ref[pl.ds(lax.axis_index("head"), 1), :]
     margin = KER // 2
     fetches[1].wait()
     stores = []
@@ -204,7 +221,7 @@
         store.wait()
 
 
-def normalize_and_sample(place, gain, corner_row, corner_col, fraction, tokens, moments):
+def normalize_and_sample(gain, corner_row, corner_col, fraction, tokens, moments):
     rows, columns, channels = tokens.shape
     points = corner_row.shape[0]
     vmem = pl.BlockSpec(memory_space=pltpu.VMEM)
@@ -212,7 +229,7 @@
     edge = jax.ShapeDtypeStruct((KER // 2, columns, channels), BF)
     return pl.pallas_call(
         normalize_sample_kernel,
-        in_specs=[pl.BlockSpec(memory_space=pltpu.SMEM)] + [vmem] * 4 + [anywhere] * 2,
+        in_specs=[vmem] * 4 + [anywhere] * 2,
         out_specs=(anywhere, anywhere, anywhere, vmem),
         out_shape=(
             jax.ShapeDtypeStruct(tokens.shape, BF),
@@ -233,7 +250,6 @@
         cost_estimate=pl.CostEstimate(flops=2 * 10**9, bytes_accessed=6 * 2**20, transcendentals=0),
         name="normalize_sample",
     )(
-        place,
         gain,
         corner_row.reshape(1, points),
         corner_col.reshape(1, points),
@@ -553,10 +569,8 @@
 
     head = lax.axis_index("head")
     core = lax.axis_index("dp")
-    place = jnp.stack([head, core, lax.axis_index("band")])
-    moments, own, bulk = moments_and_bulk(
-        place, tokens, w_query, w_key, w_value, w_out, groups
-    )
+    place = jnp.stack([head, core])
+    moments, own, bulk = moments_and_bulk(tokens, w_query, w_key, w_value, w_out, groups)
     moments = lax.all_to_all(moments, "head", 0, 0, tiled=True)
 
     def to_all_heads(blocks):
@@ -573,7 +587,7 @@
     gain = norm_gain.reshape(groups, channels)
 
     normed, low, high, partial = normalize_and_sample(
-        place, gain, corner_row, corner_col, fraction, tokens, moments
+        gain, corner_row, corner_col, fraction, tokens, moments
     )
 
     parts = lax.all_to_all(partial.reshape(bands, share, channels), "band", 0, 0, tiled=True)
@@ -590,7 +604,7 @@
     scale = 1.4426950408889634 / size**0.5
     query = query_of(place, token_rows, gain, weights, columns, scale)
     half_way = columns // 2
-    chunks = ((0, half_way, half_way // 2), (half_way, half_way, half_way // 2))
+    chunks = ((0, half_way, half_way), (half_way, half_way, half_way))
     returned = []
     source = (blocks,)
     for chunk, (start, count, block) in enumerate(chunks):

time: 150 us -> 147 us (0.980)
  Pallas kernels: 55.3 us -> 53.7 us
where the time goes in v4:
time: 147 us; the launch traced here: 146 us
  Pallas kernels  53.7 us (37%)
  starting transfers between devices  31.2 us (21%)
  waiting for transfers between devices  28.9 us (20%)
  blocking collectives  24.7 us (17%)
  local copies, waits for them, and re-layouts  4.74 us (3%)
  other arithmetic  2.77 us (2%)
    pallas_call x2, Pallas kernels, attend_and_project(): pl.pallas_call(functools.partial(attend_kernel, HEADS // groups, first, s...  31.1 us
    ppermute x3, waiting for transfers between devices, to_all_heads(): arrived[distance] = lax.ppermute(blocks[distance], 'head', ring)  28 us
    all_to_all x1, blocking collectives, body(): lax.all_to_all(partial.reshape(bands, share, channels), 'band', 0, 0, til...  15.1 us
    all_to_all x2, starting transfers between devices, body(): returned.append(lax.all_to_all(projected, 'head', 0, 0, tiled=True))  10.7 us
    all_to_all x1, blocking collectives, body(): moments = lax.all_to_all(moments, 'head', 0, 0, tiled=True)  9.54 us
    pallas_call x1, Pallas kernels, convolve(): pl.pallas_call(convolve_kernel, grid=(steps,), in_specs=[edge, whole, edg...  7.79 us
    all_to_all x1, starting transfers between devices, body(): blocks = lax.all_to_all(copies, ('band', 'head'), 0, 0, tiled=True)  7.53 us
    pallas_call x1, Pallas kernels, query_of(): pl.pallas_call(functools.partial(query_kernel, scale, groups), grid_spec=...  5.4 us
  transfers between devices with their start and end apart: 11, of which 4 were waited for; matrix products, arithmetic and copies ran while one was open for 0% of the time, Pallas kernels for 19%

profile of v4, /device:TPU:10, one launch (start us, length us, event | category | flops | bytes accessed | tf_op | source)
XLA Modules:
  0.0 146.2 jit_solution(11444186175620671727)
XLA Ops:
  0.0 4.2 %moments.1 = (f32[4,2,4096]{2,1,0:T(2,128)}, bf16[4,512,128]{2,1,0:T(8,128)(2,1)}, bf16[2048,128]{1,0:T(8,128)(2,1)}, bf16[2048,128]{1,0:T(8,128)(2,1)}, bf16[2048,128]{1,0:T(8,128)(2,1)}) custom-call(bf16[4,1024,128]{2,1,0:T(8,128)(2,1)} %tokens_ref.1, bf16[512,128]{1,0:T(8,128)(2,1)} %query_hbm.1, bf16[512,128]{1,0:T(8,128)(2,1)} %key_hbm.1, ...), custom_call_target="tpu_custom_call" | custom-call | flops 1000000000 | bytes 1048576 | tf_op jit(solution)/shard_map/moments/pallas_call | solution.py:87
  4.2 9.5 %all_to_all.25.moments_hbm = f32[4,2,4096]{2,1,0:T(2,128)} all-to-all(f32[4,2,4096]{2,1,0:T(2,128)} %get-tuple-element.19), channel_id=1, replica_groups=mesh['band'=16,'head'=4,'dp'=2] {'head'}, dimensions={0} | all-to-all | bytes 262144 | tf_op jit(solution)/shard_map/all_to_all | solution.py:574
  13.8 5.2 %normalize_sample.1 = (bf16[4,1024,128]{2,1,0:T(8,128)(2,1)}, bf16[2,1024,128]{2,1,0:T(8,128)(2,1)}, bf16[2,1024,128]{2,1,0:T(8,128)(2,1)}, bf16[1024,128]{1,0:T(8,128)(2,1)}) custom-call(f32[4,128]{1,0:T(4,128)} %bitcast.11, s32[1,1024]{1,0:T(1,128)} %bitcast.9, s32[1,1024]{1,0:T(1,128)} %bitcast.10, f32[2,1024]{1,0:T(2,128)} %fraction_ref.1, ...), custom_call_target="tpu_custom_call" | custom-call | flops 2000000000 | bytes 6291456 | tf_op jit(solution)/shard_map/normalize_sample/pallas_call | solution.py:230
  19.0 15.1 %all_to_all.26 = bf16[16,64,128]{2,1,0:T(8,128)(2,1)S(1)} all-to-all(bf16[16,64,128]{2,1,0:T(8,128)(2,1)} %bitcast.8), channel_id=1, replica_groups=mesh['band'=16,'head'=4,'dp'=2] {'band'}, dimensions={0} | all-to-all | bytes 524288 | tf_op jit(solution)/shard_map/all_to_all | solution.py:593
  34.2 1.2 broadcast_in_dim.3
  35.4 0.0 copy-start.14
  35.4 0.0 copy-start.11
  35.4 0.0 copy-start.10
  35.4 7.5 %all-to-all-start.2 = ((bf16[64,64,128]{2,1,0:T(8,128)(2,1)}), bf16[64,64,128]{2,1,0:T(8,128)(2,1)S(1)}, u32[]{:S(2)}, u32[]{:S(2)}) async-start(bf16[64,64,128]{2,1,0:T(8,128)(2,1)} %broadcast_in_dim.3), calls=%async_computation.2 | async-start | bytes 2097152 | tf_op jit(solution)/shard_map/all_to_all | solution.py:600
  42.9 0.0 copy-done.14
  42.9 1.5 %collective-permute-start.2 = (bf16[2048,128]{1,0:T(8,128)(2,1)S(1)}, bf16[2048,128]{1,0:T(8,128)(2,1)S(1)}, u32[]{:S(2)}, u32[]{:S(2)}) collective-permute-start(bf16[2048,128]{1,0:T(8,128)(2,1)S(1)} %copy-done.14), channel_id=1, source_target_pairs={{0,2},{2,4},{4,6},{6,0},{1,3},{3,5},{5,7},{7,1},{8,10},{10,12},{12... | collective-permute-start | bytes 1572872 | tf_op jit(solution)/shard_map/ppermute | solution.py:580
  44.5 0.0 copy-done.11
  44.5 1.2 collective-permute-start.3
  45.6 0.0 copy-done.10
  45.6 2.1 %collective-permute-start.4 = (bf16[2048,128]{1,0:T(8,128)(2,1)S(1)}, bf16[2048,128]{1,0:T(8,128)(2,1)S(1)}, u32[]{:S(2)}, u32[]{:S(2)}) collective-permute-start(bf16[2048,128]{1,0:T(8,128)(2,1)S(1)} %copy-done.10), channel_id=1, source_target_pairs={{0,6},{2,0},{4,2},{6,4},{1,7},{3,1},{5,3},{7,5},{8,14},{10,8},{12,... | collective-permute-start | bytes 1572872 | tf_op jit(solution)/shard_map/ppermute | solution.py:580
  47.7 17.3 %collective-permute-done.2.refs_1_.refs_6_.refs_2_.refs_3_ = bf16[2048,128]{1,0:T(8,128)(2,1)S(1)} collective-permute-done((bf16[2048,128]{1,0:T(8,128)(2,1)S(1)}, bf16[2048,128]{1,0:T(8,128)(2,1)S(1)}, u32[]{:S(2)}, u32[]{:S(2)}) %collective-permute-start.2) | collective-permute-done | bytes 524320 | tf_op jit(solution)/shard_map/ppermute | solution.py:580
  65.1 0.0 copy-start.1
  65.1 0.1 collective-permute-start.5
  65.2 1.2 collective-permute-done.3.refs_2_.refs_7_.refs_3_.refs_4_
  66.4 0.0 copy-start.2
  66.4 0.0 copy-done.1
  66.4 0.1 collective-permute-start.6
  66.5 9.4 %collective-permute-done.4.refs_3_.refs_8_.refs_4_.refs_5_ = bf16[2048,128]{1,0:T(8,128)(2,1)S(1)} collective-permute-done((bf16[2048,128]{1,0:T(8,128)(2,1)S(1)}, bf16[2048,128]{1,0:T(8,128)(2,1)S(1)}, u32[]{:S(2)}, u32[]{:S(2)}) %collective-permute-start.4) | collective-permute-done | bytes 524320 | tf_op jit(solution)/shard_map/ppermute | solution.py:580
  75.9 0.0 copy-start.3
  75.9 0.0 copy-done.2
  76.0 0.1 collective-permute-start.7
  76.1 0.6 pad_add_fusion.place_ref
  76.7 0.0 collective-permute-done.5.refs_9_.refs_5_.refs_6_
  76.7 0.0 copy-start.4
  76.7 0.0 collective-permute-done.6.refs_10_.refs_6_.refs_7_
  76.7 0.0 copy-start.5
  76.7 0.9 collective-permute-done.7.refs_11_.refs_7_.refs_8_
  77.6 0.0 copy-start.6
  77.6 0.0 copy-done.3
  77.6 0.0 copy-done.4
  77.6 0.0 copy-done.5
  77.6 0.7 copy-done.6
  78.3 5.4 %query.1.query_hbm = bf16[4,1024,128]{2,1,0:T(8,128)(2,1)} custom-call(s32[2]{0:T(128)} %pad_add_fusion.place_ref, bf16[4,1024,128]{2,1,0:T(8,128)(2,1)} %tokens_ref.1, bf16[2048,128]{1,0:T(8,128)(2,1)} %copy-done.1, bf16[2048,128]{1,0:T(8,128)(2,1)} %copy-done.2, bf16[2048,128]{1,0:T(8,128)(2,1)} %copy-done.3, f32[4,128]{1,0:T(4,128)} %bitcast.12, ...), custom_call_target="tpu_custom_call" | custom-call | flops 2000000000 | bytes 3145728 | tf_op jit(solution)/shard_map/query/pallas_call | solution.py:309
  83.7 0.0 all-to-all-done.2
  83.7 0.0 copy-start
  83.7 1.0 copy-done
  84.7 16.6 %attend.2 = (bf16[4,512,128]{2,1,0:T(8,128)(2,1)}, bf16[4,1024,128]{2,1,0:T(8,128)(2,1)}, bf16[4,1024,128]{2,1,0:T(8,128)(2,1)}) custom-call(s32[2]{0:T(128)} %pad_add_fusion.place_ref, bf16[4,1024,128]{2,1,0:T(8,128)(2,1)} %query.1.query_hbm, bf16[16,4,64,128]{3,2,1,0:T(8,128)(2,1)} %bitcast.7, ...), custom_call_target="tpu_custom_call" | custom-call | flops 1073741824 | bytes 4194304 | tf_op jit(solution)/shard_map/attend/pallas_call | solution.py:469
  101.3 0.0 copy-start.9
  101.3 0.0 copy-start.8
  101.3 5.9 %all-to-all-start.3 = ((bf16[4,512,128]{2,1,0:T(8,128)(2,1)}), bf16[4,512,128]{2,1,0:T(8,128)(2,1)S(1)}, u32[]{:S(2)}, u32[]{:S(2)}) async-start(bf16[4,512,128]{2,1,0:T(8,128)(2,1)} %get-tuple-element.28), calls=%async_computation.3 | async-start | bytes 1048576 | tf_op jit(solution)/shard_map/all_to_all | solution.py:614
  107.3 0.0 copy-done.9
  107.3 3.4 %collective-permute-start = (bf16[2,1024,128]{2,1,0:T(8,128)(2,1)S(1)}, bf16[2,1024,128]{2,1,0:T(8,128)(2,1)S(1)}, u32[]{:S(2)}, u32[]{:S(2)}) collective-permute-start(bf16[2,1024,128]{2,1,0:T(8,128)(2,1)S(1)} %copy-done.9), channel_id=1, source_target_pairs={{0,8},{8,16},{16,24},{24,32},{32,40},{40,48},{48,56},{56,64},{64,7... | collective-permute-start | bytes 1572872 | tf_op jit(solution)/shard_map/ppermute | solution.py:596
  110.7 0.0 copy-done.8
  110.7 4.5 %collective-permute-start.1 = (bf16[2,1024,128]{2,1,0:T(8,128)(2,1)S(1)}, bf16[2,1024,128]{2,1,0:T(8,128)(2,1)S(1)}, u32[]{:S(2)}, u32[]{:S(2)}) collective-permute-start(bf16[2,1024,128]{2,1,0:T(8,128)(2,1)S(1)} %copy-done.8), channel_id=1, source_target_pairs={{8,0},{16,8},{24,16},{32,24},{40,32},{48,40},{56,48},{64,56},{72,6... | collective-permute-start | bytes 1572872 | tf_op jit(solution)/shard_map/ppermute | solution.py:597
  115.2 14.5 %attend.3 = bf16[4,512,128]{2,1,0:T(8,128)(2,1)} custom-call(s32[2]{0:T(128)} %pad_add_fusion.place_ref, bf16[4,1024,128]{2,1,0:T(8,128)(2,1)} %query.1.query_hbm, bf16[4,1024,128]{2,1,0:T(8,128)(2,1)} %get-tuple-element.31.refs_0_, bf16[4,1024,128]{2,1,0:T(8,128)(2,1)} %get-tuple-element.32.refs_1_, ...), custom_call_target="tpu_custom_call" | custom-call | flops 1073741824 | bytes 4194304 | tf_op jit(solution)/shard_map/attend/pallas_call | solution.py:469
  129.7 0.0 all-to-all-done.3.added_ref
  129.7 0.0 copy-start.7
  129.7 0.8 copy-done.7
  130.5 4.8 %all-to-all-start.4 = ((bf16[4,512,128]{2,1,0:T(8,128)(2,1)}), bf16[4,512,128]{2,1,0:T(8,128)(2,1)S(1)}, u32[]{:S(2)}, u32[]{:S(2)}) async-start(bf16[4,512,128]{2,1,0:T(8,128)(2,1)} %attend.3), calls=%async_computation.4 | async-start | bytes 1048576 | tf_op jit(solution)/shard_map/all_to_all | solution.py:614
  135.3 0.0 collective-permute-done.low_ref
  135.3 0.0 copy-start.12
  135.3 0.0 collective-permute-done.1.high_ref
  135.4 0.0 copy-start.13
  135.4 0.8 copy-done.12
  136.2 0.2 copy-done.13
  136.3 7.8 %convolve.1 = (bf16[4,1024,128]{2,1,0:T(8,128)(2,1)}, f32[4,512,128]{2,1,0:T(8,128)}) custom-call(bf16[2,1024,128]{2,1,0:T(8,128)(2,1)} %copy-done.12, bf16[4,1024,128]{2,1,0:T(8,128)(2,1)} %get-tuple-element.21.normed_ref, bf16[2,1024,128]{2,1,0:T(8,128)(2,1)} %copy-done.13, bf16[4,1024,128]{2,1,0:T(8,128)(2,1)} %tokens_ref.1, ...), custom_call_target="tpu_custom_call" | custom-call | flops 1000000000 | bytes 6291456 | tf_op jit(solution)/shard_map/convolve/pallas_call | solution.py:545
  144.1 0.0 all-to-all-done.4
  144.1 2.1 %fusion = bf16[4,1024,128]{2,1,0:T(8,128)(2,1)} fusion(bf16[4,1024,128]{2,1,0:T(8,128)(2,1)} %get-tuple-element.29, f32[4,512,128]{2,1,0:T(8,128)} %get-tuple-element.30, bf16[4,512,128]{2,1,0:T(8,128)(2,1)S(1)} %all-to-all-done.4), kind=kLoop, calls=%fused_computation.1 | loop fusion | flops 786432 | bytes 2097152 | tf_op jit(solution)/shard_map/dynamic_update_slice | solution.py:617
  (4 shorter events, 0.1 us)
Async XLA Ops:
  35.4 7.5 %copy-start.14 = (bf16[2048,128]{1,0:T(8,128)(2,1)S(1)}, bf16[2048,128]{1,0:T(8,128)(2,1)}, u32[]{:S(2)}) copy-start(bf16[2048,128]{1,0:T(8,128)(2,1)} %get-tuple-element.23) | copy-start | bytes 1572868
  35.4 9.1 %copy-start.11 = (bf16[2048,128]{1,0:T(8,128)(2,1)S(1)}, bf16[2048,128]{1,0:T(8,128)(2,1)}, u32[]{:S(2)}) copy-start(bf16[2048,128]{1,0:T(8,128)(2,1)} %get-tuple-element.24) | copy-start | bytes 1572868
  35.4 10.3 %copy-start.10 = (bf16[2048,128]{1,0:T(8,128)(2,1)S(1)}, bf16[2048,128]{1,0:T(8,128)(2,1)}, u32[]{:S(2)}) copy-start(bf16[2048,128]{1,0:T(8,128)(2,1)} %get-tuple-element.25) | copy-start | bytes 1572868
  35.4 48.3 %all-to-all-start.2 = ((bf16[64,64,128]{2,1,0:T(8,128)(2,1)}), bf16[64,64,128]{2,1,0:T(8,128)(2,1)S(1)}, u32[]{:S(2)}, u32[]{:S(2)}) async-start(bf16[64,64,128]{2,1,0:T(8,128)(2,1)} %broadcast_in_dim.3), calls=%async_computation.2 | async-start | bytes 2097152 | tf_op jit(solution)/shard_map/all_to_all | solution.py:600
  42.9 22.1 %collective-permute-start.2 = (bf16[2048,128]{1,0:T(8,128)(2,1)S(1)}, bf16[2048,128]{1,0:T(8,128)(2,1)S(1)}, u32[]{:S(2)}, u32[]{:S(2)}) collective-permute-start(bf16[2048,128]{1,0:T(8,128)(2,1)S(1)} %copy-done.14), channel_id=1, source_target_pairs={{0,2},{2,4},{4,6},{6,0},{1,3},{3,5},{5,7},{7,1},{8,10},{10,12},{12... | collective-permute-start | bytes 1572872 | tf_op jit(solution)/shard_map/ppermute | solution.py:580
  44.5 21.9 %collective-permute-start.3 = (bf16[2048,128]{1,0:T(8,128)(2,1)S(1)}, bf16[2048,128]{1,0:T(8,128)(2,1)S(1)}, u32[]{:S(2)}, u32[]{:S(2)}) collective-permute-start(bf16[2048,128]{1,0:T(8,128)(2,1)S(1)} %copy-done.11), channel_id=1, source_target_pairs={{0,4},{2,6},{4,0},{6,2},{1,5},{3,7},{5,1},{7,3},{8,12},{10,14},{12... | collective-permute-start | bytes 1572872 | tf_op jit(solution)/shard_map/ppermute | solution.py:580
  45.6 30.3 %collective-permute-start.4 = (bf16[2048,128]{1,0:T(8,128)(2,1)S(1)}, bf16[2048,128]{1,0:T(8,128)(2,1)S(1)}, u32[]{:S(2)}, u32[]{:S(2)}) collective-permute-start(bf16[2048,128]{1,0:T(8,128)(2,1)S(1)} %copy-done.10), channel_id=1, source_target_pairs={{0,6},{2,0},{4,2},{6,4},{1,7},{3,1},{5,3},{7,5},{8,14},{10,8},{12,... | collective-permute-start | bytes 1572872 | tf_op jit(solution)/shard_map/ppermute | solution.py:580
  65.1 1.3 copy-start.1
  65.1 11.6 %collective-permute-start.5 = (bf16[1024,128]{1,0:T(8,128)(2,1)S(1)}, bf16[1024,128]{1,0:T(8,128)(2,1)S(1)}, u32[]{:S(2)}, u32[]{:S(2)}) collective-permute-start(bf16[1024,128]{1,0:T(8,128)(2,1)S(1)} %slice.12), channel_id=1, source_target_pairs={{0,1},{1,0},{2,3},{3,2},{4,5},{5,4},{6,7},{7,6},{8,9},{9,8},{10,11... | collective-permute-start | bytes 786440 | tf_op jit(solution)/shard_map/ppermute | solution.py:585
  66.4 9.6 %copy-start.2 = (bf16[2048,128]{1,0:T(8,128)(2,1)}, bf16[2048,128]{1,0:T(8,128)(2,1)S(1)}, u32[]{:S(2)}) copy-start(bf16[2048,128]{1,0:T(8,128)(2,1)S(1)} %collective-permute-done.3.refs_2_.refs_7_.refs_3_.refs_4_) | copy-start | bytes 1572868
  66.4 10.3 %collective-permute-start.6 = (bf16[1024,128]{1,0:T(8,128)(2,1)S(1)}, bf16[1024,128]{1,0:T(8,128)(2,1)S(1)}, u32[]{:S(2)}, u32[]{:S(2)}) collective-permute-start(bf16[1024,128]{1,0:T(8,128)(2,1)S(1)} %slice.13), channel_id=1, source_target_pairs={{0,1},{1,0},{2,3},{3,2},{4,5},{5,4},{6,7},{7,6},{8,9},{9,8},{10,11... | collective-permute-start | bytes 786440 | tf_op jit(solution)/shard_map/ppermute | solution.py:585
  75.9 1.7 %copy-start.3 = (bf16[2048,128]{1,0:T(8,128)(2,1)}, bf16[2048,128]{1,0:T(8,128)(2,1)S(1)}, u32[]{:S(2)}) copy-start(bf16[2048,128]{1,0:T(8,128)(2,1)S(1)} %collective-permute-done.4.refs_3_.refs_8_.refs_4_.refs_5_) | copy-start | bytes 1572868
  76.0 1.6 %collective-permute-start.7 = (bf16[1024,128]{1,0:T(8,128)(2,1)S(1)}, bf16[1024,128]{1,0:T(8,128)(2,1)S(1)}, u32[]{:S(2)}, u32[]{:S(2)}) collective-permute-start(bf16[1024,128]{1,0:T(8,128)(2,1)S(1)} %slice.14), channel_id=1, source_target_pairs={{0,1},{1,0},{2,3},{3,2},{4,5},{5,4},{6,7},{7,6},{8,9},{9,8},{10,11... | collective-permute-start | bytes 786440 | tf_op jit(solution)/shard_map/ppermute | solution.py:585
  76.7 0.9 copy-start.4
  76.7 0.9 copy-start.5
  77.6 0.7 copy-start.6
  83.7 1.0 copy-start
  101.3 5.9 %copy-start.9 = (bf16[2,1024,128]{2,1,0:T(8,128)(2,1)S(1)}, bf16[2,1024,128]{2,1,0:T(8,128)(2,1)}, u32[]{:S(2)}) copy-start(bf16[2,1024,128]{2,1,0:T(8,128)(2,1)} %get-tuple-element.20) | copy-start | bytes 1572868
  101.3 9.4 %copy-start.8 = (bf16[2,1024,128]{2,1,0:T(8,128)(2,1)S(1)}, bf16[2,1024,128]{2,1,0:T(8,128)(2,1)}, u32[]{:S(2)}) copy-start(bf16[2,1024,128]{2,1,0:T(8,128)(2,1)} %get-tuple-element.22) | copy-start | bytes 1572868
  101.3 28.4 %all-to-all-start.3 = ((bf16[4,512,128]{2,1,0:T(8,128)(2,1)}), bf16[4,512,128]{2,1,0:T(8,128)(2,1)S(1)}, u32[]{:S(2)}, u32[]{:S(2)}) async-start(bf16[4,512,128]{2,1,0:T(8,128)(2,1)} %get-tuple-element.28), calls=%async_computation.3 | async-start | bytes 1048576 | tf_op jit(solution)/shard_map/all_to_all | solution.py:614
  107.3 28.1 %collective-permute-start = (bf16[2,1024,128]{2,1,0:T(8,128)(2,1)S(1)}, bf16[2,1024,128]{2,1,0:T(8,128)(2,1)S(1)}, u32[]{:S(2)}, u32[]{:S(2)}) collective-permute-start(bf16[2,1024,128]{2,1,0:T(8,128)(2,1)S(1)} %copy-done.9), channel_id=1, source_target_pairs={{0,8},{8,16},{16,24},{24,32},{32,40},{40,48},{48,56},{56,64},{64,7... | collective-permute-start | bytes 1572872 | tf_op jit(solution)/shard_map/ppermute | solution.py:596
  110.7 24.6 %collective-permute-start.1 = (bf16[2,1024,128]{2,1,0:T(8,128)(2,1)S(1)}, bf16[2,1024,128]{2,1,0:T(8,128)(2,1)S(1)}, u32[]{:S(2)}, u32[]{:S(2)}) collective-permute-start(bf16[2,1024,128]{2,1,0:T(8,128)(2,1)S(1)} %copy-done.8), channel_id=1, source_target_pairs={{8,0},{16,8},{24,16},{32,24},{40,32},{48,40},{56,48},{64,56},{72,6... | collective-permute-start | bytes 1572872 | tf_op jit(solution)/shard_map/ppermute | solution.py:597
  129.7 0.8 copy-start.7
  130.5 13.6 %all-to-all-start.4 = ((bf16[4,512,128]{2,1,0:T(8,128)(2,1)}), bf16[4,512,128]{2,1,0:T(8,128)(2,1)S(1)}, u32[]{:S(2)}, u32[]{:S(2)}) async-start(bf16[4,512,128]{2,1,0:T(8,128)(2,1)} %attend.3), calls=%async_computation.4 | async-start | bytes 1048576 | tf_op jit(solution)/shard_map/all_to_all | solution.py:614
  135.3 0.8 copy-start.12
  135.4 1.0 copy-start.13

commit v5 on v4

--- a/solution.py
+++ b/solution.py
@@ -479,16 +479,12 @@
     )(place, *operands)
 
 
-def convolve_kernel(
-    low_ref, normed_ref, high_ref, tokens_ref, added_ref, taps_ref, mixed_ref, base_ref, padded
-):
+def convolve_kernel(low_ref, normed_ref, high_ref, tokens_ref, taps_ref, out_ref, padded):
     rows, columns, channels = normed_ref.shape
     margin = KER // 2
     pad = 8
-    step = pl.program_id(0)
-    finished = pl.num_programs(0) // 2
-
-    @pl.when(step == 0)
+
+    @pl.when(pl.program_id(0) == 0)
     def _():
         padded[:, 0:pad, :] = jnp.zeros((rows + 2 * margin, pad, channels), F32)
         padded[:, pad + columns :, :] = jnp.zeros((rows + 2 * margin, pad, channels), F32)
@@ -499,62 +495,48 @@
     taps = taps_ref[...]
     strip = 16
     span = tokens_ref.shape[1]
-    begin = step * span
-
-    def convolve_into(out_ref, added):
-        def one_strip(index, carry):
-            inside = pl.multiple_of(index * strip, strip)
-            at = pl.ds(inside, strip)
-            start = pl.multiple_of(begin + inside, strip)
-            totals = [tokens_ref[r, at, :].astype(F32) for r in range(rows)]
-            if added:
-                totals = [t + added_ref[r, at, :].astype(F32) for r, t in enumerate(totals)]
-            for second in range(KER):
-                for line in range(rows + 2 * margin):
-                    values = padded[line, pl.ds(start + pad - margin + second, strip), :]
-                    for r in range(rows):
-                        first = line - r
-                        if 0 <= first < KER:
-                            tap = first * KER + second
-                            totals[r] = totals[r] + taps[tap : tap + 1, :] * values
-            for r in range(rows):
-                out_ref[r, at, :] = totals[r].astype(out_ref.dtype)
-            return carry
-
-        lax.fori_loop(0, span // strip, one_strip, 0)
-
-    @pl.when(step < finished)
-    def _():
-        convolve_into(mixed_ref, True)
-
-    @pl.when(step >= finished)
-    def _():
-        convolve_into(base_ref, False)
-
-
-def convolve(low, normed, high, tokens, added, taps):
+    begin = pl.program_id(0) * span
+
+    def one_strip(index, carry):
+        inside = pl.multiple_of(index * strip, strip)
+        start = pl.multiple_of(begin + inside, strip)
+        totals = [tokens_ref[r, pl.ds(inside, strip), :].astype(F32) for r in range(rows)]
+        for second in range(KER):
+            for line in range(rows + 2 * margin):
+                values = padded[line, pl.ds(start + pad - margin + second, strip), :]
+                for r in range(rows):
+                    first = line - r
+                    if 0 <= first < KER:
+                        tap = first * KER + second
+                        totals[r] = totals[r] + taps[tap : tap + 1, :] * values
+        for r in range(rows):
+            out_ref[r, pl.ds(inside, strip), :] = totals[r]
+        return carry
+
+    lax.fori_loop(0, span // strip, one_strip, 0)
+
+
+def convolve(low, normed, high, tokens, taps):
     rows, columns, channels = normed.shape
-    steps = 4
-    span = columns // steps
-    last = steps // 2 - 1
-    whole = pl.BlockSpec(normed.shape, lambda i: (0, 0, 0))
+    span = columns // 4
     piece = pl.BlockSpec((rows, span, channels), lambda i: (0, i, 0))
-    front = pl.BlockSpec((rows, span, channels), lambda i: (0, jnp.minimum(i, last), 0))
-    back = pl.BlockSpec((rows, span, channels), lambda i: (0, jnp.maximum(i - last - 1, 0), 0))
     edge = pl.BlockSpec(low.shape, lambda i: (0, 0, 0))
     return pl.pallas_call(
         convolve_kernel,
-        grid=(steps,),
-        in_specs=[edge, whole, edge, piece, front, pl.BlockSpec(taps.shape, lambda i: (0, 0))],
-        out_specs=(front, back),
-        out_shape=(
-            jax.ShapeDtypeStruct(normed.shape, BF),
-            jax.ShapeDtypeStruct((rows, columns // 2, channels), F32),
-        ),
+        grid=(columns // span,),
+        in_specs=[
+            edge,
+            pl.BlockSpec(normed.shape, lambda i: (0, 0, 0)),
+            edge,
+            piece,
+            pl.BlockSpec(taps.shape, lambda i: (0, 0)),
+        ],
+        out_specs=piece,
+        out_shape=jax.ShapeDtypeStruct(normed.shape, F32),
         scratch_shapes=[pltpu.VMEM((rows + 2 * (KER // 2), columns + 16, channels), F32)],
         cost_estimate=pl.CostEstimate(flops=10**9, bytes_accessed=6 * 2**20, transcendentals=0),
         name="convolve",
-    )(low, normed, high, tokens, added, taps)
+    )(low, normed, high, tokens, taps)
 
 
 def body(
@@ -603,8 +585,8 @@
     size = width // HEADS
     scale = 1.4426950408889634 / size**0.5
     query = query_of(place, token_rows, gain, weights, columns, scale)
-    half_way = columns // 2
-    chunks = ((0, half_way, half_way), (half_way, half_way, half_way))
+    cut = 5 * columns // 8
+    chunks = ((0, cut, cut), (cut, columns - cut, columns - cut))
     returned = []
     source = (blocks,)
     for chunk, (start, count, block) in enumerate(chunks):
@@ -612,9 +594,9 @@
         if chunk == 0:
             projected, *source = projected
         returned.append(lax.all_to_all(projected, "head", 0, 0, tiled=True))
-    mixed, base = convolve(low, normed, high, tokens, returned[0], conv_kernel)
-    rest = (base + returned[1].astype(F32)).astype(BF)
-    return lax.dynamic_update_slice_in_dim(mixed, rest, half_way, 1)
+    base = convolve(low, normed, high, tokens, conv_kernel)
+    projected = jnp.concatenate(returned, axis=1)
+    return (base + projected.astype(F32)).astype(BF)
 
 
 def solution(mesh):

time: 147 us -> 155 us (1.054)
  the two profiles are of different devices: /device:TPU:10 before, /device:TPU:0 now
where the time goes in v5:
time: 155 us; the launch traced here: 153 us
  Pallas kernels  53.5 us (35%)
  waiting for transfers between devices  39.4 us (25%)
  blocking collectives  27.2 us (18%)
  starting transfers between devices  23.1 us (15%)
  local copies, waits for them, and re-layouts  6.1 us (4%)
  other arithmetic  3.4 us (2%)
    pallas_call x2, Pallas kernels, attend_and_project(): pl.pallas_call(functools.partial(attend_kernel, HEADS // groups, first, s...  31.2 us
    ppermute x3, waiting for transfers between devices, to_all_heads(): arrived[distance] = lax.ppermute(blocks[distance], 'head', ring)  27.6 us
    all_to_all x1, blocking collectives, body(): lax.all_to_all(partial.reshape(bands, share, channels), 'band', 0, 0, til...  16.5 us
    all_to_all x1, blocking collectives, body(): moments = lax.all_to_all(moments, 'head', 0, 0, tiled=True)  10.7 us
    pallas_call x1, Pallas kernels, convolve(): pl.pallas_call(convolve_kernel, grid=(columns // span,), in_specs=[edge,...  7.47 us
    all_to_all x2, starting transfers between devices, body(): returned.append(lax.all_to_all(projected, 'head', 0, 0, tiled=True))  6.95 us
    ppermute x3, starting transfers between devices, to_all_heads(): arrived[distance] = lax.ppermute(blocks[distance], 'head', ring)  5.78 us
    pallas_call x1, Pallas kernels, query_of(): pl.pallas_call(functools.partial(query_kernel, scale, groups), grid_spec=...  5.42 us
  transfers between devices with their start and end apart: 11, of which 6 were waited for; matrix products, arithmetic and copies ran while one was open for 2% of the time, Pallas kernels for 8%

profile of v5, /device:TPU:0, one launch (start us, length us, event | category | flops | bytes accessed | tf_op | source)
XLA Modules:
  0.0 152.9 jit_solution(16492229488264398058)
XLA Ops:
  0.0 4.2 %moments.1 = (f32[4,2,4096]{2,1,0:T(2,128)}, bf16[4,512,128]{2,1,0:T(8,128)(2,1)}, bf16[2048,128]{1,0:T(8,128)(2,1)}, bf16[2048,128]{1,0:T(8,128)(2,1)}, bf16[2048,128]{1,0:T(8,128)(2,1)}) custom-call(bf16[4,1024,128]{2,1,0:T(8,128)(2,1)} %refs_0_.1, bf16[512,128]{1,0:T(8,128)(2,1)} %query_hbm.1, bf16[512,128]{1,0:T(8,128)(2,1)} %key_hbm.1, ...), custom_call_target="tpu_custom_call" | custom-call | flops 1000000000 | bytes 1048576 | tf_op jit(solution)/shard_map/moments/pallas_call | solution.py:87
  4.2 10.7 %all_to_all.25.moments_hbm = f32[4,2,4096]{2,1,0:T(2,128)} all-to-all(f32[4,2,4096]{2,1,0:T(2,128)} %get-tuple-element.17), channel_id=1, replica_groups=mesh['band'=16,'head'=4,'dp'=2] {'head'}, dimensions={0} | all-to-all | bytes 262144 | tf_op jit(solution)/shard_map/all_to_all | solution.py:556
  14.9 5.2 %normalize_sample.1 = (bf16[4,1024,128]{2,1,0:T(8,128)(2,1)}, bf16[2,1024,128]{2,1,0:T(8,128)(2,1)}, bf16[2,1024,128]{2,1,0:T(8,128)(2,1)}, bf16[1024,128]{1,0:T(8,128)(2,1)}) custom-call(f32[4,128]{1,0:T(4,128)} %bitcast.11, s32[1,1024]{1,0:T(1,128)} %bitcast.9, s32[1,1024]{1,0:T(1,128)} %bitcast.10, f32[2,1024]{1,0:T(2,128)} %fraction_ref.1, ...), custom_call_target="tpu_custom_call" | custom-call | flops 2000000000 | bytes 6291456 | tf_op jit(solution)/shard_map/normalize_sample/pallas_call | solution.py:230
  20.1 0.0 copy-start.11
  20.1 16.5 %all_to_all.26 = bf16[16,64,128]{2,1,0:T(8,128)(2,1)S(1)} all-to-all(bf16[16,64,128]{2,1,0:T(8,128)(2,1)} %bitcast.8), channel_id=1, replica_groups=mesh['band'=16,'head'=4,'dp'=2] {'band'}, dimensions={0} | all-to-all | bytes 524288 | tf_op jit(solution)/shard_map/all_to_all | solution.py:575
  36.6 1.3 broadcast_in_dim.3
  37.9 5.2 %all-to-all-start.2 = ((bf16[64,64,128]{2,1,0:T(8,128)(2,1)}), bf16[64,64,128]{2,1,0:T(8,128)(2,1)S(1)}, u32[]{:S(2)}, u32[]{:S(2)}) async-start(bf16[64,64,128]{2,1,0:T(8,128)(2,1)} %broadcast_in_dim.3), calls=%async_computation.2 | async-start | bytes 2097152 | tf_op jit(solution)/shard_map/all_to_all | solution.py:582
  43.1 1.6 %collective-permute-start.2 = (bf16[2048,128]{1,0:T(8,128)(2,1)}, bf16[2048,128]{1,0:T(8,128)(2,1)S(1)}, u32[]{:S(2)}, u32[]{:S(2)}) collective-permute-start(bf16[2048,128]{1,0:T(8,128)(2,1)} %get-tuple-element.21), channel_id=1, source_target_pairs={{0,2},{2,4},{4,6},{6,0},{1,3},{3,5},{5,7},{7,1},{8,10},{10,12},{12... | collective-permute-start | bytes 1572872 | tf_op jit(solution)/shard_map/ppermute | solution.py:562
  44.8 0.0 copy-done.11
  44.8 2.7 %collective-permute-start.3 = (bf16[2048,128]{1,0:T(8,128)(2,1)S(1)}, bf16[2048,128]{1,0:T(8,128)(2,1)S(1)}, u32[]{:S(2)}, u32[]{:S(2)}) collective-permute-start(bf16[2048,128]{1,0:T(8,128)(2,1)S(1)} %copy-done.11), channel_id=1, source_target_pairs={{0,4},{2,6},{4,0},{6,2},{1,5},{3,7},{5,1},{7,3},{8,12},{10,14},{12... | collective-permute-start | bytes 1572872 | tf_op jit(solution)/shard_map/ppermute | solution.py:562
  47.4 1.5 collective-permute-start.4
  48.9 18.8 %collective-permute-done.2.refs_1_.refs_6_.refs_2_.refs_3_ = bf16[2048,128]{1,0:T(8,128)(2,1)S(1)} collective-permute-done((bf16[2048,128]{1,0:T(8,128)(2,1)}, bf16[2048,128]{1,0:T(8,128)(2,1)S(1)}, u32[]{:S(2)}, u32[]{:S(2)}) %collective-permute-start.2) | collective-permute-done | bytes 524320 | tf_op jit(solution)/shard_map/ppermute | solution.py:562
  67.7 0.0 copy-start.1
  67.7 0.8 slice.12
  68.5 0.0 collective-permute-start.5
  68.5 8.8 %collective-permute-done.3.refs_2_.refs_7_.refs_3_.refs_4_ = bf16[2048,128]{1,0:T(8,128)(2,1)S(1)} collective-permute-done((bf16[2048,128]{1,0:T(8,128)(2,1)S(1)}, bf16[2048,128]{1,0:T(8,128)(2,1)S(1)}, u32[]{:S(2)}, u32[]{:S(2)}) %collective-permute-start.3) | collective-permute-done | bytes 524320 | tf_op jit(solution)/shard_map/ppermute | solution.py:562
  77.3 0.0 copy-start.2
  77.3 0.8 slice.13
  78.1 0.0 collective-permute-start.6
  78.1 0.0 collective-permute-done.4.refs_3_.refs_8_.refs_4_.refs_5_
  78.1 0.0 copy-start.3
  78.1 0.8 slice.14
  78.9 0.5 collective-permute-start.7
  79.4 0.6 pad_add_fusion.place_ref
  80.0 0.0 collective-permute-done.5.refs_9_.refs_5_.refs_6_
  80.0 0.0 copy-start.4
  80.0 0.0 collective-permute-done.6.refs_10_.refs_6_.refs_7_
  80.0 0.0 copy-start.5
  80.0 0.8 collective-permute-done.7.refs_11_.refs_7_.refs_8_
  80.8 0.0 copy-start.6
  80.8 0.0 copy-done.1
  80.8 0.0 copy-done.2
  80.8 0.0 copy-done.3
  80.8 0.0 copy-done.4
  80.8 0.0 copy-done.5
  80.8 0.6 copy-done.6
  81.5 5.4 %query.1.query_hbm = bf16[4,1024,128]{2,1,0:T(8,128)(2,1)} custom-call(s32[2]{0:T(128)} %pad_add_fusion.place_ref, bf16[4,1024,128]{2,1,0:T(8,128)(2,1)} %refs_0_.1, bf16[2048,128]{1,0:T(8,128)(2,1)} %copy-done.1, bf16[2048,128]{1,0:T(8,128)(2,1)} %copy-done.2, bf16[2048,128]{1,0:T(8,128)(2,1)} %copy-done.3, f32[4,128]{1,0:T(4,128)} %bitcast.12, ...), custom_call_target="tpu_custom_call" | custom-call | flops 2000000000 | bytes 3145728 | tf_op jit(solution)/shard_map/query/pallas_call | solution.py:309
  86.9 0.0 all-to-all-done.2
  86.9 0.0 copy-start
  86.9 0.9 copy-done
  87.9 19.3 %attend.2 = (bf16[4,640,128]{2,1,0:T(8,128)(2,1)}, bf16[4,1024,128]{2,1,0:T(8,128)(2,1)}, bf16[4,1024,128]{2,1,0:T(8,128)(2,1)}) custom-call(s32[2]{0:T(128)} %pad_add_fusion.place_ref, bf16[4,1024,128]{2,1,0:T(8,128)(2,1)} %query.1.query_hbm, bf16[16,4,64,128]{3,2,1,0:T(8,128)(2,1)} %bitcast.7, ...), custom_call_target="tpu_custom_call" | custom-call | flops 1342177280 | bytes 4194304 | tf_op jit(solution)/shard_map/attend/pallas_call | solution.py:469
  107.1 0.0 copy-start.10
  107.2 0.0 copy-start.9
  107.2 12.0 %attend.3 = bf16[4,384,128]{2,1,0:T(8,128)(2,1)} custom-call(s32[2]{0:T(128)} %pad_add_fusion.place_ref, bf16[4,1024,128]{2,1,0:T(8,128)(2,1)} %query.1.query_hbm, bf16[4,1024,128]{2,1,0:T(8,128)(2,1)} %get-tuple-element.27.refs_0_, bf16[4,1024,128]{2,1,0:T(8,128)(2,1)} %get-tuple-element.28.refs_1_, ...), custom_call_target="tpu_custom_call" | custom-call | flops 805306368 | bytes 4194304 | tf_op jit(solution)/shard_map/attend/pallas_call | solution.py:469
  119.1 3.5 %all-to-all-start.4 = ((bf16[4,384,128]{2,1,0:T(8,128)(2,1)}), bf16[4,384,128]{2,1,0:T(8,128)(2,1)S(1)}, u32[]{:S(2)}, u32[]{:S(2)}) async-start(bf16[4,384,128]{2,1,0:T(8,128)(2,1)} %attend.3), calls=%async_computation.4 | async-start | bytes 786432 | tf_op jit(solution)/shard_map/all_to_all | solution.py:596
  122.6 0.0 copy-done.10
  122.6 3.4 %collective-permute-start = (bf16[2,1024,128]{2,1,0:T(8,128)(2,1)S(1)}, bf16[2,1024,128]{2,1,0:T(8,128)(2,1)S(1)}, u32[]{:S(2)}, u32[]{:S(2)}) collective-permute-start(bf16[2,1024,128]{2,1,0:T(8,128)(2,1)S(1)} %copy-done.10), channel_id=1, source_target_pairs={{0,8},{8,16},{16,24},{24,32},{32,40},{40,48},{48,56},{56,64},{64,7... | collective-permute-start | bytes 1572872 | tf_op jit(solution)/shard_map/ppermute | solution.py:578
  126.0 0.0 copy-done.9
  126.0 1.3 collective-permute-start.1
  127.3 4.1 %all-to-all-done.4 = bf16[4,384,128]{2,1,0:T(8,128)(2,1)S(1)} async-done(((bf16[4,384,128]{2,1,0:T(8,128)(2,1)}), bf16[4,384,128]{2,1,0:T(8,128)(2,1)S(1)}, u32[]{:S(2)}, u32[]{:S(2)}) %all-to-all-start.4) | async-done | bytes 393248 | tf_op jit(solution)/shard_map/all_to_all | solution.py:596
  131.5 3.5 %all-to-all-start.3 = ((bf16[4,640,128]{2,1,0:T(8,128)(2,1)}), bf16[4,640,128]{2,1,0:T(8,128)(2,1)S(1)}, u32[]{:S(2)}, u32[]{:S(2)}) async-start(bf16[4,640,128]{2,1,0:T(8,128)(2,1)} %get-tuple-element.26), calls=%async_computation.3 | async-start | bytes 1310720 | tf_op jit(solution)/shard_map/all_to_all | solution.py:596
  135.0 2.7 %collective-permute-done.low_ref = bf16[2,1024,128]{2,1,0:T(8,128)(2,1)S(1)} collective-permute-done((bf16[2,1024,128]{2,1,0:T(8,128)(2,1)S(1)}, bf16[2,1024,128]{2,1,0:T(8,128)(2,1)S(1)}, u32[]{:S(2)}, u32[]{:S(2)}) %collective-permute-start) | collective-permute-done | bytes 524320 | tf_op jit(solution)/shard_map/ppermute | solution.py:578
  137.7 0.0 copy-start.7
  137.7 4.2 %collective-permute-done.1.high_ref = bf16[2,1024,128]{2,1,0:T(8,128)(2,1)S(1)} collective-permute-done((bf16[2,1024,128]{2,1,0:T(8,128)(2,1)S(1)}, bf16[2,1024,128]{2,1,0:T(8,128)(2,1)S(1)}, u32[]{:S(2)}, u32[]{:S(2)}) %collective-permute-start.1) | collective-permute-done | bytes 524320 | tf_op jit(solution)/shard_map/ppermute | solution.py:579
  141.9 0.0 copy-start.8
  141.9 0.0 copy-done.7
  141.9 0.8 copy-done.8
  142.7 7.5 %convolve.1 = f32[4,1024,128]{2,1,0:T(8,128)} custom-call(bf16[2,1024,128]{2,1,0:T(8,128)(2,1)} %copy-done.7, bf16[4,1024,128]{2,1,0:T(8,128)(2,1)} %get-tuple-element.19.normed_ref, bf16[2,1024,128]{2,1,0:T(8,128)(2,1)} %copy-done.8, bf16[4,1024,128]{2,1,0:T(8,128)(2,1)} %refs_0_.1, f32[25,128]{1,0:T(8,128)} %taps_ref.1), custom_call_target="tpu_custom_call" | custom-call | flops 1000000000 | bytes 6291456 | tf_op jit(solution)/shard_map/convolve/pallas_call | solution.py:524
  150.1 0.0 all-to-all-done.3
  150.1 2.8 %add_convert_fusion = bf16[4,1024,128]{2,1,0:T(8,128)(2,1)} fusion(f32[4,1024,128]{2,1,0:T(8,128)} %convolve.1, bf16[4,384,128]{2,1,0:T(8,128)(2,1)S(1)} %all-to-all-done.4, bf16[4,640,128]{2,1,0:T(8,128)(2,1)S(1)} %all-to-all-done.3), kind=kLoop, calls=%fused_computation | loop fusion | flops 3145728 | bytes 4194304 | tf_op jit(solution)/shard_map/convert_element_type | solution.py:599
  (1 shorter events, 0.0 us)
Async XLA Ops:
  20.1 24.7 %copy-start.11 = (bf16[2048,128]{1,0:T(8,128)(2,1)S(1)}, bf16[2048,128]{1,0:T(8,128)(2,1)}, u32[]{:S(2)}) copy-start(bf16[2048,128]{1,0:T(8,128)(2,1)} %get-tuple-element.22) | copy-start | bytes 1572868
  37.9 49.0 %all-to-all-start.2 = ((bf16[64,64,128]{2,1,0:T(8,128)(2,1)}), bf16[64,64,128]{2,1,0:T(8,128)(2,1)S(1)}, u32[]{:S(2)}, u32[]{:S(2)}) async-start(bf16[64,64,128]{2,1,0:T(8,128)(2,1)} %broadcast_in_dim.3), calls=%async_computation.2 | async-start | bytes 2097152 | tf_op jit(solution)/shard_map/all_to_all | solution.py:582
  43.1 24.6 %collective-permute-start.2 = (bf16[2048,128]{1,0:T(8,128)(2,1)}, bf16[2048,128]{1,0:T(8,128)(2,1)S(1)}, u32[]{:S(2)}, u32[]{:S(2)}) collective-permute-start(bf16[2048,128]{1,0:T(8,128)(2,1)} %get-tuple-element.21), channel_id=1, source_target_pairs={{0,2},{2,4},{4,6},{6,0},{1,3},{3,5},{5,7},{7,1},{8,10},{10,12},{12... | collective-permute-start | bytes 1572872 | tf_op jit(solution)/shard_map/ppermute | solution.py:562
  44.8 32.6 %collective-permute-start.3 = (bf16[2048,128]{1,0:T(8,128)(2,1)S(1)}, bf16[2048,128]{1,0:T(8,128)(2,1)S(1)}, u32[]{:S(2)}, u32[]{:S(2)}) collective-permute-start(bf16[2048,128]{1,0:T(8,128)(2,1)S(1)} %copy-done.11), channel_id=1, source_target_pairs={{0,4},{2,6},{4,0},{6,2},{1,5},{3,7},{5,1},{7,3},{8,12},{10,14},{12... | collective-permute-start | bytes 1572872 | tf_op jit(solution)/shard_map/ppermute | solution.py:562
  47.4 30.7 %collective-permute-start.4 = (bf16[2048,128]{1,0:T(8,128)(2,1)}, bf16[2048,128]{1,0:T(8,128)(2,1)S(1)}, u32[]{:S(2)}, u32[]{:S(2)}) collective-permute-start(bf16[2048,128]{1,0:T(8,128)(2,1)} %get-tuple-element.23), channel_id=1, source_target_pairs={{0,6},{2,0},{4,2},{6,4},{1,7},{3,1},{5,3},{7,5},{8,14},{10,8},{12,... | collective-permute-start | bytes 1572872 | tf_op jit(solution)/shard_map/ppermute | solution.py:562
  67.7 13.0 %copy-start.1 = (bf16[2048,128]{1,0:T(8,128)(2,1)}, bf16[2048,128]{1,0:T(8,128)(2,1)S(1)}, u32[]{:S(2)}) copy-start(bf16[2048,128]{1,0:T(8,128)(2,1)S(1)} %collective-permute-done.2.refs_1_.refs_6_.refs_2_.refs_3_) | copy-start | bytes 1572868
  68.5 11.5 %collective-permute-start.5 = (bf16[1024,128]{1,0:T(8,128)(2,1)}, bf16[1024,128]{1,0:T(8,128)(2,1)S(1)}, u32[]{:S(2)}, u32[]{:S(2)}) collective-permute-start(bf16[1024,128]{1,0:T(8,128)(2,1)} %slice.12), channel_id=1, source_target_pairs={{0,1},{1,0},{2,3},{3,2},{4,5},{5,4},{6,7},{7,6},{8,9},{9,8},{10,11... | collective-permute-start | bytes 786440 | tf_op jit(solution)/shard_map/ppermute | solution.py:567
  77.3 3.5 %copy-start.2 = (bf16[2048,128]{1,0:T(8,128)(2,1)}, bf16[2048,128]{1,0:T(8,128)(2,1)S(1)}, u32[]{:S(2)}) copy-start(bf16[2048,128]{1,0:T(8,128)(2,1)S(1)} %collective-permute-done.3.refs_2_.refs_7_.refs_3_.refs_4_) | copy-start | bytes 1572868
  78.1 1.9 %collective-permute-start.6 = (bf16[1024,128]{1,0:T(8,128)(2,1)}, bf16[1024,128]{1,0:T(8,128)(2,1)S(1)}, u32[]{:S(2)}, u32[]{:S(2)}) collective-permute-start(bf16[1024,128]{1,0:T(8,128)(2,1)} %slice.13), channel_id=1, source_target_pairs={{0,1},{1,0},{2,3},{3,2},{4,5},{5,4},{6,7},{7,6},{8,9},{9,8},{10,11... | collective-permute-start | bytes 786440 | tf_op jit(solution)/shard_map/ppermute | solution.py:567
  78.1 2.7 %copy-start.3 = (bf16[2048,128]{1,0:T(8,128)(2,1)}, bf16[2048,128]{1,0:T(8,128)(2,1)S(1)}, u32[]{:S(2)}) copy-start(bf16[2048,128]{1,0:T(8,128)(2,1)S(1)} %collective-permute-done.4.refs_3_.refs_8_.refs_4_.refs_5_) | copy-start | bytes 1572868
  78.9 1.9 %collective-permute-start.7 = (bf16[1024,128]{1,0:T(8,128)(2,1)}, bf16[1024,128]{1,0:T(8,128)(2,1)S(1)}, u32[]{:S(2)}, u32[]{:S(2)}) collective-permute-start(bf16[1024,128]{1,0:T(8,128)(2,1)} %slice.14), channel_id=1, source_target_pairs={{0,1},{1,0},{2,3},{3,2},{4,5},{5,4},{6,7},{7,6},{8,9},{9,8},{10,11... | collective-permute-start | bytes 786440 | tf_op jit(solution)/shard_map/ppermute | solution.py:567
  80.0 0.8 copy-start.4
  80.0 0.8 copy-start.5
  80.8 0.7 copy-start.6
  86.9 1.0 copy-start
  107.1 15.5 %copy-start.10 = (bf16[2,1024,128]{2,1,0:T(8,128)(2,1)S(1)}, bf16[2,1024,128]{2,1,0:T(8,128)(2,1)}, u32[]{:S(2)}) copy-start(bf16[2,1024,128]{2,1,0:T(8,128)(2,1)} %get-tuple-element.18) | copy-start | bytes 1572868
  107.2 18.9 %copy-start.9 = (bf16[2,1024,128]{2,1,0:T(8,128)(2,1)S(1)}, bf16[2,1024,128]{2,1,0:T(8,128)(2,1)}, u32[]{:S(2)}) copy-start(bf16[2,1024,128]{2,1,0:T(8,128)(2,1)} %get-tuple-element.20) | copy-start | bytes 1572868
  119.1 12.3 %all-to-all-start.4 = ((bf16[4,384,128]{2,1,0:T(8,128)(2,1)}), bf16[4,384,128]{2,1,0:T(8,128)(2,1)S(1)}, u32[]{:S(2)}, u32[]{:S(2)}) async-start(bf16[4,384,128]{2,1,0:T(8,128)(2,1)} %attend.3), calls=%async_computation.4 | async-start | bytes 786432 | tf_op jit(solution)/shard_map/all_to_all | solution.py:596
  122.6 15.1 %collective-permute-start = (bf16[2,1024,128]{2,1,0:T(8,128)(2,1)S(1)}, bf16[2,1024,128]{2,1,0:T(8,128)(2,1)S(1)}, u32[]{:S(2)}, u32[]{:S(2)}) collective-permute-start(bf16[2,1024,128]{2,1,0:T(8,128)(2,1)S(1)} %copy-done.10), channel_id=1, source_target_pairs={{0,8},{8,16},{16,24},{24,32},{32,40},{40,48},{48,56},{56,64},{64,7... | collective-permute-start | bytes 1572872 | tf_op jit(solution)/shard_map/ppermute | solution.py:578
  126.0 15.8 %collective-permute-start.1 = (bf16[2,1024,128]{2,1,0:T(8,128)(2,1)S(1)}, bf16[2,1024,128]{2,1,0:T(8,128)(2,1)S(1)}, u32[]{:S(2)}, u32[]{:S(2)}) collective-permute-start(bf16[2,1024,128]{2,1,0:T(8,128)(2,1)S(1)} %copy-done.9), channel_id=1, source_target_pairs={{8,0},{16,8},{24,16},{32,24},{40,32},{48,40},{56,48},{64,56},{72,6... | collective-permute-start | bytes 1572872 | tf_op jit(solution)/shard_map/ppermute | solution.py:579
  131.5 18.7 %all-to-all-start.3 = ((bf16[4,640,128]{2,1,0:T(8,128)(2,1)}), bf16[4,640,128]{2,1,0:T(8,128)(2,1)S(1)}, u32[]{:S(2)}, u32[]{:S(2)}) async-start(bf16[4,640,128]{2,1,0:T(8,128)(2,1)} %get-tuple-element.26), calls=%async_computation.3 | async-start | bytes 1310720 | tf_op jit(solution)/shard_map/all_to_all | solution.py:596
  137.7 4.2 %copy-start.7 = (bf16[2,1024,128]{2,1,0:T(8,128)(2,1)}, bf16[2,1024,128]{2,1,0:T(8,128)(2,1)S(1)}, u32[]{:S(2)}) copy-start(bf16[2,1024,128]{2,1,0:T(8,128)(2,1)S(1)} %collective-permute-done.low_ref) | copy-start | bytes 1572868
  141.9 0.8 copy-start.8
